TPU v7x, 32 devices: a whole 2x2x4 slice. The times are simulated.
32 devices in a mesh: group: 8 (over y, x, core), member: 4 (over z).
Axes of the slice: x: 2, y: 2, z: 4, core: 2. Of those that a mesh axis runs over, the one named last changes fastest.
Arguments:
- points: bfloat16 [49152, 128], P(('group', 'member')), may hold values from -3 to 3
- right_sides: float32 [49152, 256], P(('group', 'member')), may hold values from -6 to 6
- leaf_order: int32 [32, 1536], P(('group', 'member')), may hold values from 0 to 1535, each once within a row
- near_leaves: int32 [32, 2], P(('group', 'member')), may hold values from 0 to 3, as said below
- bases: bfloat16 [49152, 128], P(('group', 'member')), may hold values from -0.15625 to 0.15625
- couplings: bfloat16 [32, 4, 128, 128], P(('group', 'member')), may hold values from -0.25 to 0.25
- transfers: bfloat16 [32, 128, 128], P(('group', 'member')), may hold values from -0.5 to 0.5
- cross_couplings: bfloat16 [8, 8, 128, 128], P('group'), may hold values from -0.1875 to 0.1875
- low_bound: float32 [1], replicated, may hold values from 0.5 to 2.5
- high_bound: float32 [1], replicated, may hold values from 4 to 8
Outputs:
- solution: float32 [49152, 256], P(('group', 'member'))
- residual: float32 [49152, 256], P(('group', 'member'))
Inputs may be any that keep to these rules, and one draw needn't show every extreme that they name: `near_leaves`: each leaf's two entries differ from each other and from the leaf's own member index, and lie within two member positions of it.
All inputs are finite; a program needn't handle non-finite values.
Results may differ from a plain program's by a relative error of at most 0.0085.
Values may be sent and summed in bfloat16 or wider, within the bound.
No kernel may reach another device: no remote copies, remote signals or barrier semaphores. Data moves between devices by JAX's collectives and lax.ppermute only.
A program may use at most 128 MiB of HBM per device.

v0:
```python
import math

import jax
import jax.numpy as jnp
from jax import lax
from jax.experimental import pallas as pl
from jax.experimental.pallas import tpu as pltpu
from jax.sharding import PartitionSpec as P


RIDGE = 0.5
KERNEL_WIDTH = 8.0
REACH = 2
F32 = jnp.float32
BF16 = jnp.bfloat16
VMEM = pltpu.VMEM
ANY = pl.ANY


def shift(array, axis, by):
    count = lax.axis_size(axis)
    pairs = [(i, i + by) for i in range(count) if 0 <= i + by < count]
    return lax.ppermute(array, axis, pairs)


def cycle(array, axis, by):
    count = lax.axis_size(axis)
    return lax.ppermute(array, axis, [(i, (i + by) % count) for i in range(count)])


def tile_of(rows):
    return 256 if rows % 256 == 0 else rows


def whole(array):
    dims = array.ndim
    return pl.BlockSpec(array.shape, lambda *_: (0,) * dims)


def by_rows(tile, width):
    return pl.BlockSpec((tile, width), lambda i: (i, 0))


SMEM_SPEC = pl.BlockSpec(memory_space=pltpu.SMEM)
ANY_SPEC = pl.BlockSpec(memory_space=ANY)


def call(body, out, args, in_specs, out_specs, grid=(), scratch=(), flops=0, bytes_=0, exps=0):
    return pl.pallas_call(
        body,
        out_shape=out,
        grid=grid,
        in_specs=in_specs,
        out_specs=out_specs,
        scratch_shapes=list(scratch),
        cost_estimate=pl.CostEstimate(flops=flops, bytes_accessed=bytes_, transcendentals=exps),
        compiler_params=pltpu.CompilerParams(vmem_limit_bytes=16 * 1024 * 1024),
    )(*args)


def dot(left, right):
    return jnp.dot(left, right, preferred_element_type=F32)


def dot_tn(left, right):
    return lax.dot_general(left, right, (((0,), (0,)), ((), ())), preferred_element_type=F32)


def dot_nt(left, right):
    return lax.dot_general(left, right, (((1,), (1,)), ((), ())), preferred_element_type=F32)


def pieces(value):
    first = value.astype(BF16).astype(F32)
    rest = value - first
    second = rest.astype(BF16).astype(F32)
    return first, second, rest - second


def augmented(block, left):
    rows, dims = block.shape
    wide = block.astype(F32)
    norm = jnp.sum(wide * wide, axis=1, keepdims=True)
    value = -norm / KERNEL_WIDTH
    if left:
        value = value + (dims / 16.0 - math.log(2.0 * rows))
        block = (wide * (2.0 / KERNEL_WIDTH)).astype(BF16)
    lane = lax.broadcasted_iota(jnp.int32, (rows, 128), 1)
    at, ones_at = (0, 3) if left else (3, 0)
    extra = jnp.where((lane >= ones_at) & (lane < ones_at + 3), 1.0, 0.0)
    for k, piece in enumerate(pieces(value)):
        extra = jnp.where(lane == at + k, piece, extra)
    return block, extra.astype(BF16)


def fill_augmented(target, block, left):
    dims = block.shape[1]
    main, extra = augmented(block, left)
    target[:, :dims] = main
    target[:, dims:] = extra


def kernel_tile(left_tile, right_all):
    return jnp.exp(dot_nt(left_tile, right_all)).astype(BF16)


def pick(choice, candidates, target, sem):
    for k, ref in enumerate(candidates):
        @pl.when(choice == k)
        def _():
            copy = pltpu.make_async_copy(ref, target, sem)
            copy.start()
            copy.wait()


def slots(near_ref, members):
    member = lax.axis_index("member")
    one = near_ref[0, 0] - member
    two = near_ref[0, 1] - member
    if members <= 2 * REACH:
        before = (one == -1) | (two == -1)
        after = (one == 1) | (two == 1)
        behind = (one == -2) | (two == -2)
        slot_a = jnp.where(before, 0, 1)
        slot_b = jnp.where(before & after, 0, jnp.where(behind, 1, 2))
        return slot_a, slot_b

    def index(offset):
        return jnp.where(offset == -1, 0, jnp.where(offset == 1, 1, jnp.where(offset == -2, 2, 3)))

    return index(one), index(two)


def slot_candidates(moved, members):
    before, after, behind, ahead = moved
    if members <= 2 * REACH:
        return (before, after), (after, behind, ahead)
    return moved, moved


def factors(low_ref, high_ref, width):
    low = jnp.full((1, width), low_ref[0], F32)
    high = jnp.full((1, width), high_ref[0], F32)
    theta = (high + low) / 2.0
    delta = (high - low) / 2.0
    sigma = theta / delta
    rho_zero = 1.0 / sigma
    rho_one = 1.0 / (2.0 * sigma - rho_zero)
    return theta, rho_one * rho_zero, 2.0 * rho_one / delta


def prep(ordered, bases, transfer, low, high):
    rows, width = ordered.shape
    rank = bases.shape[1]
    tile = tile_of(rows)

    def body(low_ref, high_ref, ordered_ref, bases_ref, transfer_ref, v_ref, message_ref, total):
        step = pl.program_id(0)
        theta, _, _ = factors(low_ref, high_ref, width)
        v = (ordered_ref[...] / theta).astype(BF16)
        v_ref[...] = v
        part = dot_tn(bases_ref[...], v)

        @pl.when(step == 0)
        def _():
            total[...] = part

        @pl.when(step > 0)
        def _():
            total[...] += part

        @pl.when(step == pl.num_programs(0) - 1)
        def _():
            message_ref[:, :width] = total[...].astype(BF16)
            message_ref[:, width:] = transfer_ref[...]

    return call(
        body,
        (jax.ShapeDtypeStruct((rows, width), BF16), jax.ShapeDtypeStruct((rank, width + rank), BF16)),
        (low, high, ordered, bases, transfer),
        [SMEM_SPEC, SMEM_SPEC, by_rows(tile, width), by_rows(tile, rank), whole(transfer)],
        (by_rows(tile, width), pl.BlockSpec((rank, width + rank), lambda i: (0, 0))),
        grid=(rows // tile,), scratch=[VMEM((rank, width), F32)],
        flops=2 * rows * width * rank, bytes_=rows * width * 6 + rows * rank * 2,
    )


def self_first(points, ordered, v, low, high):
    rows, width = ordered.shape
    dims = points.shape[1]
    tile = tile_of(rows)

    def body(low_ref, high_ref, points_ref, ordered_ref, v_ref, block_ref, rest_ref, left, right):
        step = pl.program_id(0)

        @pl.when(step == 0)
        def _():
            fill_augmented(left, points_ref[...], True)
            fill_augmented(right, points_ref[...], False)

        theta, _, _ = factors(low_ref, high_ref, width)
        block = kernel_tile(left[pl.ds(step * tile, tile), :], right[...])
        block_ref[...] = block
        own = ordered_ref[...]
        rest_ref[...] = own - RIDGE * (own / theta) - dot(block, v_ref[...])

    return call(
        body,
        (jax.ShapeDtypeStruct((rows, rows), BF16), jax.ShapeDtypeStruct((rows, width), F32)),
        (low, high, points, ordered, v),
        [SMEM_SPEC, SMEM_SPEC, whole(points), by_rows(tile, width), whole(v)],
        (by_rows(tile, rows), by_rows(tile, width)),
        grid=(rows // tile,),
        scratch=[VMEM((rows, dims + 128), BF16), VMEM((rows, dims + 128), BF16)],
        flops=2 * rows * rows * (width + dims), bytes_=rows * rows * 2 + rows * width * 10,
        exps=rows * rows,
    )


def near_block(which, near, points, candidates):
    rows, dims = points.shape
    members = lax.axis_size("member")
    tile = tile_of(rows)
    count = len(candidates)

    def body(near_ref, points_ref, *rest):
        others, (block_ref, other, left, right, sem) = rest[:count], rest[count:]
        step = pl.program_id(0)

        @pl.when(step == 0)
        def _():
            pick(slots(near_ref, members)[which], others, other, sem)
            fill_augmented(left, points_ref[...], True)
            fill_augmented(right, other[...], False)

        block_ref[...] = kernel_tile(left[pl.ds(step * tile, tile), :], right[...])

    return call(
        body,
        jax.ShapeDtypeStruct((rows, rows), BF16),
        (near, points, *candidates),
        [SMEM_SPEC, whole(points)] + [ANY_SPEC] * count,
        by_rows(tile, rows),
        grid=(rows // tile,),
        scratch=[VMEM((rows, dims), BF16), VMEM((rows, dims + 128), BF16),
                 VMEM((rows, dims + 128), BF16), pltpu.SemaphoreType.DMA],
        flops=2 * rows * rows * dims, bytes_=rows * rows * 2 + rows * dims * 4, exps=rows * rows,
    )


def subtract_near(which, near, block, rest, candidates):
    rows, width = rest.shape
    members = lax.axis_size("member")
    tile = tile_of(rows)
    count = len(candidates)

    def body(near_ref, block_ref, rest_ref, *refs):
        others, (out_ref, v, sem) = refs[:count], refs[count:]

        @pl.when(pl.program_id(0) == 0)
        def _():
            pick(slots(near_ref, members)[which], others, v, sem)

        out_ref[...] = rest_ref[...] - dot(block_ref[...], v[...])

    return call(
        body,
        jax.ShapeDtypeStruct((rows, width), F32),
        (near, block, rest, *candidates),
        [SMEM_SPEC, by_rows(tile, rows), by_rows(tile, width)] + [ANY_SPEC] * count,
        by_rows(tile, width),
        grid=(rows // tile,),
        scratch=[VMEM((rows, width), BF16), pltpu.SemaphoreType.DMA],
        flops=2 * rows * rows * width, bytes_=rows * rows * 2 + rows * width * 10,
    )


def turn(near, block, rest, candidates, bases, coupled, ordered, low, high):
    rows, width = rest.shape
    rank = bases.shape[1]
    members = lax.axis_size("member")
    tile = tile_of(rows)
    count = len(candidates)

    def body(low_ref, high_ref, near_ref, block_ref, rest_ref, bases_ref, coupled_ref, ordered_ref, *refs):
        others, (first_ref, v_ref, coeff_ref, v, total, sem) = refs[:count], refs[count:]
        step = pl.program_id(0)

        @pl.when(step == 0)
        def _():
            pick(slots(near_ref, members)[1], others, v, sem)

        theta, keep, push = factors(low_ref, high_ref, width)
        own = bases_ref[...]
        first = rest_ref[...] - dot(block_ref[...], v[...]) - dot(own, coupled_ref[...])
        first_ref[...] = first
        moved = (keep * (ordered_ref[...] / theta) + push * first).astype(BF16)
        v_ref[...] = moved
        part = dot_tn(own, moved)

        @pl.when(step == 0)
        def _():
            total[...] = part

        @pl.when(step > 0)
        def _():
            total[...] += part

        @pl.when(step == pl.num_programs(0) - 1)
        def _():
            coeff_ref[...] = total[...].astype(BF16)

    return call(
        body,
        (jax.ShapeDtypeStruct((rows, width), F32), jax.ShapeDtypeStruct((rows, width), BF16),
         jax.ShapeDtypeStruct((rank, width), BF16)),
        (low, high, near, block, rest, bases, coupled, ordered, *candidates),
        [SMEM_SPEC, SMEM_SPEC, SMEM_SPEC, by_rows(tile, rows), by_rows(tile, width), by_rows(tile, rank),
         whole(coupled), by_rows(tile, width)] + [ANY_SPEC] * count,
        (by_rows(tile, width), by_rows(tile, width), pl.BlockSpec((rank, width), lambda i: (0, 0))),
        grid=(rows // tile,),
        scratch=[VMEM((rows, width), BF16), VMEM((rank, width), F32), pltpu.SemaphoreType.DMA],
        flops=2 * rows * rows * width, bytes_=rows * rows * 2 + rows * width * 16,
    )


def self_second(block, v, first, ordered, low, high):
    rows, width = first.shape
    tile = tile_of(rows)

    def body(low_ref, high_ref, block_ref, v_ref, first_ref, ordered_ref, solution_ref, rest_ref):
        theta, keep, push = factors(low_ref, high_ref, width)
        first = first_ref[...]
        step_zero = ordered_ref[...] / theta
        step_one = keep * step_zero + push * first
        solution_ref[...] = step_zero + step_one
        rest_ref[...] = first - RIDGE * step_one - dot(block_ref[...], v_ref[...])

    return call(
        body,
        (jax.ShapeDtypeStruct((rows, width), F32), jax.ShapeDtypeStruct((rows, width), F32)),
        (low, high, block, v, first, ordered),
        [SMEM_SPEC, SMEM_SPEC, by_rows(tile, rows), whole(v), by_rows(tile, width), by_rows(tile, width)],
        (by_rows(tile, width), by_rows(tile, width)),
        grid=(rows // tile,),
        flops=2 * rows * rows * width, bytes_=rows * rows * 2 + rows * width * 18,
    )


def final(near, block, rest, candidates, bases, coupled):
    rows, width = rest.shape
    rank = bases.shape[1]
    members = lax.axis_size("member")
    tile = tile_of(rows)
    count = len(candidates)

    def body(near_ref, block_ref, rest_ref, bases_ref, coupled_ref, *refs):
        others, (out_ref, v, sem) = refs[:count], refs[count:]

        @pl.when(pl.program_id(0) == 0)
        def _():
            pick(slots(near_ref, members)[1], others, v, sem)

        out_ref[...] = rest_ref[...] - dot(block_ref[...], v[...]) - dot(bases_ref[...], coupled_ref[...])

    return call(
        body,
        jax.ShapeDtypeStruct((rows, width), F32),
        (near, block, rest, bases, coupled, *candidates),
        [SMEM_SPEC, by_rows(tile, rows), by_rows(tile, width), by_rows(tile, rank), whole(coupled)]
        + [ANY_SPEC] * count,
        by_rows(tile, width),
        grid=(rows // tile,),
        scratch=[VMEM((rows, width), BF16), pltpu.SemaphoreType.DMA],
        flops=2 * rows * rows * width, bytes_=rows * rows * 2 + rows * width * 10,
    )


def merge(own, messages, first_own, first_messages):
    rank = own.shape[0]
    width = first_own.shape[1] - rank
    count = len(messages)

    def body(*refs):
        coeffs, firsts, out_ref = refs[: count + 1], refs[count + 1 : 2 * count + 2], refs[-1]
        total = None
        for coeff, carried in zip(coeffs, firsts):
            part = dot_tn(carried[:, width:], coeff[:, :width])
            total = part if total is None else total + part
        out_ref[...] = total.astype(BF16)

    args = (own, *messages, first_own, *first_messages)
    return call(
        body, jax.ShapeDtypeStruct((rank, width), BF16), args,
        [whole(a) for a in args], pl.BlockSpec((rank, width), lambda: (0, 0)),
        flops=2 * rank * rank * width * (count + 1), bytes_=rank * width * 2 * (2 * count + 3),
    )


def couple(near, couplings, transfer, cross, messages, merged):
    rank = transfer.shape[0]
    width = merged[0].shape[1]
    members = lax.axis_size("member")
    groups = lax.axis_size("group")

    def body(near_ref, couplings_ref, transfer_ref, cross_ref, *refs):
        coeffs, others, out_ref = refs[: members - 1], refs[members - 1 : -1], refs[-1]
        member = lax.axis_index("member")
        group = lax.axis_index("group")
        crossed = jnp.zeros((rank, width), F32)
        for k, other in enumerate(others):
            source = lax.rem(group + (groups - 1 - k), groups)
            crossed = crossed + dot(cross_ref[source], other[...])
        within = dot(transfer_ref[...], crossed.astype(BF16))
        for k, coeff in enumerate(coeffs):
            source = lax.rem(member + (members - 1 - k), members)
            far = (source != near_ref[0, 0]) & (source != near_ref[0, 1])
            within = within + jnp.where(far, 1.0, 0.0) * dot(couplings_ref[source], coeff[:, :width])
        out_ref[...] = within.astype(BF16)

    args = (near, couplings, transfer, cross, *messages, *merged)
    return call(
        body, jax.ShapeDtypeStruct((rank, width), BF16), args,
        [SMEM_SPEC] + [whole(a) for a in args[1:]], pl.BlockSpec((rank, width), lambda: (0, 0)),
        flops=2 * rank * rank * width * (members + groups), bytes_=rank * width * 2 * (members + groups) * 2,
    )


def around(array, axis):
    moved = []
    for k in range(1, lax.axis_size(axis)):
        moved.append(cycle(array, axis, k))
    return moved


def exchange(block):
    before = shift(block, "member", 1)
    after = shift(block, "member", -1)
    behind = shift(before, "member", 1)
    ahead = shift(after, "member", -1)
    return before, after, behind, ahead


def shards(
    points,
    right_sides,
    leaf_order,
    near_leaves,
    bases,
    couplings,
    transfers,
    cross_couplings,
    low_bound,
    high_bound,
):
    members = lax.axis_size("member")
    transfer = transfers[0]
    couplings = couplings[0]
    cross = cross_couplings[0]
    near = near_leaves
    low, high = low_bound, high_bound

    points_moved = exchange(points)
    points_a, points_b = slot_candidates(points_moved, members)
    ordered = right_sides.at[leaf_order[0]].get(mode="promise_in_bounds", unique_indices=True)
    v0, message = prep(ordered, bases, transfer, low, high)
    messages = around(message, "member")
    v0_a, v0_b = slot_candidates(exchange(v0), members)
    own_block, rest = self_first(points, ordered, v0, low, high)
    merged = merge(message, messages, message, messages)
    merged_all = around(merged, "group")
    coupled = couple(near, couplings, transfer, cross, messages, merged_all)
    block_a = near_block(0, near, points, points_a)
    rest = subtract_near(0, near, block_a, rest, v0_a)
    block_b = near_block(1, near, points, points_b)
    first, v1, coeff = turn(near, block_b, rest, v0_b, bases, coupled, ordered, low, high)

    coeffs = around(coeff, "member")
    v1_a, v1_b = slot_candidates(exchange(v1), members)
    solution_rows, rest = self_second(own_block, v1, first, ordered, low, high)
    merged = merge(coeff, coeffs, message, messages)
    merged_all = around(merged, "group")
    coupled = couple(near, couplings, transfer, cross, coeffs, merged_all)
    rest = subtract_near(0, near, block_a, rest, v1_a)
    residual = final(near, block_b, rest, v1_b, bases, coupled)
    return solution_rows, residual


def solution(mesh):
    return jax.shard_map(
        shards,
        mesh=mesh,
        in_specs=(
            P(("group", "member"), None),
            P(("group", "member"), None),
            P(("group", "member"), None),
            P(("group", "member"), None),
            P(("group", "member"), None),
            P(("group", "member"), None, None, None),
            P(("group", "member"), None, None),
            P("group", None, None, None),
            P(),
            P(),
        ),
        out_specs=(P(("group", "member"), None), P(("group", "member"), None)),
        check_vma=False,
    )
```

profile of v0, /device:TPU:0, one launch (start us, length us, event | category | flops | bytes accessed | tf_op | source)
XLA Modules:
  0.0 175.5 jit_solution(228172735211831045)
XLA Ops:
  2.8 3.7 %gather_fusion = f32[1536,256]{1,0:T(8,128)S(1)} fusion(f32[1536,256]{1,0:T(8,128)S(1)} %copy-done, s32[2048]{0:T(1024)S(1)} %pad_clamp_fusion), kind=kCustom, calls=%fused_computation | custom fusion | bytes 3151872 | tf_op jit(solution)/shard_map/gather | solution.py:465
  7.3 1.3 shard_map.113
  8.7 1.3 collective-permute-start.5
  10.0 5.6 %collective-permute-start.4 = (bf16[1536,256]{1,0:T(8,128)(2,1)S(1)}, bf16[1536,256]{1,0:T(8,128)(2,1)S(1)}, u32[]{:S(2)}, u32[]{:S(2)}) collective-permute-start(bf16[1536,256]{1,0:T(8,128)(2,1)S(1)} %get-tuple-element.11.v_ref), channel_id=1, source_target_pairs={{0,1},{1,2},{2,3},{4,5},{5,6},{6,7},{8,9},{9,10},{10,11},{12,13},{... | collective-permute-start | bytes 2359304 | tf_op jit(solution)/shard_map/ppermute | solution.py:23
  15.6 1.9 %collective-permute-start.8 = (bf16[128,384]{1,0:T(8,128)(2,1)S(1)}, bf16[128,384]{1,0:T(8,128)(2,1)S(1)}, u32[]{:S(2)}, u32[]{:S(2)}) collective-permute-start(bf16[128,384]{1,0:T(8,128)(2,1)S(1)} %get-tuple-element.14.refs_0_.refs_4_), channel_id=1, source_target_pairs={{0,3},{1,0},{2,1},{3,2},{4,7},{5,4},{6,5},{7,6},{8,11},{9,8},{10,9... | collective-permute-start | bytes 294920 | tf_op jit(solution)/shard_map/ppermute | solution.py:28
  17.5 1.6 collective-permute-start.7
  19.1 3.5 %collective-permute-start.1 = (bf16[1536,128]{1,0:T(8,128)(2,1)S(1)}, bf16[1536,128]{1,0:T(8,128)(2,1)S(1)}, u32[]{:S(2)}, u32[]{:S(2)}) collective-permute-start(bf16[1536,128]{1,0:T(8,128)(2,1)S(1)} %copy-done.2), channel_id=1, source_target_pairs={{0,1},{1,2},{2,3},{4,5},{5,6},{6,7},{8,9},{9,10},{10,11},{12,13},{... | collective-permute-start | bytes 1179656 | tf_op jit(solution)/shard_map/ppermute | solution.py:23
  22.6 13.0 %collective-permute-done.8.refs_3_.refs_7_.refs_2_ = bf16[128,384]{1,0:T(8,128)(2,1)S(1)} collective-permute-done((bf16[128,384]{1,0:T(8,128)(2,1)S(1)}, bf16[128,384]{1,0:T(8,128)(2,1)S(1)}, u32[]{:S(2)}, u32[]{:S(2)}) %collective-permute-start.8) | collective-permute-done | bytes 98336 | tf_op jit(solution)/shard_map/ppermute | solution.py:28
  35.6 1.3 collective-permute-start
  36.9 2.5 %collective-permute-done.7.refs_2_.refs_6_.refs_1_ = bf16[128,384]{1,0:T(8,128)(2,1)S(1)} collective-permute-done((bf16[128,384]{1,0:T(8,128)(2,1)S(1)}, bf16[128,384]{1,0:T(8,128)(2,1)S(1)}, u32[]{:S(2)}, u32[]{:S(2)}) %collective-permute-start.7) | collective-permute-done | bytes 98336 | tf_op jit(solution)/shard_map/ppermute | solution.py:28
  39.4 2.4 %collective-permute-start.6 = (bf16[128,384]{1,0:T(8,128)(2,1)S(1)}, bf16[128,384]{1,0:T(8,128)(2,1)S(1)}, u32[]{:S(2)}, u32[]{:S(2)}) collective-permute-start(bf16[128,384]{1,0:T(8,128)(2,1)S(1)} %get-tuple-element.14.refs_0_.refs_4_), channel_id=1, source_target_pairs={{0,1},{1,2},{2,3},{3,0},{4,5},{5,6},{6,7},{7,4},{8,9},{9,10},{10,1... | collective-permute-start | bytes 294920 | tf_op jit(solution)/shard_map/ppermute | solution.py:28
  41.8 8.3 %collective-permute-done.6.refs_1_.refs_5_.refs_0_ = bf16[128,384]{1,0:T(8,128)(2,1)S(1)} collective-permute-done((bf16[128,384]{1,0:T(8,128)(2,1)S(1)}, bf16[128,384]{1,0:T(8,128)(2,1)S(1)}, u32[]{:S(2)}, u32[]{:S(2)}) %collective-permute-start.6) | collective-permute-done | bytes 98336 | tf_op jit(solution)/shard_map/ppermute | solution.py:28
  50.4 1.4 collective-permute-start.17
  51.9 4.6 %collective-permute-start.16 = (bf16[1536,256]{1,0:T(8,128)(2,1)S(1)}, bf16[1536,256]{1,0:T(8,128)(2,1)S(1)}, u32[]{:S(2)}, u32[]{:S(2)}) collective-permute-start(bf16[1536,256]{1,0:T(8,128)(2,1)S(1)} %collective-permute-done.4.refs_0_), channel_id=1, source_target_pairs={{0,1},{1,2},{2,3},{4,5},{5,6},{6,7},{8,9},{9,10},{10,11},{12,13},{... | collective-permute-start | bytes 2359304 | tf_op jit(solution)/shard_map/ppermute | solution.py:23
  56.5 2.4 %collective-permute-start.14 = (bf16[128,256]{1,0:T(8,128)(2,1)S(1)}, bf16[128,256]{1,0:T(8,128)(2,1)S(1)}, u32[]{:S(2)}, u32[]{:S(2)}) collective-permute-start(bf16[128,256]{1,0:T(8,128)(2,1)S(1)} %shard_map.118), channel_id=1, source_target_pairs={{0,24},{4,28},{8,0},{12,4},{16,8},{20,12},{24,16},{28,20},{1,25},{... | collective-permute-start | bytes 196616 | tf_op jit(solution)/shard_map/ppermute | solution.py:28
  58.9 1.9 %collective-permute-done.14.refs_8_ = bf16[128,256]{1,0:T(8,128)(2,1)S(1)} collective-permute-done((bf16[128,256]{1,0:T(8,128)(2,1)S(1)}, bf16[128,256]{1,0:T(8,128)(2,1)S(1)}, u32[]{:S(2)}, u32[]{:S(2)}) %collective-permute-start.14) | collective-permute-done | bytes 65568 | tf_op jit(solution)/shard_map/ppermute | solution.py:28
  60.8 3.7 %collective-permute-done.13.refs_7_ = bf16[128,256]{1,0:T(8,128)(2,1)S(1)} collective-permute-done((bf16[128,256]{1,0:T(8,128)(2,1)S(1)}, bf16[128,256]{1,0:T(8,128)(2,1)S(1)}, u32[]{:S(2)}, u32[]{:S(2)}) %collective-permute-start.13) | collective-permute-done | bytes 65568 | tf_op jit(solution)/shard_map/ppermute | solution.py:28
  64.5 1.4 collective-permute-start.12
  65.9 3.3 %collective-permute-start.2 = (bf16[1536,128]{1,0:T(8,128)(2,1)S(1)}, bf16[1536,128]{1,0:T(8,128)(2,1)S(1)}, u32[]{:S(2)}, u32[]{:S(2)}) collective-permute-start(bf16[1536,128]{1,0:T(8,128)(2,1)S(1)} %collective-permute-done.1.rest_0_), channel_id=1, source_target_pairs={{0,1},{1,2},{2,3},{4,5},{5,6},{6,7},{8,9},{9,10},{10,11},{12,13},{... | collective-permute-start | bytes 1179656 | tf_op jit(solution)/shard_map/ppermute | solution.py:23
  69.2 1.3 collective-permute-start.3
  71.2 3.0 %collective-permute-done.11.refs_5_ = bf16[128,256]{1,0:T(8,128)(2,1)S(1)} collective-permute-done((bf16[128,256]{1,0:T(8,128)(2,1)S(1)}, bf16[128,256]{1,0:T(8,128)(2,1)S(1)}, u32[]{:S(2)}, u32[]{:S(2)}) %collective-permute-start.11) | collective-permute-done | bytes 65568 | tf_op jit(solution)/shard_map/ppermute | solution.py:28
  74.3 3.3 %collective-permute-start.10 = (bf16[128,256]{1,0:T(8,128)(2,1)S(1)}, bf16[128,256]{1,0:T(8,128)(2,1)S(1)}, u32[]{:S(2)}, u32[]{:S(2)}) collective-permute-start(bf16[128,256]{1,0:T(8,128)(2,1)S(1)} %shard_map.118), channel_id=1, source_target_pairs={{0,8},{4,12},{8,16},{12,20},{16,24},{20,28},{24,0},{28,4},{1,9},{5... | collective-permute-start | bytes 196616 | tf_op jit(solution)/shard_map/ppermute | solution.py:28
  77.6 2.6 %collective-permute-done.10.refs_4_ = bf16[128,256]{1,0:T(8,128)(2,1)S(1)} collective-permute-done((bf16[128,256]{1,0:T(8,128)(2,1)S(1)}, bf16[128,256]{1,0:T(8,128)(2,1)S(1)}, u32[]{:S(2)}, u32[]{:S(2)}) %collective-permute-start.10) | collective-permute-done | bytes 65568 | tf_op jit(solution)/shard_map/ppermute | solution.py:28
  80.3 5.1 %shard_map.114 = (bf16[1536,1536]{1,0:T(8,128)(2,1)S(1)}, f32[1536,256]{1,0:T(8,128)S(1)}) custom-call(f32[1]{0:T(128)S(6)} %copy.12.low_ref, f32[1]{0:T(128)S(6)} %copy.13.high_ref, bf16[1536,128]{1,0:T(8,128)(2,1)S(1)} %copy-done.2, f32[1536,256]{1,0:T(8,128)S(1)} %gather_fusion, bf16[1536,256]{1,0:T(8,128)(2,1)S(1)} %get-tuple-element.11.v_ref), custom_call_target="tpu_custom_call" | custom-call | flops 1811939328 | bytes 8650752 | tf_op jit(solution)/shard_map/pallas_call | solution.py:49
  85.5 1.1 shard_map.119.coupled_ref
  86.6 4.1 %shard_map.116.block_ref = bf16[1536,1536]{1,0:T(8,128)(2,1)S(1)} custom-call(s32[1,2]{1,0:T(1,128)S(1)} %copy-done.6, bf16[1536,128]{1,0:T(8,128)(2,1)S(1)} %copy-done.2, bf16[1536,128]{1,0:T(8,128)(2,1)S(1)} %collective-permute-done.1.rest_0_, bf16[1536,128]{1,0:T(8,128)(2,1)S(1)} %collective-permute-done.rest_0_.rest_1_), custom_call_target="tpu_custom_call" | custom-call | flops 603979776 | bytes 5505024 | tf_op jit(solution)/shard_map/pallas_call | solution.py:49
  90.7 4.1 %shard_map.115.block_ref = bf16[1536,1536]{1,0:T(8,128)(2,1)S(1)} custom-call(s32[1,2]{1,0:T(1,128)S(1)} %copy-done.6, bf16[1536,128]{1,0:T(8,128)(2,1)S(1)} %copy-done.2, bf16[1536,128]{1,0:T(8,128)(2,1)S(1)} %collective-permute-done.rest_0_.rest_1_, bf16[1536,128]{1,0:T(8,128)(2,1)S(1)} %collective-permute-done.2.rest_1_, ...), custom_call_target="tpu_custom_call" | custom-call | flops 603979776 | bytes 5505024 | tf_op jit(solution)/shard_map/pallas_call | solution.py:49
  94.8 3.0 %shard_map.117.rest_ref = f32[1536,256]{1,0:T(8,128)S(1)} custom-call(s32[1,2]{1,0:T(1,128)S(1)} %copy-done.6, bf16[1536,1536]{1,0:T(8,128)(2,1)S(1)} %shard_map.116.block_ref, f32[1536,256]{1,0:T(8,128)S(1)} %get-tuple-element.13.rest_ref, bf16[1536,256]{1,0:T(8,128)(2,1)S(1)} %collective-permute-done.4.refs_0_, ...), custom_call_target="tpu_custom_call" | custom-call | flops 1207959552 | bytes 8650752 | tf_op jit(solution)/shard_map/pallas_call | solution.py:49
  97.8 4.4 %shard_map.120 = (f32[1536,256]{1,0:T(8,128)S(1)}, bf16[1536,256]{1,0:T(8,128)(2,1)S(1)}, bf16[128,256]{1,0:T(8,128)(2,1)S(1)}) custom-call(f32[1]{0:T(128)S(6)} %copy.12.low_ref, f32[1]{0:T(128)S(6)} %copy.13.high_ref, s32[1,2]{1,0:T(1,128)S(1)} %copy-done.6, bf16[1536,1536]{1,0:T(8,128)(2,1)S(1)} %shard_map.115.block_ref, ...), custom_call_target="tpu_custom_call" | custom-call | flops 1207959552 | bytes 11010048 | tf_op jit(solution)/shard_map/pallas_call | solution.py:49
  102.2 1.3 collective-permute-start.19
  103.5 5.2 %collective-permute-start.18 = (bf16[1536,256]{1,0:T(8,128)(2,1)S(1)}, bf16[1536,256]{1,0:T(8,128)(2,1)S(1)}, u32[]{:S(2)}, u32[]{:S(2)}) collective-permute-start(bf16[1536,256]{1,0:T(8,128)(2,1)S(1)} %get-tuple-element.15.v_ref), channel_id=1, source_target_pairs={{0,1},{1,2},{2,3},{4,5},{5,6},{6,7},{8,9},{9,10},{10,11},{12,13},{... | collective-permute-start | bytes 2359304 | tf_op jit(solution)/shard_map/ppermute | solution.py:23
  108.8 15.4 %collective-permute-done.19.refs_1_.refs_0_ = bf16[1536,256]{1,0:T(8,128)(2,1)S(1)} collective-permute-done((bf16[1536,256]{1,0:T(8,128)(2,1)S(1)}, bf16[1536,256]{1,0:T(8,128)(2,1)S(1)}, u32[]{:S(2)}, u32[]{:S(2)}) %collective-permute-start.19) | collective-permute-done | bytes 786464 | tf_op jit(solution)/shard_map/ppermute | solution.py:23
  124.2 1.3 collective-permute-start.31
  125.9 4.4 %collective-permute-start.30 = (bf16[1536,256]{1,0:T(8,128)(2,1)S(1)}, bf16[1536,256]{1,0:T(8,128)(2,1)S(1)}, u32[]{:S(2)}, u32[]{:S(2)}) collective-permute-start(bf16[1536,256]{1,0:T(8,128)(2,1)S(1)} %collective-permute-done.18.refs_0_), channel_id=1, source_target_pairs={{0,1},{1,2},{2,3},{4,5},{5,6},{6,7},{8,9},{9,10},{10,11},{12,13},{... | collective-permute-start | bytes 2359304 | tf_op jit(solution)/shard_map/ppermute | solution.py:23
  130.4 2.6 %collective-permute-start.22 = (bf16[128,256]{1,0:T(8,128)(2,1)S(1)}, bf16[128,256]{1,0:T(8,128)(2,1)S(1)}, u32[]{:S(2)}, u32[]{:S(2)}) collective-permute-start(bf16[128,256]{1,0:T(8,128)(2,1)S(1)} %get-tuple-element.19.refs_0_), channel_id=1, source_target_pairs={{0,3},{1,0},{2,1},{3,2},{4,7},{5,4},{6,5},{7,6},{8,11},{9,8},{10,9... | collective-permute-start | bytes 196616 | tf_op jit(solution)/shard_map/ppermute | solution.py:28
  133.0 1.3 collective-permute-start.21
  134.3 1.9 %collective-permute-start.20 = (bf16[128,256]{1,0:T(8,128)(2,1)S(1)}, bf16[128,256]{1,0:T(8,128)(2,1)S(1)}, u32[]{:S(2)}, u32[]{:S(2)}) collective-permute-start(bf16[128,256]{1,0:T(8,128)(2,1)S(1)} %get-tuple-element.19.refs_0_), channel_id=1, source_target_pairs={{0,1},{1,2},{2,3},{3,0},{4,5},{5,6},{6,7},{7,4},{8,9},{9,10},{10,1... | collective-permute-start | bytes 196616 | tf_op jit(solution)/shard_map/ppermute | solution.py:28
  136.2 13.5 %collective-permute-done.22.refs_3_.refs_2_ = bf16[128,256]{1,0:T(8,128)(2,1)S(1)} collective-permute-done((bf16[128,256]{1,0:T(8,128)(2,1)S(1)}, bf16[128,256]{1,0:T(8,128)(2,1)S(1)}, u32[]{:S(2)}, u32[]{:S(2)}) %collective-permute-start.22) | collective-permute-done | bytes 65568 | tf_op jit(solution)/shard_map/ppermute | solution.py:28
  149.7 1.4 collective-permute-done.21.refs_2_.refs_1_
  151.1 2.8 %collective-permute-done.20.refs_1_.refs_0_ = bf16[128,256]{1,0:T(8,128)(2,1)S(1)} collective-permute-done((bf16[128,256]{1,0:T(8,128)(2,1)S(1)}, bf16[128,256]{1,0:T(8,128)(2,1)S(1)}, u32[]{:S(2)}, u32[]{:S(2)}) %collective-permute-start.20) | collective-permute-done | bytes 65568 | tf_op jit(solution)/shard_map/ppermute | solution.py:28
  155.9 1.3 collective-permute-start.27
  157.2 1.3 collective-permute-start.26
  158.5 1.4 collective-permute-done.28.refs_8_
  159.9 1.1 collective-permute-start.25
  161.0 1.3 collective-permute-start.24
  162.6 3.4 %shard_map.121 = (f32[1536,256]{1,0:T(8,128)}, f32[1536,256]{1,0:T(8,128)S(1)}) custom-call(f32[1]{0:T(128)S(6)} %copy.12.low_ref, f32[1]{0:T(128)S(6)} %copy.13.high_ref, bf16[1536,1536]{1,0:T(8,128)(2,1)S(1)} %get-tuple-element.12.block_ref, bf16[1536,256]{1,0:T(8,128)(2,1)S(1)} %get-tuple-element.15.v_ref, f32[1536,256]{1,0:T(8,128)S(1)} %get-tuple-element.16.first_ref, ...), custom_call_target="tpu_custom_call" | custom-call | flops 1207959552 | bytes 11796480 | tf_op jit(solution)/shard_map/pallas_call | solution.py:49
  168.0 3.0 %shard_map.122.rest_ref = f32[1536,256]{1,0:T(8,128)S(1)} custom-call(s32[1,2]{1,0:T(1,128)S(1)} %copy-done.6, bf16[1536,1536]{1,0:T(8,128)(2,1)S(1)} %shard_map.116.block_ref, f32[1536,256]{1,0:T(8,128)S(1)} %get-tuple-element.18.rest_ref, bf16[1536,256]{1,0:T(8,128)(2,1)S(1)} %collective-permute-done.18.refs_0_, ...), custom_call_target="tpu_custom_call" | custom-call | flops 1207959552 | bytes 8650752 | tf_op jit(solution)/shard_map/pallas_call | solution.py:49
  171.0 4.5 %shard_map.125 = f32[1536,256]{1,0:T(8,128)} custom-call(s32[1,2]{1,0:T(1,128)S(1)} %copy-done.6, bf16[1536,1536]{1,0:T(8,128)(2,1)S(1)} %shard_map.115.block_ref, f32[1536,256]{1,0:T(8,128)S(1)} %shard_map.122.rest_ref, bf16[1536,128]{1,0:T(8,128)(2,1)S(1)} %copy-done.1, bf16[128,256]{1,0:T(8,128)(2,1)S(1)} %shard_map.124.coupled_ref, ...), custom_call_target="tpu_custom_call" | custom-call | flops 1207959552 | bytes 8650752 | tf_op jit(solution)/shard_map/pallas_call | solution.py:49
  (46 shorter events, 7.5 us)
Async XLA Ops:
  0.6 2.2 %copy-start = (f32[1536,256]{1,0:T(8,128)S(1)}, f32[1536,256]{1,0:T(8,128)}, u32[]{:S(2)}) copy-start(f32[1536,256]{1,0:T(8,128)} %param.11) | copy-start | bytes 4718596
  2.8 3.7 %copy-start.1 = (bf16[1536,128]{1,0:T(8,128)(2,1)S(1)}, bf16[1536,128]{1,0:T(8,128)(2,1)}, u32[]{:S(2)}) copy-start(bf16[1536,128]{1,0:T(8,128)(2,1)} %bases_ref.5) | copy-start | bytes 1179652
  6.5 12.6 %copy-start.2 = (bf16[1536,128]{1,0:T(8,128)(2,1)S(1)}, bf16[1536,128]{1,0:T(8,128)(2,1)}, u32[]{:S(2)}) copy-start(bf16[1536,128]{1,0:T(8,128)(2,1)} %points_ref.5) | copy-start | bytes 1179652
  6.5 0.8 copy-start.5
  8.7 41.8 %collective-permute-start.5 = (bf16[1536,256]{1,0:T(8,128)(2,1)S(1)}, bf16[1536,256]{1,0:T(8,128)(2,1)S(1)}, u32[]{:S(2)}, u32[]{:S(2)}) collective-permute-start(bf16[1536,256]{1,0:T(8,128)(2,1)S(1)} %get-tuple-element.11.v_ref), channel_id=1, source_target_pairs={{1,0},{2,1},{3,2},{5,4},{6,5},{7,6},{9,8},{10,9},{11,10},{13,12},{... | collective-permute-start | bytes 2359304 | tf_op jit(solution)/shard_map/ppermute | solution.py:23
  10.0 41.9 %collective-permute-start.4 = (bf16[1536,256]{1,0:T(8,128)(2,1)S(1)}, bf16[1536,256]{1,0:T(8,128)(2,1)S(1)}, u32[]{:S(2)}, u32[]{:S(2)}) collective-permute-start(bf16[1536,256]{1,0:T(8,128)(2,1)S(1)} %get-tuple-element.11.v_ref), channel_id=1, source_target_pairs={{0,1},{1,2},{2,3},{4,5},{5,6},{6,7},{8,9},{9,10},{10,11},{12,13},{... | collective-permute-start | bytes 2359304 | tf_op jit(solution)/shard_map/ppermute | solution.py:23
  15.6 20.0 %collective-permute-start.8 = (bf16[128,384]{1,0:T(8,128)(2,1)S(1)}, bf16[128,384]{1,0:T(8,128)(2,1)S(1)}, u32[]{:S(2)}, u32[]{:S(2)}) collective-permute-start(bf16[128,384]{1,0:T(8,128)(2,1)S(1)} %get-tuple-element.14.refs_0_.refs_4_), channel_id=1, source_target_pairs={{0,3},{1,0},{2,1},{3,2},{4,7},{5,4},{6,5},{7,6},{8,11},{9,8},{10,9... | collective-permute-start | bytes 294920 | tf_op jit(solution)/shard_map/ppermute | solution.py:28
  17.5 21.9 %collective-permute-start.7 = (bf16[128,384]{1,0:T(8,128)(2,1)S(1)}, bf16[128,384]{1,0:T(8,128)(2,1)S(1)}, u32[]{:S(2)}, u32[]{:S(2)}) collective-permute-start(bf16[128,384]{1,0:T(8,128)(2,1)S(1)} %get-tuple-element.14.refs_0_.refs_4_), channel_id=1, source_target_pairs={{0,2},{1,3},{2,0},{3,1},{4,6},{5,7},{6,4},{7,5},{8,10},{9,11},{10,... | collective-permute-start | bytes 294920 | tf_op jit(solution)/shard_map/ppermute | solution.py:28
  19.1 46.8 %collective-permute-start.1 = (bf16[1536,128]{1,0:T(8,128)(2,1)S(1)}, bf16[1536,128]{1,0:T(8,128)(2,1)S(1)}, u32[]{:S(2)}, u32[]{:S(2)}) collective-permute-start(bf16[1536,128]{1,0:T(8,128)(2,1)S(1)} %copy-done.2), channel_id=1, source_target_pairs={{0,1},{1,2},{2,3},{4,5},{5,6},{6,7},{8,9},{9,10},{10,11},{12,13},{... | collective-permute-start | bytes 1179656 | tf_op jit(solution)/shard_map/ppermute | solution.py:23
  35.6 33.6 %collective-permute-start = (bf16[1536,128]{1,0:T(8,128)(2,1)S(1)}, bf16[1536,128]{1,0:T(8,128)(2,1)S(1)}, u32[]{:S(2)}, u32[]{:S(2)}) collective-permute-start(bf16[1536,128]{1,0:T(8,128)(2,1)S(1)} %copy-done.2), channel_id=1, source_target_pairs={{1,0},{2,1},{3,2},{5,4},{6,5},{7,6},{9,8},{10,9},{11,10},{13,12},{... | collective-permute-start | bytes 1179656 | tf_op jit(solution)/shard_map/ppermute | solution.py:23
  39.4 10.7 %collective-permute-start.6 = (bf16[128,384]{1,0:T(8,128)(2,1)S(1)}, bf16[128,384]{1,0:T(8,128)(2,1)S(1)}, u32[]{:S(2)}, u32[]{:S(2)}) collective-permute-start(bf16[128,384]{1,0:T(8,128)(2,1)S(1)} %get-tuple-element.14.refs_0_.refs_4_), channel_id=1, source_target_pairs={{0,1},{1,2},{2,3},{3,0},{4,5},{5,6},{6,7},{7,4},{8,9},{9,10},{10,1... | collective-permute-start | bytes 294920 | tf_op jit(solution)/shard_map/ppermute | solution.py:28
  50.3 35.1 %copy-start.3 = (bf16[1,8,128,128]{3,2,1,0:T(8,128)(2,1)S(1)}, bf16[1,8,128,128]{3,2,1,0:T(8,128)(2,1)}, u32[]{:S(2)}) copy-start(bf16[1,8,128,128]{3,2,1,0:T(8,128)(2,1)} %param.17) | copy-start | bytes 786436
  50.3 35.1 %copy-start.4 = (bf16[1,4,128,128]{3,2,1,0:T(8,128)(2,1)S(1)}, bf16[1,4,128,128]{3,2,1,0:T(8,128)(2,1)}, u32[]{:S(2)}) copy-start(bf16[1,4,128,128]{3,2,1,0:T(8,128)(2,1)} %param.15) | copy-start | bytes 393220
  50.3 35.1 %copy-start.6 = (s32[1,2]{1,0:T(1,128)S(1)}, s32[1,2]{1,0:T(1,128)}, u32[]{:S(2)}) copy-start(s32[1,2]{1,0:T(1,128)} %near_ref.15) | copy-start | bytes 28
  50.4 6.1 %collective-permute-start.15 = (bf16[128,256]{1,0:T(8,128)(2,1)S(1)}, bf16[128,256]{1,0:T(8,128)(2,1)S(1)}, u32[]{:S(2)}, u32[]{:S(2)}) collective-permute-start(bf16[128,256]{1,0:T(8,128)(2,1)S(1)} %shard_map.118), channel_id=1, source_target_pairs={{0,28},{4,0},{8,4},{12,8},{16,12},{20,16},{24,20},{28,24},{1,29},{... | collective-permute-start | bytes 196616 | tf_op jit(solution)/shard_map/ppermute | solution.py:28
  50.4 47.4 %collective-permute-start.17 = (bf16[1536,256]{1,0:T(8,128)(2,1)S(1)}, bf16[1536,256]{1,0:T(8,128)(2,1)S(1)}, u32[]{:S(2)}, u32[]{:S(2)}) collective-permute-start(bf16[1536,256]{1,0:T(8,128)(2,1)S(1)} %collective-permute-done.5.refs_1_.refs_0_), channel_id=1, source_target_pairs={{1,0},{2,1},{3,2},{5,4},{6,5},{7,6},{9,8},{10,9},{11,10},{13,12},{... | collective-permute-start | bytes 2359304 | tf_op jit(solution)/shard_map/ppermute | solution.py:23
  51.9 45.9 %collective-permute-start.16 = (bf16[1536,256]{1,0:T(8,128)(2,1)S(1)}, bf16[1536,256]{1,0:T(8,128)(2,1)S(1)}, u32[]{:S(2)}, u32[]{:S(2)}) collective-permute-start(bf16[1536,256]{1,0:T(8,128)(2,1)S(1)} %collective-permute-done.4.refs_0_), channel_id=1, source_target_pairs={{0,1},{1,2},{2,3},{4,5},{5,6},{6,7},{8,9},{9,10},{10,11},{12,13},{... | collective-permute-start | bytes 2359304 | tf_op jit(solution)/shard_map/ppermute | solution.py:23
  56.5 4.3 %collective-permute-start.14 = (bf16[128,256]{1,0:T(8,128)(2,1)S(1)}, bf16[128,256]{1,0:T(8,128)(2,1)S(1)}, u32[]{:S(2)}, u32[]{:S(2)}) collective-permute-start(bf16[128,256]{1,0:T(8,128)(2,1)S(1)} %shard_map.118), channel_id=1, source_target_pairs={{0,24},{4,28},{8,0},{12,4},{16,8},{20,12},{24,16},{28,20},{1,25},{... | collective-permute-start | bytes 196616 | tf_op jit(solution)/shard_map/ppermute | solution.py:28
  60.8 3.7 %collective-permute-start.13 = (bf16[128,256]{1,0:T(8,128)(2,1)S(1)}, bf16[128,256]{1,0:T(8,128)(2,1)S(1)}, u32[]{:S(2)}, u32[]{:S(2)}) collective-permute-start(bf16[128,256]{1,0:T(8,128)(2,1)S(1)} %shard_map.118), channel_id=1, source_target_pairs={{0,20},{4,24},{8,28},{12,0},{16,4},{20,8},{24,12},{28,16},{1,21},{... | collective-permute-start | bytes 196616 | tf_op jit(solution)/shard_map/ppermute | solution.py:28
  64.5 6.0 %collective-permute-start.12 = (bf16[128,256]{1,0:T(8,128)(2,1)S(1)}, bf16[128,256]{1,0:T(8,128)(2,1)S(1)}, u32[]{:S(2)}, u32[]{:S(2)}) collective-permute-start(bf16[128,256]{1,0:T(8,128)(2,1)S(1)} %shard_map.118), channel_id=1, source_target_pairs={{0,16},{4,20},{8,24},{12,28},{16,0},{20,4},{24,8},{28,12},{1,17},{... | collective-permute-start | bytes 196616 | tf_op jit(solution)/shard_map/ppermute | solution.py:28
  65.9 24.8 %collective-permute-start.2 = (bf16[1536,128]{1,0:T(8,128)(2,1)S(1)}, bf16[1536,128]{1,0:T(8,128)(2,1)S(1)}, u32[]{:S(2)}, u32[]{:S(2)}) collective-permute-start(bf16[1536,128]{1,0:T(8,128)(2,1)S(1)} %collective-permute-done.1.rest_0_), channel_id=1, source_target_pairs={{0,1},{1,2},{2,3},{4,5},{5,6},{6,7},{8,9},{9,10},{10,11},{12,13},{... | collective-permute-start | bytes 1179656 | tf_op jit(solution)/shard_map/ppermute | solution.py:23
  69.2 21.4 %collective-permute-start.3 = (bf16[1536,128]{1,0:T(8,128)(2,1)S(1)}, bf16[1536,128]{1,0:T(8,128)(2,1)S(1)}, u32[]{:S(2)}, u32[]{:S(2)}) collective-permute-start(bf16[1536,128]{1,0:T(8,128)(2,1)S(1)} %collective-permute-done.rest_0_.rest_1_), channel_id=1, source_target_pairs={{1,0},{2,1},{3,2},{5,4},{6,5},{7,6},{9,8},{10,9},{11,10},{13,12},{... | collective-permute-start | bytes 1179656 | tf_op jit(solution)/shard_map/ppermute | solution.py:23
  70.5 3.7 %collective-permute-start.11 = (bf16[128,256]{1,0:T(8,128)(2,1)S(1)}, bf16[128,256]{1,0:T(8,128)(2,1)S(1)}, u32[]{:S(2)}, u32[]{:S(2)}) collective-permute-start(bf16[128,256]{1,0:T(8,128)(2,1)S(1)} %shard_map.118), channel_id=1, source_target_pairs={{0,12},{4,16},{8,20},{12,24},{16,28},{20,0},{24,4},{28,8},{1,13},{... | collective-permute-start | bytes 196616 | tf_op jit(solution)/shard_map/ppermute | solution.py:28
  74.3 5.8 %collective-permute-start.10 = (bf16[128,256]{1,0:T(8,128)(2,1)S(1)}, bf16[128,256]{1,0:T(8,128)(2,1)S(1)}, u32[]{:S(2)}, u32[]{:S(2)}) collective-permute-start(bf16[128,256]{1,0:T(8,128)(2,1)S(1)} %shard_map.118), channel_id=1, source_target_pairs={{0,8},{4,12},{8,16},{12,20},{16,24},{20,28},{24,0},{28,4},{1,9},{5... | collective-permute-start | bytes 196616 | tf_op jit(solution)/shard_map/ppermute | solution.py:28
  80.1 5.3 %collective-permute-start.9 = (bf16[128,256]{1,0:T(8,128)(2,1)S(1)}, bf16[128,256]{1,0:T(8,128)(2,1)S(1)}, u32[]{:S(2)}, u32[]{:S(2)}) collective-permute-start(bf16[128,256]{1,0:T(8,128)(2,1)S(1)} %shard_map.118), channel_id=1, source_target_pairs={{0,4},{4,8},{8,12},{12,16},{16,20},{20,24},{24,28},{28,0},{1,5},{5... | collective-permute-start | bytes 196616 | tf_op jit(solution)/shard_map/ppermute | solution.py:28
  102.2 22.0 %collective-permute-start.19 = (bf16[1536,256]{1,0:T(8,128)(2,1)S(1)}, bf16[1536,256]{1,0:T(8,128)(2,1)S(1)}, u32[]{:S(2)}, u32[]{:S(2)}) collective-permute-start(bf16[1536,256]{1,0:T(8,128)(2,1)S(1)} %get-tuple-element.15.v_ref), channel_id=1, source_target_pairs={{1,0},{2,1},{3,2},{5,4},{6,5},{7,6},{9,8},{10,9},{11,10},{13,12},{... | collective-permute-start | bytes 2359304 | tf_op jit(solution)/shard_map/ppermute | solution.py:23
  103.5 22.4 %collective-permute-start.18 = (bf16[1536,256]{1,0:T(8,128)(2,1)S(1)}, bf16[1536,256]{1,0:T(8,128)(2,1)S(1)}, u32[]{:S(2)}, u32[]{:S(2)}) collective-permute-start(bf16[1536,256]{1,0:T(8,128)(2,1)S(1)} %get-tuple-element.15.v_ref), channel_id=1, source_target_pairs={{0,1},{1,2},{2,3},{4,5},{5,6},{6,7},{8,9},{9,10},{10,11},{12,13},{... | collective-permute-start | bytes 2359304 | tf_op jit(solution)/shard_map/ppermute | solution.py:23
  124.2 46.8 %collective-permute-start.31 = (bf16[1536,256]{1,0:T(8,128)(2,1)S(1)}, bf16[1536,256]{1,0:T(8,128)(2,1)S(1)}, u32[]{:S(2)}, u32[]{:S(2)}) collective-permute-start(bf16[1536,256]{1,0:T(8,128)(2,1)S(1)} %collective-permute-done.19.refs_1_.refs_0_), channel_id=1, source_target_pairs={{1,0},{2,1},{3,2},{5,4},{6,5},{7,6},{9,8},{10,9},{11,10},{13,12},{... | collective-permute-start | bytes 2359304 | tf_op jit(solution)/shard_map/ppermute | solution.py:23
  125.9 45.1 %collective-permute-start.30 = (bf16[1536,256]{1,0:T(8,128)(2,1)S(1)}, bf16[1536,256]{1,0:T(8,128)(2,1)S(1)}, u32[]{:S(2)}, u32[]{:S(2)}) collective-permute-start(bf16[1536,256]{1,0:T(8,128)(2,1)S(1)} %collective-permute-done.18.refs_0_), channel_id=1, source_target_pairs={{0,1},{1,2},{2,3},{4,5},{5,6},{6,7},{8,9},{9,10},{10,11},{12,13},{... | collective-permute-start | bytes 2359304 | tf_op jit(solution)/shard_map/ppermute | solution.py:23
  130.4 19.3 %collective-permute-start.22 = (bf16[128,256]{1,0:T(8,128)(2,1)S(1)}, bf16[128,256]{1,0:T(8,128)(2,1)S(1)}, u32[]{:S(2)}, u32[]{:S(2)}) collective-permute-start(bf16[128,256]{1,0:T(8,128)(2,1)S(1)} %get-tuple-element.19.refs_0_), channel_id=1, source_target_pairs={{0,3},{1,0},{2,1},{3,2},{4,7},{5,4},{6,5},{7,6},{8,11},{9,8},{10,9... | collective-permute-start | bytes 196616 | tf_op jit(solution)/shard_map/ppermute | solution.py:28
  133.0 18.1 %collective-permute-start.21 = (bf16[128,256]{1,0:T(8,128)(2,1)S(1)}, bf16[128,256]{1,0:T(8,128)(2,1)S(1)}, u32[]{:S(2)}, u32[]{:S(2)}) collective-permute-start(bf16[128,256]{1,0:T(8,128)(2,1)S(1)} %get-tuple-element.19.refs_0_), channel_id=1, source_target_pairs={{0,2},{1,3},{2,0},{3,1},{4,6},{5,7},{6,4},{7,5},{8,10},{9,11},{10,... | collective-permute-start | bytes 196616 | tf_op jit(solution)/shard_map/ppermute | solution.py:28
  134.3 19.6 %collective-permute-start.20 = (bf16[128,256]{1,0:T(8,128)(2,1)S(1)}, bf16[128,256]{1,0:T(8,128)(2,1)S(1)}, u32[]{:S(2)}, u32[]{:S(2)}) collective-permute-start(bf16[128,256]{1,0:T(8,128)(2,1)S(1)} %get-tuple-element.19.refs_0_), channel_id=1, source_target_pairs={{0,1},{1,2},{2,3},{3,0},{4,5},{5,6},{6,7},{7,4},{8,9},{9,10},{10,1... | collective-permute-start | bytes 196616 | tf_op jit(solution)/shard_map/ppermute | solution.py:28
  154.1 3.1 %collective-permute-start.29 = (bf16[128,256]{1,0:T(8,128)(2,1)S(1)}, bf16[128,256]{1,0:T(8,128)(2,1)S(1)}, u32[]{:S(2)}, u32[]{:S(2)}) collective-permute-start(bf16[128,256]{1,0:T(8,128)(2,1)S(1)} %shard_map.123), channel_id=1, source_target_pairs={{0,28},{4,0},{8,4},{12,8},{16,12},{20,16},{24,20},{28,24},{1,29},{... | collective-permute-start | bytes 196616 | tf_op jit(solution)/shard_map/ppermute | solution.py:28
  154.9 5.0 %collective-permute-start.28 = (bf16[128,256]{1,0:T(8,128)(2,1)S(1)}, bf16[128,256]{1,0:T(8,128)(2,1)S(1)}, u32[]{:S(2)}, u32[]{:S(2)}) collective-permute-start(bf16[128,256]{1,0:T(8,128)(2,1)S(1)} %shard_map.123), channel_id=1, source_target_pairs={{0,24},{4,28},{8,0},{12,4},{16,8},{20,12},{24,16},{28,20},{1,25},{... | collective-permute-start | bytes 196616 | tf_op jit(solution)/shard_map/ppermute | solution.py:28
  155.9 5.1 %collective-permute-start.27 = (bf16[128,256]{1,0:T(8,128)(2,1)S(1)}, bf16[128,256]{1,0:T(8,128)(2,1)S(1)}, u32[]{:S(2)}, u32[]{:S(2)}) collective-permute-start(bf16[128,256]{1,0:T(8,128)(2,1)S(1)} %shard_map.123), channel_id=1, source_target_pairs={{0,20},{4,24},{8,28},{12,0},{16,4},{20,8},{24,12},{28,16},{1,21},{... | collective-permute-start | bytes 196616 | tf_op jit(solution)/shard_map/ppermute | solution.py:28
  157.2 5.2 %collective-permute-start.26 = (bf16[128,256]{1,0:T(8,128)(2,1)S(1)}, bf16[128,256]{1,0:T(8,128)(2,1)S(1)}, u32[]{:S(2)}, u32[]{:S(2)}) collective-permute-start(bf16[128,256]{1,0:T(8,128)(2,1)S(1)} %shard_map.123), channel_id=1, source_target_pairs={{0,16},{4,20},{8,24},{12,28},{16,0},{20,4},{24,8},{28,12},{1,17},{... | collective-permute-start | bytes 196616 | tf_op jit(solution)/shard_map/ppermute | solution.py:28
  159.9 6.1 %collective-permute-start.25 = (bf16[128,256]{1,0:T(8,128)(2,1)S(1)}, bf16[128,256]{1,0:T(8,128)(2,1)S(1)}, u32[]{:S(2)}, u32[]{:S(2)}) collective-permute-start(bf16[128,256]{1,0:T(8,128)(2,1)S(1)} %shard_map.123), channel_id=1, source_target_pairs={{0,12},{4,16},{8,20},{12,24},{16,28},{20,0},{24,4},{28,8},{1,13},{... | collective-permute-start | bytes 196616 | tf_op jit(solution)/shard_map/ppermute | solution.py:28
  161.0 5.2 %collective-permute-start.24 = (bf16[128,256]{1,0:T(8,128)(2,1)S(1)}, bf16[128,256]{1,0:T(8,128)(2,1)S(1)}, u32[]{:S(2)}, u32[]{:S(2)}) collective-permute-start(bf16[128,256]{1,0:T(8,128)(2,1)S(1)} %shard_map.123), channel_id=1, source_target_pairs={{0,8},{4,12},{8,16},{12,20},{16,24},{20,28},{24,0},{28,4},{1,9},{5... | collective-permute-start | bytes 196616 | tf_op jit(solution)/shard_map/ppermute | solution.py:28
  162.3 4.6 %collective-permute-start.23 = (bf16[128,256]{1,0:T(8,128)(2,1)S(1)}, bf16[128,256]{1,0:T(8,128)(2,1)S(1)}, u32[]{:S(2)}, u32[]{:S(2)}) collective-permute-start(bf16[128,256]{1,0:T(8,128)(2,1)S(1)} %shard_map.123), channel_id=1, source_target_pairs={{0,4},{4,8},{8,12},{12,16},{16,20},{20,24},{24,28},{28,0},{1,5},{5... | collective-permute-start | bytes 196616 | tf_op jit(solution)/shard_map/ppermute | solution.py:28
where the time goes:
time: 177 us; the launch traced here: 176 us
  waiting for transfers between devices  70.9 us (40%)
  starting transfers between devices  61.3 us (35%)
  Pallas kernels  35.6 us (20%)
  local copies, waits for them, and re-layouts  4.51 us (3%)
  between operations  2.46 us (1%)
    ppermute x20, waiting for transfers between devices, cycle(): lax.ppermute(array, axis, [(i, (i + by) % count) for i in range(count)])  55 us
    pallas_call x13, Pallas kernels, call(): pl.pallas_call(body, out_shape=out, grid=grid, in_specs=in_specs, out_spe...  35.6 us
    ppermute x12, starting transfers between devices, shift(): return lax.ppermute(array, axis, pairs)  34.6 us
    ppermute x20, starting transfers between devices, cycle(): lax.ppermute(array, axis, [(i, (i + by) % count) for i in range(count)])  26.7 us
    ppermute x12, waiting for transfers between devices, shift(): return lax.ppermute(array, axis, pairs)  15.9 us
    gather x1, local copies, waits for them, and re-layouts, shards(): right_sides.at[leaf_order[0]]  3.66 us
  transfers between devices with their start and end apart: 32, of which 15 were waited for; matrix products, arithmetic and copies ran while one was open for 0% of the time, Pallas kernels for 14%

commit v1 on v0

v1 whole, which is shorter than its diff:
```python
import functools
import math

import jax
import jax.numpy as jnp
from jax import lax
from jax.experimental import pallas as pl
from jax.experimental.pallas import tpu as pltpu
from jax.sharding import PartitionSpec as P


RIDGE = 0.5
KERNEL_WIDTH = 8.0
REACH = 2
F32 = jnp.float32
BF16 = jnp.bfloat16
VMEM = pltpu.VMEM
ANY = pl.ANY


def shift(array, axis, by):
    count = lax.axis_size(axis)
    pairs = [(i, i + by) for i in range(count) if 0 <= i + by < count]
    return lax.ppermute(array, axis, pairs)


def cycle(array, axis, by):
    count = lax.axis_size(axis)
    return lax.ppermute(array, axis, [(i, (i + by) % count) for i in range(count)])


def tile_of(rows):
    return 512 if rows % 512 == 0 else rows


def over_tiles(rows, body):
    tile = tile_of(rows)

    def step(k, carry):
        body(pl.ds(pl.multiple_of(k * tile, tile), tile))
        return carry

    lax.fori_loop(0, rows // tile, step, 0)


def shape(dtype, *dims):
    return jax.ShapeDtypeStruct(dims, dtype)


SMEM_SPEC = pl.BlockSpec(memory_space=pltpu.SMEM)
ANY_SPEC = pl.BlockSpec(memory_space=ANY)


VMEM_SPEC = pl.BlockSpec(memory_space=VMEM)
HBM_SPEC = pl.BlockSpec(memory_space=pltpu.HBM)


def call(body, out, args, scratch=(), scalars=0, in_specs=None, out_specs=None, flops=0, bytes_=0, exps=0,
         aliases=None):
    many = isinstance(out, tuple)
    return pl.pallas_call(
        body,
        out_shape=out,
        in_specs=in_specs or [SMEM_SPEC] * scalars + [VMEM_SPEC] * (len(args) - scalars),
        out_specs=out_specs or ((VMEM_SPEC,) * len(out) if many else VMEM_SPEC),
        scratch_shapes=list(scratch),
        input_output_aliases=aliases or {},
        cost_estimate=pl.CostEstimate(flops=flops, bytes_accessed=bytes_, transcendentals=exps),
        compiler_params=pltpu.CompilerParams(vmem_limit_bytes=20 * 1024 * 1024),
    )(*args)


def dot(left, right):
    return jnp.dot(left, right, preferred_element_type=F32)


def dot_tn(left, right):
    return lax.dot_general(left, right, (((0,), (0,)), ((), ())), preferred_element_type=F32)


def dot_nt(left, right):
    return lax.dot_general(left, right, (((1,), (1,)), ((), ())), preferred_element_type=F32)


def pieces(value):
    first = value.astype(BF16).astype(F32)
    rest = value - first
    second = rest.astype(BF16).astype(F32)
    return first, second, rest - second


def augmented(block, left):
    rows, dims = block.shape
    wide = block.astype(F32)
    norm = jnp.sum(wide * wide, axis=1, keepdims=True)
    value = -norm / KERNEL_WIDTH
    if left:
        value = value + (dims / 16.0 - math.log(2.0 * rows))
        block = (wide * (2.0 / KERNEL_WIDTH)).astype(BF16)
    lane = lax.broadcasted_iota(jnp.int32, (rows, 128), 1)
    at, ones_at = (0, 3) if left else (3, 0)
    extra = jnp.where((lane >= ones_at) & (lane < ones_at + 3), 1.0, 0.0)
    for k, piece in enumerate(pieces(value)):
        extra = jnp.where(lane == at + k, piece, extra)
    return block, extra.astype(BF16)


def fill_augmented(target, block, left):
    dims = block.shape[1]
    main, extra = augmented(block, left)
    target[:, :dims] = main
    target[:, dims:] = extra


def kernel_tile(left_tile, right_all):
    return jnp.exp(dot_nt(left_tile, right_all)).astype(BF16)


def pick(choice, candidates, use):
    for k, candidate in enumerate(candidates):
        @pl.when(choice == k)
        def _():
            use(candidate)


def paired(members):
    return members == 2 * REACH


def slots(near_ref, members):
    member = lax.axis_index("member")
    one = near_ref[0, 0] - member
    two = near_ref[0, 1] - member
    if paired(members):
        toward = 1 - 2 * lax.rem(member, 2)
        outer = (one == toward) | (two == toward)
        inner = (one == -toward) | (two == -toward)
        return jnp.where(outer, 0, 1), jnp.where(outer & inner, 0, 1)

    def index(offset):
        return jnp.where(offset == -1, 0, jnp.where(offset == 1, 1, jnp.where(offset == -2, 2, 3)))

    return index(one), index(two)


def beside_pair(member, members):
    other = member - 1 if member % 2 == 0 else member + 1
    return other if 0 <= other < members else member


def exchange(block):
    members = lax.axis_size("member")
    if paired(members):
        beside = [beside_pair(i, members) for i in range(members)]
        across_of = [b + REACH if b + REACH < members else b - REACH for b in beside]
        inner = lax.ppermute(block, "member", list(enumerate(beside)))
        outer = lax.ppermute(block, "member", [(i, i + 1 - 2 * (i % 2)) for i in range(members)])
        across = lax.ppermute(inner, "member", list(enumerate(across_of)))
        return (outer, inner), (inner, across)
    before = shift(block, "member", 1)
    after = shift(block, "member", -1)
    behind = shift(before, "member", 1)
    ahead = shift(after, "member", -1)
    moved = (before, after, behind, ahead)
    return moved, moved


def factors(low_ref, high_ref, width):
    low = jnp.broadcast_to(low_ref[...], (1, width))
    high = jnp.broadcast_to(high_ref[...], (1, width))
    theta = (high + low) / 2.0
    delta = (high - low) / 2.0
    sigma = theta / delta
    rho_zero = 1.0 / sigma
    rho_one = 1.0 / (2.0 * sigma - rho_zero)
    return theta, rho_one * rho_zero, 2.0 * rho_one / delta


def prep(ordered, bases, transfer, low, high):
    rows, width = ordered.shape
    rank = bases.shape[1]
    half = width // 2

    def body(low_ref, high_ref, ordered_ref, bases_hbm, transfer_hbm, lead_ref, trail_ref, message_ref,
             bases_ref, transfer_ref, total, sems):
        copies = (pltpu.make_async_copy(bases_hbm, bases_ref, sems.at[0]),
                  pltpu.make_async_copy(transfer_hbm, transfer_ref, sems.at[1]))
        for copy in copies:
            copy.start()
        theta, _, _ = factors(low_ref, high_ref, width)
        total[...] = jnp.zeros_like(total)

        def scale(at):
            v = (ordered_ref[at, :] / theta).astype(BF16)
            lead_ref[at, :] = v[:, :half]
            trail_ref[at, :] = v[:, half:]

        over_tiles(rows, scale)
        for copy in copies:
            copy.wait()

        def project(at):
            own = bases_ref[at, :]
            total[:, :half] += dot_tn(own, lead_ref[at, :])
            total[:, half:] += dot_tn(own, trail_ref[at, :])

        over_tiles(rows, project)
        message_ref[:, :width] = total[...].astype(BF16)
        message_ref[:, width:] = transfer_ref[...]

    return call(
        body,
        (shape(BF16, rows, half), shape(BF16, rows, width - half), shape(BF16, rank, width + rank)),
        (low, high, ordered, pltpu.with_memory_space_constraint(bases, pltpu.HBM),
         pltpu.with_memory_space_constraint(transfer, pltpu.HBM)),
        in_specs=[VMEM_SPEC, VMEM_SPEC, VMEM_SPEC, HBM_SPEC, HBM_SPEC],
        scratch=[VMEM((rows, rank), BF16), VMEM((rank, rank), BF16), VMEM((rank, width), F32),
                 pltpu.SemaphoreType.DMA((2,))],
        flops=2 * rows * width * rank, bytes_=rows * width * 6 + rows * rank * 2,
    )


def join(lead_ref, trail_ref, target):
    half = trail_ref.shape[1]
    target[:, :half] = lead_ref[...]
    target[:, half:] = trail_ref[...]


def self_first(points, ordered, lead, trail, low, high):
    rows, width = ordered.shape
    dims = points.shape[1]

    def body(low_ref, high_ref, points_ref, ordered_ref, lead_ref, trail_ref, block_ref, rest_ref,
             left, right, v):
        theta, _, _ = factors(low_ref, high_ref, width)
        join(lead_ref, trail_ref, v)
        fill_augmented(left, points_ref[...], True)
        fill_augmented(right, points_ref[...], False)

        def tile(at):
            block = kernel_tile(left[at, :], right[...])
            block_ref[at, :] = block
            own = ordered_ref[at, :]
            rest_ref[at, :] = own - RIDGE * (own / theta) - dot(block, v[...])

        over_tiles(rows, tile)

    return call(
        body, (shape(BF16, rows, rows), shape(F32, rows, width)),
        (low, high, points, ordered, lead, trail),
        scratch=[VMEM((rows, dims + 128), BF16), VMEM((rows, dims + 128), BF16), VMEM((rows, width), BF16)],
        flops=2 * rows * rows * (width + dims), bytes_=rows * rows * 2 + rows * width * 10,
        exps=rows * rows,
    )


def near_block(which, near, points, candidates):
    rows, dims = points.shape
    members = lax.axis_size("member")
    count = len(candidates)

    def body(near_ref, points_ref, *rest):
        others, (block_ref, left, right) = rest[:count], rest[count:]
        fill_augmented(left, points_ref[...], True)
        pick(slots(near_ref, members)[which], others,
             lambda points_of: fill_augmented(right, points_of[...], False))

        def tile(at):
            block_ref[at, :] = kernel_tile(left[at, :], right[...])

        over_tiles(rows, tile)

    return call(
        body, shape(BF16, rows, rows), (near, points, *candidates), scalars=1,
        scratch=[VMEM((rows, dims + 128), BF16), VMEM((rows, dims + 128), BF16)],
        flops=2 * rows * rows * dims, bytes_=rows * rows * 2 + rows * dims * 4, exps=rows * rows,
    )


def subtract_near(near, block, rest, leads, trails):
    rows, width = rest.shape
    members = lax.axis_size("member")
    count = len(leads)

    def body(near_ref, block_ref, rest_ref, *refs):
        pairs = list(zip(refs[:count], refs[count : 2 * count]))
        out_ref, v = refs[2 * count :]
        pick(slots(near_ref, members)[0], pairs, lambda pair: join(*pair, v))

        def tile(at):
            out_ref[at, :] = rest_ref[at, :] - dot(block_ref[at, :], v[...])

        over_tiles(rows, tile)

    return call(
        body, shape(F32, rows, width), (near, block, rest, *leads, *trails), scalars=1,
        scratch=[VMEM((rows, width), BF16)],
        flops=2 * rows * rows * width, bytes_=rows * rows * 2 + rows * width * 10,
    )


def turn(column, near, block, rest, candidates, bases, coupled, ordered, low, high, joined=()):
    rows, width = rest.shape
    rank = bases.shape[1]
    half = width // 2
    members = lax.axis_size("member")
    count = len(candidates)
    kept = len(joined)
    columns = slice(column * half, (column + 1) * half)

    def body(near_ref, low_ref, high_ref, block_ref, rest_ref, bases_ref, coupled_ref, ordered_ref, *refs):
        others, joined_refs = refs[:count], refs[count : count + kept]
        first_ref, v_ref, coeff_ref, v, total = refs[count + kept :]

        def copy(ref):
            v[...] = ref[...]

        pick(slots(near_ref, members)[1], others, copy)
        theta, keep, push = factors(low_ref, high_ref, half)
        total[...] = jnp.zeros_like(total)

        def tile(at):
            own = bases_ref[at, :]
            first = rest_ref[at, columns] - dot(block_ref[at, :], v[...]) - dot(own, coupled_ref[:, columns])
            first_ref[at, :] = first
            moved = (keep * (ordered_ref[at, columns] / theta) + push * first).astype(BF16)
            v_ref[at, :] = moved
            total[...] += dot_tn(own, moved)

        over_tiles(rows, tile)
        for joined_ref in joined_refs:
            coeff_ref[:, :half] = joined_ref[...]
        coeff_ref[:, kept * half :] = total[...].astype(BF16)

    return call(
        body,
        (shape(F32, rows, half), shape(BF16, rows, half), shape(BF16, rank, half * (kept + 1))),
        (near, low, high, block, rest, bases, coupled, ordered, *candidates, *joined), scalars=1,
        scratch=[VMEM((rows, half), BF16), VMEM((rank, half), F32)],
        flops=2 * rows * rows * half, bytes_=rows * rows * 2 + rows * half * 16,
    )


def self_second(block, lead, trail, first_lead, first_trail, ordered, low, high):
    rows, width = ordered.shape
    half = width // 2

    def body(low_ref, high_ref, block_ref, lead_ref, trail_ref, first_lead_ref, first_trail_ref, ordered_ref,
             solution_ref, rest_ref, v):
        join(lead_ref, trail_ref, v)
        theta, keep, push = factors(low_ref, high_ref, half)

        def tile(at):
            product = dot(block_ref[at, :], v[...])
            for k, ref in enumerate((first_lead_ref, first_trail_ref)):
                columns = slice(k * half, (k + 1) * half)
                first = ref[at, :]
                step_zero = ordered_ref[at, columns] / theta
                step_one = keep * step_zero + push * first
                solution_ref[at, columns] = step_zero + step_one
                rest_ref[at, columns] = first - RIDGE * step_one - product[:, columns]

        over_tiles(rows, tile)

    return call(
        body, (shape(F32, rows, width), shape(F32, rows, width)),
        (low, high, block, lead, trail, first_lead, first_trail, ordered),
        scratch=[VMEM((rows, width), BF16)],
        flops=2 * rows * rows * width, bytes_=rows * rows * 2 + rows * width * 18,
    )


def final(column, near, block, rest, candidates, bases, coupled, whole_rows=()):
    rows, width = rest.shape
    half = width // 2
    members = lax.axis_size("member")
    count = len(candidates)
    tile_rows = tile_of(rows)
    columns = pl.ds(column * half, half)

    def body(near_ref, block_ref, rest_ref, bases_ref, coupled_ref, *refs):
        others, (out_ref, v, result, sems) = refs[:count], refs[-4:]

        def copy(ref):
            v[...] = ref[...]

        pick(slots(near_ref, members)[1], others, copy)
        copies = []
        for k in range(rows // tile_rows):
            at = pl.ds(k * tile_rows, tile_rows)
            result[at, :] = (rest_ref[at, columns] - dot(block_ref[at, :], v[...])
                             - dot(bases_ref[at, :], coupled_ref[:, columns]))
            copies.append(pltpu.make_async_copy(result.at[at, :], out_ref.at[at, columns], sems.at[k]))
            copies[-1].start()
        for started in copies:
            started.wait()

    args = (near, block, rest, bases, coupled, *candidates, *whole_rows)
    return call(
        body, shape(F32, rows, width), args,
        in_specs=[SMEM_SPEC] + [VMEM_SPEC] * (4 + count) + [ANY_SPEC] * len(whole_rows), out_specs=ANY_SPEC,
        scratch=[VMEM((rows, half), BF16), VMEM((rows, half), F32),
                 pltpu.SemaphoreType.DMA((rows // tile_rows,))],
        flops=2 * rows * rows * half, bytes_=rows * rows * 2 + rows * half * 10,
        aliases={5 + count: 0} if whole_rows else {},
    )


def pair_mate(member):
    return member + 1 - 2 * lax.rem(member, 2)


def gather_messages(message):
    members = lax.axis_size("member")
    rank = message.shape[0]
    if not paired(members):
        others = around(message, "member")
        sources = [functools.partial(lambda k, m: lax.rem(m + (members - k), members), k)
                   for k in range(1, members)]
        return [(other, 0) for other in others], sources
    mates = [(i, i + 1 - 2 * (i % 2)) for i in range(members)]
    mate = lax.ppermute(message, "member", mates)
    pair = pack((message, mate))
    crossed = lax.ppermute(
        pair, "member", [(i, beside_pair(i, members)) for i in range(members)])
    handed = lax.ppermute(crossed, "member", mates)
    return [(mate, 0), (crossed, 0), (crossed, rank), (handed, 0), (handed, rank)], None


def message_views(refs, spots, rank, sources, members):
    member = lax.axis_index("member")
    if sources is not None:
        return [(source(member), ref[row : row + rank, :]) for (ref, row), source in zip(
            zip(refs, [row for _, row in spots]), sources)]
    at_end = (member == 0) | (member == members - 1)
    near_end = jnp.where(member < members // 2, members // 2, members // 2 - 1)
    views = [(pair_mate(member), refs[0][...])]
    for k, number in enumerate((near_end, pair_mate(near_end))):
        rows = slice(k * rank, (k + 1) * rank)
        views.append((number, jnp.where(at_end, refs[3][rows, :], refs[1][rows, :])))
    return views


def merge(own, messages, first_own, first_messages):
    rank = own.shape[0]
    width = first_own.shape[1] - rank
    spots, sources = messages
    first_spots, _ = first_messages
    members = lax.axis_size("member")
    count = len(spots)

    def body(*refs):
        coeffs, firsts, out_ref = refs[:count], refs[count : 2 * count], refs[-1]
        own_ref, first_own_ref = refs[2 * count], refs[2 * count + 1]
        total = dot_tn(first_own_ref[:, width:], own_ref[:, :width])
        for (_, coeff), (_, carried) in zip(
            message_views(coeffs, spots, rank, sources, members),
            message_views(firsts, first_spots, rank, sources, members),
        ):
            total = total + dot_tn(carried[:, width:], coeff[:, :width])
        out_ref[...] = total.astype(BF16)

    args = (*[array for array, _ in spots], *[array for array, _ in first_spots], own, first_own)
    return call(
        body, shape(BF16, rank, width), args,
        flops=2 * rank * rank * width * (count + 1), bytes_=rank * width * 2 * (2 * count + 3),
    )


def pack(blocks):
    rank, width = blocks[0].shape

    def body(*refs):
        for k, ref in enumerate(refs[:-1]):
            refs[-1][k * rank : (k + 1) * rank, :] = ref[...]

    return call(
        body, shape(BF16, rank * len(blocks), width), blocks,
        bytes_=rank * width * 4 * len(blocks),
    )


def inner_of(groups):
    return 2 if groups % 2 == 0 else 1


def all_merged(merged):
    groups = lax.axis_size("group")
    inner = inner_of(groups)
    moved = []
    for k in range(1, groups // inner):
        moved.append(cycle(merged, "group", k * inner))
    if inner == 1:
        return moved, None
    packed = pack((merged, *moved))
    beside = lax.ppermute(packed, "group", [(g, g + 1 - 2 * (g % 2)) for g in range(groups)])
    return moved, beside


def couple(near, couplings, transfer, cross, messages, merged, beside):
    rank = transfer.shape[0]
    width = merged[0].shape[1]
    members = lax.axis_size("member")
    groups = lax.axis_size("group")
    inner = inner_of(groups)
    packed = () if beside is None else (beside,)

    spots, sources = messages
    count = len(spots)

    def body(near_ref, couplings_ref, transfer_ref, cross_ref, *refs):
        coeffs, others, out_ref = refs[:count], refs[count:-1], refs[-1]
        group = lax.axis_index("group")
        crossed = jnp.zeros((rank, width), F32)
        for k in range(1, groups // inner):
            source = lax.rem(group + (groups - k * inner), groups)
            crossed = crossed + dot(cross_ref[source], others[k - 1][...])
        if packed:
            side = group + 1 - 2 * lax.rem(group, 2)
            for k in range(groups // inner):
                source = lax.rem(side + (groups - k * inner), groups)
                crossed = crossed + dot(cross_ref[source], others[-1][k * rank : (k + 1) * rank, :])
        within = dot(transfer_ref[...], crossed.astype(BF16))
        for source, coeff in message_views(coeffs, spots, rank, sources, members):
            far = (source != near_ref[0, 0]) & (source != near_ref[0, 1])
            within = within + jnp.where(far, 1.0, 0.0) * dot(couplings_ref[source], coeff[:, :width])
        out_ref[...] = within.astype(BF16)

    args = (near, couplings, transfer, cross, *[array for array, _ in spots], *merged, *packed)
    return call(
        body, shape(BF16, rank, width), args, scalars=1,
        flops=2 * rank * rank * width * (members + groups), bytes_=rank * width * 2 * (members + groups) * 2,
    )


def around(array, axis):
    moved = []
    for k in range(1, lax.axis_size(axis)):
        moved.append(cycle(array, axis, k))
    return moved


def take_rows(rows, order):
    dims = lax.GatherDimensionNumbers(offset_dims=(1,), collapsed_slice_dims=(0,), start_index_map=(0,))
    return lax.gather(
        rows, order[:, None], dims, (1, rows.shape[1]), unique_indices=True,
        mode=lax.GatherScatterMode.PROMISE_IN_BOUNDS,
    )


def shards(
    points,
    right_sides,
    leaf_order,
    near_leaves,
    bases,
    couplings,
    transfers,
    cross_couplings,
    low_bound,
    high_bound,
):
    transfer = transfers[0]
    couplings = couplings[0]
    cross = cross_couplings[0]
    near = near_leaves
    low, high = low_bound.reshape(1, 1), high_bound.reshape(1, 1)

    points_a, points_b = exchange(points)
    ordered = take_rows(right_sides, leaf_order[0])
    lead, trail, message = prep(ordered, bases, transfer, low, high)
    lead_a, lead_b = exchange(lead)
    messages = gather_messages(message)
    trail_a, trail_b = exchange(trail)
    own_block, rest = self_first(points, ordered, lead, trail, low, high)
    block_a = near_block(0, near, points, points_a)
    block_b = near_block(1, near, points, points_b)
    merged = merge(message, messages, message, messages)
    merged, beside = all_merged(merged)
    rest = subtract_near(near, block_a, rest, lead_a, trail_a)
    coupled = couple(near, couplings, transfer, cross, messages, merged, beside)
    first_lead, lead, coeff = turn(
        0, near, block_b, rest, lead_b, bases, coupled, ordered, low, high)
    first_trail, trail, coeff = turn(
        1, near, block_b, rest, trail_b, bases, coupled, ordered, low, high, (coeff,))

    lead_a, lead_b = exchange(lead)
    coeffs = gather_messages(coeff)
    trail_a, trail_b = exchange(trail)
    solution_rows, rest = self_second(own_block, lead, trail, first_lead, first_trail, ordered, low, high)
    merged = merge(coeff, coeffs, message, messages)
    merged, beside = all_merged(merged)
    rest = subtract_near(near, block_a, rest, lead_a, trail_a)
    coupled = couple(near, couplings, transfer, cross, coeffs, merged, beside)
    residual = final(0, near, block_b, rest, lead_b, bases, coupled)
    residual = final(1, near, block_b, rest, trail_b, bases, coupled, (residual,))
    return solution_rows, residual


def solution(mesh):
    return jax.shard_map(
        shards,
        mesh=mesh,
        in_specs=(
            P(("group", "member"), None),
            P(("group", "member"), None),
            P(("group", "member"), None),
            P(("group", "member"), None),
            P(("group", "member"), None),
            P(("group", "member"), None, None, None),
            P(("group", "member"), None, None),
            P("group", None, None, None),
            P(),
            P(),
        ),
        out_specs=(P(("group", "member"), None), P(("group", "member"), None)),
        check_vma=False,
    )
```

time: 177 us -> 134 us (0.76)
  waiting for transfers between devices: 70.9 us -> 25.4 us
  starting transfers between devices: 61.3 us -> 66.2 us
    ppermute x20 -> x6, waiting for transfers between devices: 55 us -> 9.95 us  [cycle(): lax.ppermute(array, axis, [(i, (i + by) % count) for i in range(count)])]
    ppermute x12 -> x23, starting transfers between devices: 34.6 us -> 57 us  [the longest x2 21.6 us: gather_messages(): handed = lax.ppermute(crossed, 'member', mates)]
    ppermute x20 -> x6, starting transfers between devices: 26.7 us -> 9.13 us  [cycle(): lax.ppermute(array, axis, [(i, (i + by) % count) for i in range(count)])]
    pallas_call x13 -> x19, Pallas kernels: 35.6 us -> 35.1 us  [call(): pl.pallas_call(body, out_shape=out, in_specs=in_specs or [SMEM_SPEC] * sc...]
    ppermute x12 -> x23, waiting for transfers between devices: 15.9 us -> 15.4 us  [the longest x5 8.69 us: exchange(): across = lax.ppermute(inner, 'member', list(enumerate(across_of)))]
  transfers between devices with their start and end apart: 32 -> 29, of which waited for: 15 -> 12; matrix products, arithmetic and copies ran while one was open for 0% -> 0% of each run, Pallas kernels for 14% -> 20%
where the time goes in v1:
time: 134 us
  starting transfers between devices  66.2 us (49%)
  Pallas kernels  35.1 us (26%)
  waiting for transfers between devices  25.4 us (19%)
  local copies, waits for them, and re-layouts  3.71 us (3%)
  between operations  2.46 us (2%)
    pallas_call x19, Pallas kernels, call(): pl.pallas_call(body, out_shape=out, in_specs=in_specs or [SMEM_SPEC] * sc...  35.1 us
    ppermute x2, starting transfers between devices, gather_messages(): handed = lax.ppermute(crossed, 'member', mates)  21.6 us
    ppermute x5, starting transfers between devices, exchange(): lax.ppermute(block, 'member', [(i, i + 1 - 2 * (i % 2)) for i in range(me...  13.7 us
    ppermute x6, waiting for transfers between devices, cycle(): lax.ppermute(array, axis, [(i, (i + by) % count) for i in range(count)])  9.95 us
    ppermute x5, starting transfers between devices, exchange(): across = lax.ppermute(inner, 'member', list(enumerate(across_of)))  9.94 us
    ppermute x6, starting transfers between devices, cycle(): lax.ppermute(array, axis, [(i, (i + by) % count) for i in range(count)])  9.13 us
    ppermute x5, waiting for transfers between devices, exchange(): across = lax.ppermute(inner, 'member', list(enumerate(across_of)))  8.69 us
    ppermute x2, starting transfers between devices, gather_messages(): mate = lax.ppermute(message, 'member', mates)  6.94 us
  transfers between devices with their start and end apart: 29, of which 12 were waited for; matrix products, arithmetic and copies ran while one was open for 0% of the time, Pallas kernels for 20%

profile of v1, /device:TPU:0, one launch (start us, length us, event | category | flops | bytes accessed | tf_op | source)
XLA Modules:
  0.0 133.6 jit_solution(5419110750772916013)
XLA Ops:
  0.6 0.8 reduce
  2.8 3.7 %gather_fusion = f32[1536,256]{1,0:T(8,128)S(1)} fusion(f32[1536,256]{1,0:T(8,128)S(1)} %copy-done, s32[2048]{0:T(1024)S(1)} %pad_clamp_fusion), kind=kCustom, calls=%fused_computation | custom fusion | bytes 3151872 | tf_op jit(solution)/shard_map/gather | solution.py:545
  6.5 1.9 %shard_map.113 = (bf16[1536,128]{1,0:T(8,128)(2,1)S(1)}, bf16[1536,128]{1,0:T(8,128)(2,1)S(1)}, bf16[128,384]{1,0:T(8,128)(2,1)S(1)}) custom-call(f32[1,1]{1,0:T(1,128)} %bitcast.5.low_ref, f32[1,1]{1,0:T(1,128)} %bitcast.10.high_ref, f32[1536,256]{1,0:T(8,128)S(1)} %gather_fusion, bf16[1536,128]{1,0:T(8,128)(2,1)} %bases_ref.7, bf16[128,128]{1,0:T(8,128)(2,1)} %bitcast.19), custom_call_target="tpu_custom_call" | custom-call | flops 100663296 | bytes 2752512 | tf_op jit(solution)/shard_map/pallas_call | solution.py:61
  8.4 3.1 %collective-permute-start.7 = (bf16[128,384]{1,0:T(8,128)(2,1)S(1)}, bf16[128,384]{1,0:T(8,128)(2,1)S(1)}, u32[]{:S(2)}, u32[]{:S(2)}) collective-permute-start(bf16[128,384]{1,0:T(8,128)(2,1)S(1)} %get-tuple-element.19.refs_0_.refs_10_.refs_11_), channel_id=1, source_target_pairs={{0,1},{1,0},{2,3},{3,2},{4,5},{5,4},{6,7},{7,6},{8,9},{9,8},{10,11... | collective-permute-start | bytes 294920 | tf_op jit(solution)/shard_map/ppermute | solution.py:422
  11.5 2.8 %collective-permute-done.7.refs_1_.refs_0_.refs_5_ = bf16[128,384]{1,0:T(8,128)(2,1)S(1)} collective-permute-done((bf16[128,384]{1,0:T(8,128)(2,1)S(1)}, bf16[128,384]{1,0:T(8,128)(2,1)S(1)}, u32[]{:S(2)}, u32[]{:S(2)}) %collective-permute-start.7) | collective-permute-done | bytes 98336 | tf_op jit(solution)/shard_map/ppermute | solution.py:422
  14.3 0.7 collective-permute-start.8
  15.0 0.7 collective-permute-start.4
  15.7 9.2 %collective-permute-start.9 = (bf16[256,384]{1,0:T(8,128)(2,1)S(1)}, bf16[256,384]{1,0:T(8,128)(2,1)S(1)}, u32[]{:S(2)}, u32[]{:S(2)}) collective-permute-start(bf16[256,384]{1,0:T(8,128)(2,1)S(1)} %collective-permute-done.8.refs_1_.refs_2_.refs_6_.refs_7_), channel_id=1, source_target_pairs={{0,1},{1,0},{2,3},{3,2},{4,5},{5,4},{6,7},{7,6},{8,9},{9,8},{10,11... | collective-permute-start | bytes 589832 | tf_op jit(solution)/shard_map/ppermute | solution.py:426
  24.9 0.7 collective-permute-start
  25.6 0.7 collective-permute-start.6
  26.3 5.0 %collective-permute-start.3 = (bf16[1536,128]{1,0:T(8,128)(2,1)S(1)}, bf16[1536,128]{1,0:T(8,128)(2,1)S(1)}, u32[]{:S(2)}, u32[]{:S(2)}) collective-permute-start(bf16[1536,128]{1,0:T(8,128)(2,1)S(1)} %get-tuple-element.15.lead_ref), channel_id=1, source_target_pairs={{0,1},{1,0},{2,3},{3,2},{4,5},{5,4},{6,7},{7,6},{8,9},{9,8},{10,11... | collective-permute-start | bytes 1179656 | tf_op jit(solution)/shard_map/ppermute | solution.py:157
  32.2 1.5 %collective-permute-start.10 = (bf16[128,256]{1,0:T(8,128)(2,1)S(1)}, bf16[128,256]{1,0:T(8,128)(2,1)S(1)}, u32[]{:S(2)}, u32[]{:S(2)}) collective-permute-start(bf16[128,256]{1,0:T(8,128)(2,1)S(1)} %shard_map.119.refs_0_), channel_id=1, source_target_pairs={{0,8},{4,12},{8,16},{12,20},{16,24},{20,28},{24,0},{28,4},{1,9},{5... | collective-permute-start | bytes 196616 | tf_op jit(solution)/shard_map/ppermute | solution.py:29
  33.8 1.5 %collective-permute-start.11 = (bf16[128,256]{1,0:T(8,128)(2,1)S(1)}, bf16[128,256]{1,0:T(8,128)(2,1)S(1)}, u32[]{:S(2)}, u32[]{:S(2)}) collective-permute-start(bf16[128,256]{1,0:T(8,128)(2,1)S(1)} %shard_map.119.refs_0_), channel_id=1, source_target_pairs={{0,16},{4,20},{8,24},{12,28},{16,0},{20,4},{24,8},{28,12},{1,17},{... | collective-permute-start | bytes 196616 | tf_op jit(solution)/shard_map/ppermute | solution.py:29
  35.3 2.1 %collective-permute-done.10.refs_1_.refs_5_ = bf16[128,256]{1,0:T(8,128)(2,1)S(1)} collective-permute-done((bf16[128,256]{1,0:T(8,128)(2,1)S(1)}, bf16[128,256]{1,0:T(8,128)(2,1)S(1)}, u32[]{:S(2)}, u32[]{:S(2)}) %collective-permute-start.10) | collective-permute-done | bytes 65568 | tf_op jit(solution)/shard_map/ppermute | solution.py:29
  37.5 6.0 %collective-permute-start.5 = (bf16[1536,128]{1,0:T(8,128)(2,1)S(1)}, bf16[1536,128]{1,0:T(8,128)(2,1)S(1)}, u32[]{:S(2)}, u32[]{:S(2)}) collective-permute-start(bf16[1536,128]{1,0:T(8,128)(2,1)S(1)} %get-tuple-element.16.trail_ref), channel_id=1, source_target_pairs={{0,1},{1,0},{2,3},{3,2},{4,5},{5,4},{6,7},{7,6},{8,9},{9,8},{10,11... | collective-permute-start | bytes 1179656 | tf_op jit(solution)/shard_map/ppermute | solution.py:157
  43.5 1.4 %collective-permute-start.12 = (bf16[128,256]{1,0:T(8,128)(2,1)S(1)}, bf16[128,256]{1,0:T(8,128)(2,1)S(1)}, u32[]{:S(2)}, u32[]{:S(2)}) collective-permute-start(bf16[128,256]{1,0:T(8,128)(2,1)S(1)} %shard_map.119.refs_0_), channel_id=1, source_target_pairs={{0,24},{4,28},{8,0},{12,4},{16,8},{20,12},{24,16},{28,20},{1,25},{... | collective-permute-start | bytes 196616 | tf_op jit(solution)/shard_map/ppermute | solution.py:29
  44.9 2.8 %collective-permute-done.12.refs_3_.refs_7_ = bf16[128,256]{1,0:T(8,128)(2,1)S(1)} collective-permute-done((bf16[128,256]{1,0:T(8,128)(2,1)S(1)}, bf16[128,256]{1,0:T(8,128)(2,1)S(1)}, u32[]{:S(2)}, u32[]{:S(2)}) %collective-permute-start.12) | collective-permute-done | bytes 65568 | tf_op jit(solution)/shard_map/ppermute | solution.py:29
  47.7 4.6 %collective-permute-start.1 = (bf16[1536,128]{1,0:T(8,128)(2,1)S(1)}, bf16[1536,128]{1,0:T(8,128)(2,1)S(1)}, u32[]{:S(2)}, u32[]{:S(2)}) collective-permute-start(bf16[1536,128]{1,0:T(8,128)(2,1)S(1)} %collective-permute-done.rest_0_.rest_1_), channel_id=1, source_target_pairs={{0,2},{1,0},{2,3},{3,1},{4,6},{5,4},{6,7},{7,5},{8,10},{9,8},{10,1... | collective-permute-start | bytes 1179656 | tf_op jit(solution)/shard_map/ppermute | solution.py:158
  52.4 1.2 collective-permute-start.15
  53.6 4.2 %shard_map.114 = (bf16[1536,1536]{1,0:T(8,128)(2,1)S(1)}, f32[1536,256]{1,0:T(8,128)S(1)}) custom-call(f32[1,1]{1,0:T(1,128)} %bitcast.6.low_ref, f32[1,1]{1,0:T(1,128)} %bitcast.11.high_ref, bf16[1536,128]{1,0:T(8,128)(2,1)S(1)} %copy-done.2, f32[1536,256]{1,0:T(8,128)S(1)} %gather_fusion, bf16[1536,128]{1,0:T(8,128)(2,1)S(1)} %get-tuple-element.15.lead_ref, ...), custom_call_target="tpu_custom_call" | custom-call | flops 1811939328 | bytes 8650752 | tf_op jit(solution)/shard_map/pallas_call | solution.py:61
  57.8 3.2 %shard_map.116.block_ref = bf16[1536,1536]{1,0:T(8,128)(2,1)S(1)} custom-call(s32[1,2]{1,0:T(1,128)S(1)} %copy-done.6, bf16[1536,128]{1,0:T(8,128)(2,1)S(1)} %copy-done.2, bf16[1536,128]{1,0:T(8,128)(2,1)S(1)} %collective-permute-done.2.rest_0_, bf16[1536,128]{1,0:T(8,128)(2,1)S(1)} %collective-permute-done.rest_0_.rest_1_), custom_call_target="tpu_custom_call" | custom-call | flops 603979776 | bytes 5505024 | tf_op jit(solution)/shard_map/pallas_call | solution.py:61
  61.1 2.4 %shard_map.117.rest_ref = f32[1536,256]{1,0:T(8,128)S(1)} custom-call(s32[1,2]{1,0:T(1,128)S(1)} %copy-done.6, bf16[1536,1536]{1,0:T(8,128)(2,1)S(1)} %shard_map.116.block_ref, f32[1536,256]{1,0:T(8,128)S(1)} %get-tuple-element.18.rest_ref, bf16[1536,128]{1,0:T(8,128)(2,1)S(1)} %collective-permute-done.3.refs_0_, ...), custom_call_target="tpu_custom_call" | custom-call | flops 1207959552 | bytes 8650752 | tf_op jit(solution)/shard_map/pallas_call | solution.py:61
  63.5 2.8 %collective-permute-done.1.rest_1_ = bf16[1536,128]{1,0:T(8,128)(2,1)S(1)} collective-permute-done((bf16[1536,128]{1,0:T(8,128)(2,1)S(1)}, bf16[1536,128]{1,0:T(8,128)(2,1)S(1)}, u32[]{:S(2)}, u32[]{:S(2)}) %collective-permute-start.1) | collective-permute-done | bytes 393248 | tf_op jit(solution)/shard_map/ppermute | solution.py:158
  66.3 3.2 %shard_map.115.block_ref = bf16[1536,1536]{1,0:T(8,128)(2,1)S(1)} custom-call(s32[1,2]{1,0:T(1,128)S(1)} %copy-done.6, bf16[1536,128]{1,0:T(8,128)(2,1)S(1)} %copy-done.2, bf16[1536,128]{1,0:T(8,128)(2,1)S(1)} %collective-permute-done.rest_0_.rest_1_, bf16[1536,128]{1,0:T(8,128)(2,1)S(1)} %collective-permute-done.1.rest_1_), custom_call_target="tpu_custom_call" | custom-call | flops 603979776 | bytes 5505024 | tf_op jit(solution)/shard_map/pallas_call | solution.py:61
  69.5 1.1 shard_map.121.coupled_ref
  70.6 4.1 %collective-permute-done.14.refs_1_ = bf16[1536,128]{1,0:T(8,128)(2,1)S(1)} collective-permute-done((bf16[1536,128]{1,0:T(8,128)(2,1)S(1)}, bf16[1536,128]{1,0:T(8,128)(2,1)S(1)}, u32[]{:S(2)}, u32[]{:S(2)}) %collective-permute-start.14) | collective-permute-done | bytes 393248 | tf_op jit(solution)/shard_map/ppermute | solution.py:158
  74.7 3.1 %shard_map.122 = (f32[1536,128]{1,0:T(8,128)S(1)}, bf16[1536,128]{1,0:T(8,128)(2,1)S(1)}, bf16[128,128]{1,0:T(8,128)(2,1)S(1)}) custom-call(s32[1,2]{1,0:T(1,128)S(1)} %copy-done.6, f32[1,1]{1,0:T(1,128)} %bitcast.7.low_ref, f32[1,1]{1,0:T(1,128)} %bitcast.12.high_ref, bf16[1536,1536]{1,0:T(8,128)(2,1)S(1)} %shard_map.115.block_ref, ...), custom_call_target="tpu_custom_call" | custom-call | flops 603979776 | bytes 7864320 | tf_op jit(solution)/shard_map/pallas_call | solution.py:61
  77.8 1.3 collective-permute-done.15.refs_1_
  79.1 3.1 %shard_map.123 = (f32[1536,128]{1,0:T(8,128)S(1)}, bf16[1536,128]{1,0:T(8,128)(2,1)S(1)}, bf16[128,256]{1,0:T(8,128)(2,1)S(1)}) custom-call(s32[1,2]{1,0:T(1,128)S(1)} %copy-done.6, f32[1,1]{1,0:T(1,128)} %bitcast.8.low_ref, f32[1,1]{1,0:T(1,128)} %bitcast.13.high_ref, bf16[1536,1536]{1,0:T(8,128)(2,1)S(1)} %shard_map.115.block_ref, ...), custom_call_target="tpu_custom_call" | custom-call | flops 603979776 | bytes 7864320 | tf_op jit(solution)/shard_map/pallas_call | solution.py:61
  82.3 3.8 %collective-permute-start.20 = (bf16[128,256]{1,0:T(8,128)(2,1)S(1)}, bf16[128,256]{1,0:T(8,128)(2,1)S(1)}, u32[]{:S(2)}, u32[]{:S(2)}) collective-permute-start(bf16[128,256]{1,0:T(8,128)(2,1)S(1)} %get-tuple-element.27.refs_0_.refs_10_), channel_id=1, source_target_pairs={{0,1},{1,0},{2,3},{3,2},{4,5},{5,4},{6,7},{7,6},{8,9},{9,8},{10,11... | collective-permute-start | bytes 196616 | tf_op jit(solution)/shard_map/ppermute | solution.py:422
  86.1 0.7 collective-permute-start.17
  86.8 1.6 %collective-permute-done.20.refs_1_.refs_0_ = bf16[128,256]{1,0:T(8,128)(2,1)S(1)} collective-permute-done((bf16[128,256]{1,0:T(8,128)(2,1)S(1)}, bf16[128,256]{1,0:T(8,128)(2,1)S(1)}, u32[]{:S(2)}, u32[]{:S(2)}) %collective-permute-start.20) | collective-permute-done | bytes 65568 | tf_op jit(solution)/shard_map/ppermute | solution.py:422
  88.3 0.7 collective-permute-start.21
  89.0 0.7 collective-permute-start.19
  89.7 12.4 %collective-permute-start.22 = (bf16[256,256]{1,0:T(8,128)(2,1)S(1)}, bf16[256,256]{1,0:T(8,128)(2,1)S(1)}, u32[]{:S(2)}, u32[]{:S(2)}) collective-permute-start(bf16[256,256]{1,0:T(8,128)(2,1)S(1)} %collective-permute-done.21.refs_1_.refs_2_), channel_id=1, source_target_pairs={{0,1},{1,0},{2,3},{3,2},{4,5},{5,4},{6,7},{7,6},{8,9},{9,8},{10,11... | collective-permute-start | bytes 393224 | tf_op jit(solution)/shard_map/ppermute | solution.py:426
  102.2 2.0 %collective-permute-start.16 = (bf16[1536,128]{1,0:T(8,128)(2,1)S(1)}, bf16[1536,128]{1,0:T(8,128)(2,1)S(1)}, u32[]{:S(2)}, u32[]{:S(2)}) collective-permute-start(bf16[1536,128]{1,0:T(8,128)(2,1)S(1)} %get-tuple-element.20.lead_ref), channel_id=1, source_target_pairs={{0,1},{1,0},{2,3},{3,2},{4,5},{5,4},{6,7},{7,6},{8,9},{9,8},{10,11... | collective-permute-start | bytes 1179656 | tf_op jit(solution)/shard_map/ppermute | solution.py:157
  104.2 2.3 %collective-permute-done.22.refs_3_.refs_4_ = bf16[256,256]{1,0:T(8,128)(2,1)S(1)} collective-permute-done((bf16[256,256]{1,0:T(8,128)(2,1)S(1)}, bf16[256,256]{1,0:T(8,128)(2,1)S(1)}, u32[]{:S(2)}, u32[]{:S(2)}) %collective-permute-start.22) | collective-permute-done | bytes 131104 | tf_op jit(solution)/shard_map/ppermute | solution.py:426
  106.8 1.5 %collective-permute-start.23 = (bf16[128,256]{1,0:T(8,128)(2,1)S(1)}, bf16[128,256]{1,0:T(8,128)(2,1)S(1)}, u32[]{:S(2)}, u32[]{:S(2)}) collective-permute-start(bf16[128,256]{1,0:T(8,128)(2,1)S(1)} %shard_map.127.refs_0_), channel_id=1, source_target_pairs={{0,8},{4,12},{8,16},{12,20},{16,24},{20,28},{24,0},{28,4},{1,9},{5... | collective-permute-start | bytes 196616 | tf_op jit(solution)/shard_map/ppermute | solution.py:29
  108.3 3.7 %collective-permute-done.23.refs_1_.refs_5_ = bf16[128,256]{1,0:T(8,128)(2,1)S(1)} collective-permute-done((bf16[128,256]{1,0:T(8,128)(2,1)S(1)}, bf16[128,256]{1,0:T(8,128)(2,1)S(1)}, u32[]{:S(2)}, u32[]{:S(2)}) %collective-permute-start.23) | collective-permute-done | bytes 65568 | tf_op jit(solution)/shard_map/ppermute | solution.py:29
  112.0 1.5 %collective-permute-start.24 = (bf16[128,256]{1,0:T(8,128)(2,1)S(1)}, bf16[128,256]{1,0:T(8,128)(2,1)S(1)}, u32[]{:S(2)}, u32[]{:S(2)}) collective-permute-start(bf16[128,256]{1,0:T(8,128)(2,1)S(1)} %shard_map.127.refs_0_), channel_id=1, source_target_pairs={{0,16},{4,20},{8,24},{12,28},{16,0},{20,4},{24,8},{28,12},{1,17},{... | collective-permute-start | bytes 196616 | tf_op jit(solution)/shard_map/ppermute | solution.py:29
  113.5 2.1 %collective-permute-start.28 = (bf16[1536,128]{1,0:T(8,128)(2,1)S(1)}, bf16[1536,128]{1,0:T(8,128)(2,1)S(1)}, u32[]{:S(2)}, u32[]{:S(2)}) collective-permute-start(bf16[1536,128]{1,0:T(8,128)(2,1)S(1)} %collective-permute-done.17.refs_1_.refs_0_), channel_id=1, source_target_pairs={{0,2},{1,0},{2,3},{3,1},{4,6},{5,4},{6,7},{7,5},{8,10},{9,8},{10,1... | collective-permute-start | bytes 1179656 | tf_op jit(solution)/shard_map/ppermute | solution.py:158
  116.2 1.6 %collective-permute-start.25 = (bf16[128,256]{1,0:T(8,128)(2,1)S(1)}, bf16[128,256]{1,0:T(8,128)(2,1)S(1)}, u32[]{:S(2)}, u32[]{:S(2)}) collective-permute-start(bf16[128,256]{1,0:T(8,128)(2,1)S(1)} %shard_map.127.refs_0_), channel_id=1, source_target_pairs={{0,24},{4,28},{8,0},{12,4},{16,8},{20,12},{24,16},{28,20},{1,25},{... | collective-permute-start | bytes 196616 | tf_op jit(solution)/shard_map/ppermute | solution.py:29
  117.8 2.1 %collective-permute-start.27 = (bf16[1536,128]{1,0:T(8,128)(2,1)S(1)}, bf16[1536,128]{1,0:T(8,128)(2,1)S(1)}, u32[]{:S(2)}, u32[]{:S(2)}) collective-permute-start(bf16[1536,128]{1,0:T(8,128)(2,1)S(1)} %collective-permute-done.19.refs_3_.refs_0_), channel_id=1, source_target_pairs={{0,2},{1,0},{2,3},{3,1},{4,6},{5,4},{6,7},{7,5},{8,10},{9,8},{10,1... | collective-permute-start | bytes 1179656 | tf_op jit(solution)/shard_map/ppermute | solution.py:158
  120.6 3.0 %shard_map.124 = (f32[1536,256]{1,0:T(8,128)}, f32[1536,256]{1,0:T(8,128)S(1)}) custom-call(f32[1,1]{1,0:T(1,128)} %bitcast.9.low_ref, f32[1,1]{1,0:T(1,128)} %bitcast.14.high_ref, bf16[1536,1536]{1,0:T(8,128)(2,1)S(1)} %get-tuple-element.17.block_ref, bf16[1536,128]{1,0:T(8,128)(2,1)S(1)} %get-tuple-element.20.lead_ref, ...), custom_call_target="tpu_custom_call" | custom-call | flops 1207959552 | bytes 11796480 | tf_op jit(solution)/shard_map/pallas_call | solution.py:61
  123.6 2.4 %shard_map.125.rest_ref = f32[1536,256]{1,0:T(8,128)S(1)} custom-call(s32[1,2]{1,0:T(1,128)S(1)} %copy-done.6, bf16[1536,1536]{1,0:T(8,128)(2,1)S(1)} %shard_map.116.block_ref, f32[1536,256]{1,0:T(8,128)S(1)} %get-tuple-element.26.rest_ref, bf16[1536,128]{1,0:T(8,128)(2,1)S(1)} %collective-permute-done.16.refs_0_, ...), custom_call_target="tpu_custom_call" | custom-call | flops 1207959552 | bytes 8650752 | tf_op jit(solution)/shard_map/pallas_call | solution.py:61
  126.1 1.1 shard_map.129.coupled_ref
  127.2 2.8 %shard_map.130.refs_2_ = f32[1536,256]{1,0:T(8,128)} custom-call(s32[1,2]{1,0:T(1,128)S(1)} %copy-done.6, bf16[1536,1536]{1,0:T(8,128)(2,1)S(1)} %shard_map.115.block_ref, f32[1536,256]{1,0:T(8,128)S(1)} %shard_map.125.rest_ref, bf16[1536,128]{1,0:T(8,128)(2,1)S(1)} %copy-done.1, bf16[128,256]{1,0:T(8,128)(2,1)S(1)} %shard_map.129.coupled_ref, ...), custom_call_target="tpu_custom_call" | custom-call | flops 603979776 | bytes 6684672 | tf_op jit(solution)/shard_map/pallas_call | solution.py:61
  130.6 2.8 %shard_map.131 = f32[1536,256]{1,0:T(8,128)} custom-call(s32[1,2]{1,0:T(1,128)S(1)} %copy-done.6, bf16[1536,1536]{1,0:T(8,128)(2,1)S(1)} %shard_map.115.block_ref, f32[1536,256]{1,0:T(8,128)S(1)} %shard_map.125.rest_ref, bf16[1536,128]{1,0:T(8,128)(2,1)S(1)} %copy-done.1, ...), custom_call_target="tpu_custom_call", output_to_operand_aliasing={{}: (7, {})} | custom-call | flops 603979776 | bytes 6684672 | tf_op jit(solution)/shard_map/pallas_call | solution.py:61
  (46 shorter events, 3.4 us)
Async XLA Ops:
  0.6 2.2 %copy-start = (f32[1536,256]{1,0:T(8,128)S(1)}, f32[1536,256]{1,0:T(8,128)}, u32[]{:S(2)}) copy-start(f32[1536,256]{1,0:T(8,128)} %param.11) | copy-start | bytes 4718596
  6.5 18.4 %copy-start.2 = (bf16[1536,128]{1,0:T(8,128)(2,1)S(1)}, bf16[1536,128]{1,0:T(8,128)(2,1)}, u32[]{:S(2)}) copy-start(bf16[1536,128]{1,0:T(8,128)(2,1)} %points_ref.5) | copy-start | bytes 1179652
  8.4 5.9 %collective-permute-start.7 = (bf16[128,384]{1,0:T(8,128)(2,1)S(1)}, bf16[128,384]{1,0:T(8,128)(2,1)S(1)}, u32[]{:S(2)}, u32[]{:S(2)}) collective-permute-start(bf16[128,384]{1,0:T(8,128)(2,1)S(1)} %get-tuple-element.19.refs_0_.refs_10_.refs_11_), channel_id=1, source_target_pairs={{0,1},{1,0},{2,3},{3,2},{4,5},{5,4},{6,7},{7,6},{8,9},{9,8},{10,11... | collective-permute-start | bytes 294920 | tf_op jit(solution)/shard_map/ppermute | solution.py:422
  14.3 1.4 %collective-permute-start.8 = (bf16[256,384]{1,0:T(8,128)(2,1)S(1)}, bf16[256,384]{1,0:T(8,128)(2,1)S(1)}, u32[]{:S(2)}, u32[]{:S(2)}) collective-permute-start(bf16[256,384]{1,0:T(8,128)(2,1)S(1)} %shard_map.118), channel_id=1, source_target_pairs={{0,0},{1,2},{2,1},{3,3},{4,4},{5,6},{6,5},{7,7},{8,8},{9,10},{10,9... | collective-permute-start | bytes 589832 | tf_op jit(solution)/shard_map/ppermute | solution.py:424
  15.0 17.2 %collective-permute-start.4 = (bf16[1536,128]{1,0:T(8,128)(2,1)S(1)}, bf16[1536,128]{1,0:T(8,128)(2,1)S(1)}, u32[]{:S(2)}, u32[]{:S(2)}) collective-permute-start(bf16[1536,128]{1,0:T(8,128)(2,1)S(1)} %get-tuple-element.15.lead_ref), channel_id=1, source_target_pairs={{0,0},{1,2},{2,1},{3,3},{4,4},{5,6},{6,5},{7,7},{8,8},{9,10},{10,9... | collective-permute-start | bytes 1179656 | tf_op jit(solution)/shard_map/ppermute | solution.py:156
  15.7 15.6 %collective-permute-start.9 = (bf16[256,384]{1,0:T(8,128)(2,1)S(1)}, bf16[256,384]{1,0:T(8,128)(2,1)S(1)}, u32[]{:S(2)}, u32[]{:S(2)}) collective-permute-start(bf16[256,384]{1,0:T(8,128)(2,1)S(1)} %collective-permute-done.8.refs_1_.refs_2_.refs_6_.refs_7_), channel_id=1, source_target_pairs={{0,1},{1,0},{2,3},{3,2},{4,5},{5,4},{6,7},{7,6},{8,9},{9,8},{10,11... | collective-permute-start | bytes 589832 | tf_op jit(solution)/shard_map/ppermute | solution.py:426
  24.9 8.9 %collective-permute-start = (bf16[1536,128]{1,0:T(8,128)(2,1)S(1)}, bf16[1536,128]{1,0:T(8,128)(2,1)S(1)}, u32[]{:S(2)}, u32[]{:S(2)}) collective-permute-start(bf16[1536,128]{1,0:T(8,128)(2,1)S(1)} %copy-done.2), channel_id=1, source_target_pairs={{0,0},{1,2},{2,1},{3,3},{4,4},{5,6},{6,5},{7,7},{8,8},{9,10},{10,9... | collective-permute-start | bytes 1179656 | tf_op jit(solution)/shard_map/ppermute | solution.py:156
  25.6 26.7 %collective-permute-start.6 = (bf16[1536,128]{1,0:T(8,128)(2,1)S(1)}, bf16[1536,128]{1,0:T(8,128)(2,1)S(1)}, u32[]{:S(2)}, u32[]{:S(2)}) collective-permute-start(bf16[1536,128]{1,0:T(8,128)(2,1)S(1)} %get-tuple-element.16.trail_ref), channel_id=1, source_target_pairs={{0,0},{1,2},{2,1},{3,3},{4,4},{5,6},{6,5},{7,7},{8,8},{9,10},{10,9... | collective-permute-start | bytes 1179656 | tf_op jit(solution)/shard_map/ppermute | solution.py:156
  26.3 26.1 %collective-permute-start.3 = (bf16[1536,128]{1,0:T(8,128)(2,1)S(1)}, bf16[1536,128]{1,0:T(8,128)(2,1)S(1)}, u32[]{:S(2)}, u32[]{:S(2)}) collective-permute-start(bf16[1536,128]{1,0:T(8,128)(2,1)S(1)} %get-tuple-element.15.lead_ref), channel_id=1, source_target_pairs={{0,1},{1,0},{2,3},{3,2},{4,5},{5,4},{6,7},{7,6},{8,9},{9,8},{10,11... | collective-permute-start | bytes 1179656 | tf_op jit(solution)/shard_map/ppermute | solution.py:157
  31.3 22.3 %collective-permute-start.2 = (bf16[1536,128]{1,0:T(8,128)(2,1)S(1)}, bf16[1536,128]{1,0:T(8,128)(2,1)S(1)}, u32[]{:S(2)}, u32[]{:S(2)}) collective-permute-start(bf16[1536,128]{1,0:T(8,128)(2,1)S(1)} %copy-done.2), channel_id=1, source_target_pairs={{0,1},{1,0},{2,3},{3,2},{4,5},{5,4},{6,7},{7,6},{8,9},{9,8},{10,11... | collective-permute-start | bytes 1179656 | tf_op jit(solution)/shard_map/ppermute | solution.py:157
  32.2 5.2 %collective-permute-start.10 = (bf16[128,256]{1,0:T(8,128)(2,1)S(1)}, bf16[128,256]{1,0:T(8,128)(2,1)S(1)}, u32[]{:S(2)}, u32[]{:S(2)}) collective-permute-start(bf16[128,256]{1,0:T(8,128)(2,1)S(1)} %shard_map.119.refs_0_), channel_id=1, source_target_pairs={{0,8},{4,12},{8,16},{12,20},{16,24},{20,28},{24,0},{28,4},{1,9},{5... | collective-permute-start | bytes 196616 | tf_op jit(solution)/shard_map/ppermute | solution.py:29
  33.8 9.7 %collective-permute-start.11 = (bf16[128,256]{1,0:T(8,128)(2,1)S(1)}, bf16[128,256]{1,0:T(8,128)(2,1)S(1)}, u32[]{:S(2)}, u32[]{:S(2)}) collective-permute-start(bf16[128,256]{1,0:T(8,128)(2,1)S(1)} %shard_map.119.refs_0_), channel_id=1, source_target_pairs={{0,16},{4,20},{8,24},{12,28},{16,0},{20,4},{24,8},{28,12},{1,17},{... | collective-permute-start | bytes 196616 | tf_op jit(solution)/shard_map/ppermute | solution.py:29
  37.5 23.6 %collective-permute-start.5 = (bf16[1536,128]{1,0:T(8,128)(2,1)S(1)}, bf16[1536,128]{1,0:T(8,128)(2,1)S(1)}, u32[]{:S(2)}, u32[]{:S(2)}) collective-permute-start(bf16[1536,128]{1,0:T(8,128)(2,1)S(1)} %get-tuple-element.16.trail_ref), channel_id=1, source_target_pairs={{0,1},{1,0},{2,3},{3,2},{4,5},{5,4},{6,7},{7,6},{8,9},{9,8},{10,11... | collective-permute-start | bytes 1179656 | tf_op jit(solution)/shard_map/ppermute | solution.py:157
  43.5 4.3 %collective-permute-start.12 = (bf16[128,256]{1,0:T(8,128)(2,1)S(1)}, bf16[128,256]{1,0:T(8,128)(2,1)S(1)}, u32[]{:S(2)}, u32[]{:S(2)}) collective-permute-start(bf16[128,256]{1,0:T(8,128)(2,1)S(1)} %shard_map.119.refs_0_), channel_id=1, source_target_pairs={{0,24},{4,28},{8,0},{12,4},{16,8},{20,12},{24,16},{28,20},{1,25},{... | collective-permute-start | bytes 196616 | tf_op jit(solution)/shard_map/ppermute | solution.py:29
  47.7 18.5 %collective-permute-start.1 = (bf16[1536,128]{1,0:T(8,128)(2,1)S(1)}, bf16[1536,128]{1,0:T(8,128)(2,1)S(1)}, u32[]{:S(2)}, u32[]{:S(2)}) collective-permute-start(bf16[1536,128]{1,0:T(8,128)(2,1)S(1)} %collective-permute-done.rest_0_.rest_1_), channel_id=1, source_target_pairs={{0,2},{1,0},{2,3},{3,1},{4,6},{5,4},{6,7},{7,5},{8,10},{9,8},{10,1... | collective-permute-start | bytes 1179656 | tf_op jit(solution)/shard_map/ppermute | solution.py:158
  52.3 22.4 %collective-permute-start.14 = (bf16[1536,128]{1,0:T(8,128)(2,1)S(1)}, bf16[1536,128]{1,0:T(8,128)(2,1)S(1)}, u32[]{:S(2)}, u32[]{:S(2)}) collective-permute-start(bf16[1536,128]{1,0:T(8,128)(2,1)S(1)} %collective-permute-done.4.refs_1_.refs_0_), channel_id=1, source_target_pairs={{0,2},{1,0},{2,3},{3,1},{4,6},{5,4},{6,7},{7,5},{8,10},{9,8},{10,1... | collective-permute-start | bytes 1179656 | tf_op jit(solution)/shard_map/ppermute | solution.py:158
  52.4 26.7 %collective-permute-start.15 = (bf16[1536,128]{1,0:T(8,128)(2,1)S(1)}, bf16[1536,128]{1,0:T(8,128)(2,1)S(1)}, u32[]{:S(2)}, u32[]{:S(2)}) collective-permute-start(bf16[1536,128]{1,0:T(8,128)(2,1)S(1)} %collective-permute-done.6.refs_3_.refs_0_), channel_id=1, source_target_pairs={{0,2},{1,0},{2,3},{3,1},{4,6},{5,4},{6,7},{7,5},{8,10},{9,8},{10,1... | collective-permute-start | bytes 1179656 | tf_op jit(solution)/shard_map/ppermute | solution.py:158
  53.6 15.9 %collective-permute-start.13 = (bf16[512,256]{1,0:T(8,128)(2,1)S(1)}, bf16[512,256]{1,0:T(8,128)(2,1)S(1)}, u32[]{:S(2)}, u32[]{:S(2)}) collective-permute-start(bf16[512,256]{1,0:T(8,128)(2,1)S(1)} %shard_map.120), channel_id=1, source_target_pairs={{0,4},{4,0},{8,12},{12,8},{16,20},{20,16},{24,28},{28,24},{1,5},{5... | collective-permute-start | bytes 786440 | tf_op jit(solution)/shard_map/ppermute | solution.py:496
  53.6 4.2 %copy-start.6 = (s32[1,2]{1,0:T(1,128)S(1)}, s32[1,2]{1,0:T(1,128)}, u32[]{:S(2)}) copy-start(s32[1,2]{1,0:T(1,128)} %near_ref.19) | copy-start | bytes 28
  63.5 6.0 %copy-start.3 = (bf16[1,8,128,128]{3,2,1,0:T(8,128)(2,1)S(1)}, bf16[1,8,128,128]{3,2,1,0:T(8,128)(2,1)}, u32[]{:S(2)}) copy-start(bf16[1,8,128,128]{3,2,1,0:T(8,128)(2,1)} %param.17) | copy-start | bytes 786436
  63.5 6.0 %copy-start.4 = (bf16[1,4,128,128]{3,2,1,0:T(8,128)(2,1)S(1)}, bf16[1,4,128,128]{3,2,1,0:T(8,128)(2,1)}, u32[]{:S(2)}) copy-start(bf16[1,4,128,128]{3,2,1,0:T(8,128)(2,1)} %param.15) | copy-start | bytes 393220
  63.5 6.0 %copy-start.5 = (bf16[1,128,128]{2,1,0:T(8,128)(2,1)S(1)}, bf16[1,128,128]{2,1,0:T(8,128)(2,1)}, u32[]{:S(2)}) copy-start(bf16[1,128,128]{2,1,0:T(8,128)(2,1)} %param.16) | copy-start | bytes 98308
  69.5 5.2 %copy-start.1 = (bf16[1536,128]{1,0:T(8,128)(2,1)S(1)}, bf16[1536,128]{1,0:T(8,128)(2,1)}, u32[]{:S(2)}) copy-start(bf16[1536,128]{1,0:T(8,128)(2,1)} %bases_ref.7) | copy-start | bytes 1179652
  82.3 6.1 %collective-permute-start.20 = (bf16[128,256]{1,0:T(8,128)(2,1)S(1)}, bf16[128,256]{1,0:T(8,128)(2,1)S(1)}, u32[]{:S(2)}, u32[]{:S(2)}) collective-permute-start(bf16[128,256]{1,0:T(8,128)(2,1)S(1)} %get-tuple-element.27.refs_0_.refs_10_), channel_id=1, source_target_pairs={{0,1},{1,0},{2,3},{3,2},{4,5},{5,4},{6,7},{7,6},{8,9},{9,8},{10,11... | collective-permute-start | bytes 196616 | tf_op jit(solution)/shard_map/ppermute | solution.py:422
  86.1 27.4 %collective-permute-start.17 = (bf16[1536,128]{1,0:T(8,128)(2,1)S(1)}, bf16[1536,128]{1,0:T(8,128)(2,1)S(1)}, u32[]{:S(2)}, u32[]{:S(2)}) collective-permute-start(bf16[1536,128]{1,0:T(8,128)(2,1)S(1)} %get-tuple-element.20.lead_ref), channel_id=1, source_target_pairs={{0,0},{1,2},{2,1},{3,3},{4,4},{5,6},{6,5},{7,7},{8,8},{9,10},{10,9... | collective-permute-start | bytes 1179656 | tf_op jit(solution)/shard_map/ppermute | solution.py:156
  88.3 1.4 %collective-permute-start.21 = (bf16[256,256]{1,0:T(8,128)(2,1)S(1)}, bf16[256,256]{1,0:T(8,128)(2,1)S(1)}, u32[]{:S(2)}, u32[]{:S(2)}) collective-permute-start(bf16[256,256]{1,0:T(8,128)(2,1)S(1)} %shard_map.126), channel_id=1, source_target_pairs={{0,0},{1,2},{2,1},{3,3},{4,4},{5,6},{6,5},{7,7},{8,8},{9,10},{10,9... | collective-permute-start | bytes 393224 | tf_op jit(solution)/shard_map/ppermute | solution.py:424
  89.0 28.8 %collective-permute-start.19 = (bf16[1536,128]{1,0:T(8,128)(2,1)S(1)}, bf16[1536,128]{1,0:T(8,128)(2,1)S(1)}, u32[]{:S(2)}, u32[]{:S(2)}) collective-permute-start(bf16[1536,128]{1,0:T(8,128)(2,1)S(1)} %get-tuple-element.22.trail_ref), channel_id=1, source_target_pairs={{0,0},{1,2},{2,1},{3,3},{4,4},{5,6},{6,5},{7,7},{8,8},{9,10},{10,9... | collective-permute-start | bytes 1179656 | tf_op jit(solution)/shard_map/ppermute | solution.py:156
  89.7 16.8 %collective-permute-start.22 = (bf16[256,256]{1,0:T(8,128)(2,1)S(1)}, bf16[256,256]{1,0:T(8,128)(2,1)S(1)}, u32[]{:S(2)}, u32[]{:S(2)}) collective-permute-start(bf16[256,256]{1,0:T(8,128)(2,1)S(1)} %collective-permute-done.21.refs_1_.refs_2_), channel_id=1, source_target_pairs={{0,1},{1,0},{2,3},{3,2},{4,5},{5,4},{6,7},{7,6},{8,9},{9,8},{10,11... | collective-permute-start | bytes 393224 | tf_op jit(solution)/shard_map/ppermute | solution.py:426
  102.1 21.5 %collective-permute-start.18 = (bf16[1536,128]{1,0:T(8,128)(2,1)S(1)}, bf16[1536,128]{1,0:T(8,128)(2,1)S(1)}, u32[]{:S(2)}, u32[]{:S(2)}) collective-permute-start(bf16[1536,128]{1,0:T(8,128)(2,1)S(1)} %get-tuple-element.22.trail_ref), channel_id=1, source_target_pairs={{0,1},{1,0},{2,3},{3,2},{4,5},{5,4},{6,7},{7,6},{8,9},{9,8},{10,11... | collective-permute-start | bytes 1179656 | tf_op jit(solution)/shard_map/ppermute | solution.py:157
  102.2 21.5 %collective-permute-start.16 = (bf16[1536,128]{1,0:T(8,128)(2,1)S(1)}, bf16[1536,128]{1,0:T(8,128)(2,1)S(1)}, u32[]{:S(2)}, u32[]{:S(2)}) collective-permute-start(bf16[1536,128]{1,0:T(8,128)(2,1)S(1)} %get-tuple-element.20.lead_ref), channel_id=1, source_target_pairs={{0,1},{1,0},{2,3},{3,2},{4,5},{5,4},{6,7},{7,6},{8,9},{9,8},{10,11... | collective-permute-start | bytes 1179656 | tf_op jit(solution)/shard_map/ppermute | solution.py:157
  106.8 5.2 %collective-permute-start.23 = (bf16[128,256]{1,0:T(8,128)(2,1)S(1)}, bf16[128,256]{1,0:T(8,128)(2,1)S(1)}, u32[]{:S(2)}, u32[]{:S(2)}) collective-permute-start(bf16[128,256]{1,0:T(8,128)(2,1)S(1)} %shard_map.127.refs_0_), channel_id=1, source_target_pairs={{0,8},{4,12},{8,16},{12,20},{16,24},{20,28},{24,0},{28,4},{1,9},{5... | collective-permute-start | bytes 196616 | tf_op jit(solution)/shard_map/ppermute | solution.py:29
  112.0 4.3 %collective-permute-start.24 = (bf16[128,256]{1,0:T(8,128)(2,1)S(1)}, bf16[128,256]{1,0:T(8,128)(2,1)S(1)}, u32[]{:S(2)}, u32[]{:S(2)}) collective-permute-start(bf16[128,256]{1,0:T(8,128)(2,1)S(1)} %shard_map.127.refs_0_), channel_id=1, source_target_pairs={{0,16},{4,20},{8,24},{12,28},{16,0},{20,4},{24,8},{28,12},{1,17},{... | collective-permute-start | bytes 196616 | tf_op jit(solution)/shard_map/ppermute | solution.py:29
  113.5 13.7 %collective-permute-start.28 = (bf16[1536,128]{1,0:T(8,128)(2,1)S(1)}, bf16[1536,128]{1,0:T(8,128)(2,1)S(1)}, u32[]{:S(2)}, u32[]{:S(2)}) collective-permute-start(bf16[1536,128]{1,0:T(8,128)(2,1)S(1)} %collective-permute-done.17.refs_1_.refs_0_), channel_id=1, source_target_pairs={{0,2},{1,0},{2,3},{3,1},{4,6},{5,4},{6,7},{7,5},{8,10},{9,8},{10,1... | collective-permute-start | bytes 1179656 | tf_op jit(solution)/shard_map/ppermute | solution.py:158
  116.2 4.3 %collective-permute-start.25 = (bf16[128,256]{1,0:T(8,128)(2,1)S(1)}, bf16[128,256]{1,0:T(8,128)(2,1)S(1)}, u32[]{:S(2)}, u32[]{:S(2)}) collective-permute-start(bf16[128,256]{1,0:T(8,128)(2,1)S(1)} %shard_map.127.refs_0_), channel_id=1, source_target_pairs={{0,24},{4,28},{8,0},{12,4},{16,8},{20,12},{24,16},{28,20},{1,25},{... | collective-permute-start | bytes 196616 | tf_op jit(solution)/shard_map/ppermute | solution.py:29
  117.8 12.8 %collective-permute-start.27 = (bf16[1536,128]{1,0:T(8,128)(2,1)S(1)}, bf16[1536,128]{1,0:T(8,128)(2,1)S(1)}, u32[]{:S(2)}, u32[]{:S(2)}) collective-permute-start(bf16[1536,128]{1,0:T(8,128)(2,1)S(1)} %collective-permute-done.19.refs_3_.refs_0_), channel_id=1, source_target_pairs={{0,2},{1,0},{2,3},{3,1},{4,6},{5,4},{6,7},{7,5},{8,10},{9,8},{10,1... | collective-permute-start | bytes 1179656 | tf_op jit(solution)/shard_map/ppermute | solution.py:158
  120.5 5.5 %collective-permute-start.26 = (bf16[512,256]{1,0:T(8,128)(2,1)S(1)}, bf16[512,256]{1,0:T(8,128)(2,1)S(1)}, u32[]{:S(2)}, u32[]{:S(2)}) collective-permute-start(bf16[512,256]{1,0:T(8,128)(2,1)S(1)} %shard_map.128), channel_id=1, source_target_pairs={{0,4},{4,0},{8,12},{12,8},{16,20},{20,16},{24,28},{28,24},{1,5},{5... | collective-permute-start | bytes 786440 | tf_op jit(solution)/shard_map/ppermute | solution.py:496

commit v2 on v1

--- a/solution.py
+++ b/solution.py
@@ -16,12 +16,6 @@
 BF16 = jnp.bfloat16
 VMEM = pltpu.VMEM
 ANY = pl.ANY
-
-
-def shift(array, axis, by):
-    count = lax.axis_size(axis)
-    pairs = [(i, i + by) for i in range(count) if 0 <= i + by < count]
-    return lax.ppermute(array, axis, pairs)
 
 
 def cycle(array, axis, by):
@@ -127,6 +121,10 @@
     return members == 2 * REACH
 
 
+def at_end(member, members):
+    return (member == 0) | (member == members - 1)
+
+
 def slots(near_ref, members):
     member = lax.axis_index("member")
     one = near_ref[0, 0] - member
@@ -143,26 +141,47 @@
     return index(one), index(two)
 
 
+def with_slot_b(near_ref, members, block_ref, candidates, use):
+    choice = slots(near_ref, members)[1]
+    for k, ref in enumerate(candidates):
+        @pl.when(choice == k)
+        def _():
+            use(lambda at: dot(block_ref[at, :], ref[...]))
+
+
 def beside_pair(member, members):
     other = member - 1 if member % 2 == 0 else member + 1
     return other if 0 <= other < members else member
 
 
+def permute(block, pairs):
+    return lax.ppermute(block, "member", pairs)
+
+
+def mates(members):
+    return [(i, i + 1 - 2 * (i % 2)) for i in range(members)]
+
+
+def hop(block):
+    members = lax.axis_size("member")
+    inner = permute(block, [(i, beside_pair(i, members)) for i in range(members)])
+    return inner, permute(block, mates(members))
+
+
+def across(inner):
+    members = lax.axis_size("member")
+    beside = [beside_pair(i, members) for i in range(members)]
+    return permute(
+        inner, [(i, b + REACH if b + REACH < members else b - REACH) for i, b in enumerate(beside)])
+
+
 def exchange(block):
     members = lax.axis_size("member")
-    if paired(members):
-        beside = [beside_pair(i, members) for i in range(members)]
-        across_of = [b + REACH if b + REACH < members else b - REACH for b in beside]
-        inner = lax.ppermute(block, "member", list(enumerate(beside)))
-        outer = lax.ppermute(block, "member", [(i, i + 1 - 2 * (i % 2)) for i in range(members)])
-        across = lax.ppermute(inner, "member", list(enumerate(across_of)))
-        return (outer, inner), (inner, across)
-    before = shift(block, "member", 1)
-    after = shift(block, "member", -1)
-    behind = shift(before, "member", 1)
-    ahead = shift(after, "member", -1)
-    moved = (before, after, behind, ahead)
-    return moved, moved
+    up = [(i, i + 1) for i in range(members - 1)]
+    down = [(i + 1, i) for i in range(members - 1)]
+    before = permute(block, up)
+    after = permute(block, down)
+    return before, after, permute(before, up), permute(after, down)
 
 
 def factors(low_ref, high_ref, width):
@@ -176,47 +195,40 @@
     return theta, rho_one * rho_zero, 2.0 * rho_one / delta
 
 
-def prep(ordered, bases, transfer, low, high):
+def start_rows(ordered, low, high):
     rows, width = ordered.shape
-    rank = bases.shape[1]
     half = width // 2
 
-    def body(low_ref, high_ref, ordered_ref, bases_hbm, transfer_hbm, lead_ref, trail_ref, message_ref,
-             bases_ref, transfer_ref, total, sems):
-        copies = (pltpu.make_async_copy(bases_hbm, bases_ref, sems.at[0]),
-                  pltpu.make_async_copy(transfer_hbm, transfer_ref, sems.at[1]))
-        for copy in copies:
-            copy.start()
+    def body(low_ref, high_ref, ordered_ref, lead_ref, trail_ref):
         theta, _, _ = factors(low_ref, high_ref, width)
-        total[...] = jnp.zeros_like(total)
-
-        def scale(at):
+
+        def tile(at):
             v = (ordered_ref[at, :] / theta).astype(BF16)
             lead_ref[at, :] = v[:, :half]
             trail_ref[at, :] = v[:, half:]
 
-        over_tiles(rows, scale)
-        for copy in copies:
-            copy.wait()
-
-        def project(at):
-            own = bases_ref[at, :]
-            total[:, :half] += dot_tn(own, lead_ref[at, :])
-            total[:, half:] += dot_tn(own, trail_ref[at, :])
-
-        over_tiles(rows, project)
-        message_ref[:, :width] = total[...].astype(BF16)
+        over_tiles(rows, tile)
+
+    return call(
+        body, (shape(BF16, rows, half), shape(BF16, rows, width - half)), (low, high, ordered),
+        flops=rows * width, bytes_=rows * width * 6,
+    )
+
+
+def start_message(lead, trail, bases, transfer):
+    rows, half = lead.shape
+    rank = bases.shape[1]
+    width = half + trail.shape[1]
+
+    def body(lead_ref, trail_ref, bases_ref, transfer_ref, message_ref, v):
+        join(lead_ref, trail_ref, v)
+        message_ref[:, :width] = dot_tn(bases_ref[...], v[...]).astype(BF16)
         message_ref[:, width:] = transfer_ref[...]
 
     return call(
-        body,
-        (shape(BF16, rows, half), shape(BF16, rows, width - half), shape(BF16, rank, width + rank)),
-        (low, high, ordered, pltpu.with_memory_space_constraint(bases, pltpu.HBM),
-         pltpu.with_memory_space_constraint(transfer, pltpu.HBM)),
-        in_specs=[VMEM_SPEC, VMEM_SPEC, VMEM_SPEC, HBM_SPEC, HBM_SPEC],
-        scratch=[VMEM((rows, rank), BF16), VMEM((rank, rank), BF16), VMEM((rank, width), F32),
-                 pltpu.SemaphoreType.DMA((2,))],
-        flops=2 * rows * width * rank, bytes_=rows * width * 6 + rows * rank * 2,
+        body, shape(BF16, rank, width + rank), (lead, trail, bases, transfer),
+        scratch=[VMEM((rows, width), BF16)],
+        flops=2 * rows * width * rank, bytes_=rows * width * 2 + rows * rank * 2,
     )
 
 
@@ -310,24 +322,22 @@
 
     def body(near_ref, low_ref, high_ref, block_ref, rest_ref, bases_ref, coupled_ref, ordered_ref, *refs):
         others, joined_refs = refs[:count], refs[count : count + kept]
-        first_ref, v_ref, coeff_ref, v, total = refs[count + kept :]
-
-        def copy(ref):
-            v[...] = ref[...]
-
-        pick(slots(near_ref, members)[1], others, copy)
+        first_ref, v_ref, coeff_ref, total = refs[count + kept :]
         theta, keep, push = factors(low_ref, high_ref, half)
         total[...] = jnp.zeros_like(total)
 
-        def tile(at):
-            own = bases_ref[at, :]
-            first = rest_ref[at, columns] - dot(block_ref[at, :], v[...]) - dot(own, coupled_ref[:, columns])
-            first_ref[at, :] = first
-            moved = (keep * (ordered_ref[at, columns] / theta) + push * first).astype(BF16)
-            v_ref[at, :] = moved
-            total[...] += dot_tn(own, moved)
-
-        over_tiles(rows, tile)
+        def use(slot_b):
+            def tile(at):
+                own = bases_ref[at, :]
+                first = rest_ref[at, columns] - slot_b(at) - dot(own, coupled_ref[:, columns])
+                first_ref[at, :] = first
+                moved = (keep * (ordered_ref[at, columns] / theta) + push * first).astype(BF16)
+                v_ref[at, :] = moved
+                total[...] += dot_tn(own, moved)
+
+            over_tiles(rows, tile)
+
+        with_slot_b(near_ref, members, block_ref, others, use)
         for joined_ref in joined_refs:
             coeff_ref[:, :half] = joined_ref[...]
         coeff_ref[:, kept * half :] = total[...].astype(BF16)
@@ -336,7 +346,7 @@
         body,
         (shape(F32, rows, half), shape(BF16, rows, half), shape(BF16, rank, half * (kept + 1))),
         (near, low, high, block, rest, bases, coupled, ordered, *candidates, *joined), scalars=1,
-        scratch=[VMEM((rows, half), BF16), VMEM((rank, half), F32)],
+        scratch=[VMEM((rank, half), F32)],
         flops=2 * rows * rows * half, bytes_=rows * rows * 2 + rows * half * 16,
     )
 
@@ -370,7 +380,7 @@
     )
 
 
-def final(column, near, block, rest, candidates, bases, coupled, whole_rows=()):
+def final(column, near, block, rest, candidates, bases, coupled, written=()):
     rows, width = rest.shape
     half = width // 2
     members = lax.axis_size("member")
@@ -379,30 +389,27 @@
     columns = pl.ds(column * half, half)
 
     def body(near_ref, block_ref, rest_ref, bases_ref, coupled_ref, *refs):
-        others, (out_ref, v, result, sems) = refs[:count], refs[-4:]
-
-        def copy(ref):
-            v[...] = ref[...]
-
-        pick(slots(near_ref, members)[1], others, copy)
-        copies = []
-        for k in range(rows // tile_rows):
-            at = pl.ds(k * tile_rows, tile_rows)
-            result[at, :] = (rest_ref[at, columns] - dot(block_ref[at, :], v[...])
-                             - dot(bases_ref[at, :], coupled_ref[:, columns]))
-            copies.append(pltpu.make_async_copy(result.at[at, :], out_ref.at[at, columns], sems.at[k]))
-            copies[-1].start()
-        for started in copies:
-            started.wait()
-
-    args = (near, block, rest, bases, coupled, *candidates, *whole_rows)
-    return call(
-        body, shape(F32, rows, width), args,
-        in_specs=[SMEM_SPEC] + [VMEM_SPEC] * (4 + count) + [ANY_SPEC] * len(whole_rows), out_specs=ANY_SPEC,
-        scratch=[VMEM((rows, half), BF16), VMEM((rows, half), F32),
-                 pltpu.SemaphoreType.DMA((rows // tile_rows,))],
+        others, (out_ref, result, sems) = refs[:count], refs[-3:]
+
+        def use(slot_b):
+            copies = []
+            for k in range(rows // tile_rows):
+                at = pl.ds(k * tile_rows, tile_rows)
+                result[at, :] = (
+                    rest_ref[at, columns] - slot_b(at) - dot(bases_ref[at, :], coupled_ref[:, columns]))
+                copies.append(pltpu.make_async_copy(result.at[at, :], out_ref.at[at, columns], sems.at[k]))
+                copies[-1].start()
+            for started in copies:
+                started.wait()
+
+        with_slot_b(near_ref, members, block_ref, others, use)
+
+    return call(
+        body, shape(F32, rows, width), (near, block, rest, bases, coupled, *candidates, *written),
+        in_specs=[SMEM_SPEC] + [VMEM_SPEC] * (4 + count) + [ANY_SPEC] * len(written), out_specs=ANY_SPEC,
+        scratch=[VMEM((rows, half), F32), pltpu.SemaphoreType.DMA((rows // tile_rows,))],
         flops=2 * rows * rows * half, bytes_=rows * rows * 2 + rows * half * 10,
-        aliases={5 + count: 0} if whole_rows else {},
+        aliases={5 + count: 0} if written else {},
     )
 
 
@@ -418,12 +425,10 @@
         sources = [functools.partial(lambda k, m: lax.rem(m + (members - k), members), k)
                    for k in range(1, members)]
         return [(other, 0) for other in others], sources
-    mates = [(i, i + 1 - 2 * (i % 2)) for i in range(members)]
-    mate = lax.ppermute(message, "member", mates)
+    mate = permute(message, mates(members))
     pair = pack((message, mate))
-    crossed = lax.ppermute(
-        pair, "member", [(i, beside_pair(i, members)) for i in range(members)])
-    handed = lax.ppermute(crossed, "member", mates)
+    crossed = permute(pair, [(i, beside_pair(i, members)) for i in range(members)])
+    handed = permute(crossed, mates(members))
     return [(mate, 0), (crossed, 0), (crossed, rank), (handed, 0), (handed, rank)], None
 
 
@@ -432,12 +437,12 @@
     if sources is not None:
         return [(source(member), ref[row : row + rank, :]) for (ref, row), source in zip(
             zip(refs, [row for _, row in spots]), sources)]
-    at_end = (member == 0) | (member == members - 1)
+    end = at_end(member, members)
     near_end = jnp.where(member < members // 2, members // 2, members // 2 - 1)
     views = [(pair_mate(member), refs[0][...])]
     for k, number in enumerate((near_end, pair_mate(near_end))):
         rows = slice(k * rank, (k + 1) * rank)
-        views.append((number, jnp.where(at_end, refs[3][rows, :], refs[1][rows, :])))
+        views.append((number, jnp.where(end, refs[3][rows, :], refs[1][rows, :])))
     return views
 
 
@@ -566,27 +571,36 @@
     near = near_leaves
     low, high = low_bound.reshape(1, 1), high_bound.reshape(1, 1)
 
-    points_a, points_b = exchange(points)
-    ordered = take_rows(right_sides, leaf_order[0])
-    lead, trail, message = prep(ordered, bases, transfer, low, high)
-    lead_a, lead_b = exchange(lead)
-    messages = gather_messages(message)
-    trail_a, trail_b = exchange(trail)
-    own_block, rest = self_first(points, ordered, lead, trail, low, high)
+    line = paired(lax.axis_size("member"))
+
+    def moved(block):
+        if not line:
+            blocks = exchange(block)
+            return blocks, blocks
+        inner, outer = hop(block)
+        return (outer, inner), (inner, across(inner))
+
+    points_a, points_b = moved(points)
     block_a = near_block(0, near, points, points_a)
     block_b = near_block(1, near, points, points_b)
+    ordered = take_rows(right_sides, leaf_order[0])
+    lead, trail = start_rows(ordered, low, high)
+    message = start_message(lead, trail, bases, transfer)
+    messages = gather_messages(message)
+    lead_a, lead_b = moved(lead)
+    trail_a, trail_b = moved(trail)
+    own_block, rest = self_first(points, ordered, lead, trail, low, high)
     merged = merge(message, messages, message, messages)
     merged, beside = all_merged(merged)
     rest = subtract_near(near, block_a, rest, lead_a, trail_a)
     coupled = couple(near, couplings, transfer, cross, messages, merged, beside)
-    first_lead, lead, coeff = turn(
-        0, near, block_b, rest, lead_b, bases, coupled, ordered, low, high)
+    first_lead, lead, coeff = turn(0, near, block_b, rest, lead_b, bases, coupled, ordered, low, high)
     first_trail, trail, coeff = turn(
         1, near, block_b, rest, trail_b, bases, coupled, ordered, low, high, (coeff,))
 
-    lead_a, lead_b = exchange(lead)
     coeffs = gather_messages(coeff)
-    trail_a, trail_b = exchange(trail)
+    lead_a, lead_b = moved(lead)
+    trail_a, trail_b = moved(trail)
     solution_rows, rest = self_second(own_block, lead, trail, first_lead, first_trail, ordered, low, high)
     merged = merge(coeff, coeffs, message, messages)
     merged, beside = all_merged(merged)

time: 134 us -> 133 us (level)
  Pallas kernels: 35.1 us -> 33.6 us
    pallas_call x19 -> x20, Pallas kernels: 35.1 us -> 33.6 us  [call(): pl.pallas_call(body, out_shape=out, in_specs=in_specs or [SMEM_SPEC] * sc...]
where the time goes in v2:
time: 133 us
  starting transfers between devices  66.1 us (50%)
  Pallas kernels  33.6 us (25%)
  waiting for transfers between devices  25.6 us (19%)
  local copies, waits for them, and re-layouts  4.47 us (3%)
  between operations  2.47 us (2%)
    ppermute x21, starting transfers between devices, permute(): return lax.ppermute(block, 'member', pairs)  57 us
    pallas_call x20, Pallas kernels, call(): pl.pallas_call(body, out_shape=out, in_specs=in_specs or [SMEM_SPEC] * sc...  33.6 us
    ppermute x21, waiting for transfers between devices, permute(): return lax.ppermute(block, 'member', pairs)  15.6 us
    ppermute x6, waiting for transfers between devices, cycle(): lax.ppermute(array, axis, [(i, (i + by) % count) for i in range(count)])  10 us
    ppermute x6, starting transfers between devices, cycle(): lax.ppermute(array, axis, [(i, (i + by) % count) for i in range(count)])  9.07 us
    gather x1, local copies, waits for them, and re-layouts, take_rows(): lax.gather(rows, order[:, None], dims, (1, rows.shape[1]), unique_indices...  3.66 us
  transfers between devices with their start and end apart: 29, of which 12 were waited for; matrix products, arithmetic and copies ran while one was open for 0% of the time, Pallas kernels for 20%

profile of v2, /device:TPU:0, one launch (start us, length us, event | category | flops | bytes accessed | tf_op | source)
XLA Modules:
  0.0 133.1 jit_solution(8436145558386287204)
XLA Ops:
  0.6 0.8 reduce
  2.8 3.7 %gather_fusion = f32[1536,256]{1,0:T(8,128)S(1)} fusion(f32[1536,256]{1,0:T(8,128)S(1)} %copy-done, s32[2048]{0:T(1024)S(1)} %pad_clamp_fusion), kind=kCustom, calls=%fused_computation | custom fusion | bytes 3151872 | tf_op jit(solution)/shard_map/gather | solution.py:550
  6.7 0.8 copy-done.1
  7.9 3.1 %collective-permute-start.7 = (bf16[128,384]{1,0:T(8,128)(2,1)S(1)}, bf16[128,384]{1,0:T(8,128)(2,1)S(1)}, u32[]{:S(2)}, u32[]{:S(2)}) collective-permute-start(bf16[128,384]{1,0:T(8,128)(2,1)S(1)} %shard_map.118.refs_0_.refs_10_.refs_11_), channel_id=1, source_target_pairs={{0,1},{1,0},{2,3},{3,2},{4,5},{5,4},{6,7},{7,6},{8,9},{9,8},{10,11... | collective-permute-start | bytes 294920 | tf_op jit(solution)/shard_map/ppermute | solution.py:158
  11.0 2.8 %collective-permute-done.7.refs_1_.refs_0_.refs_5_ = bf16[128,384]{1,0:T(8,128)(2,1)S(1)} collective-permute-done((bf16[128,384]{1,0:T(8,128)(2,1)S(1)}, bf16[128,384]{1,0:T(8,128)(2,1)S(1)}, u32[]{:S(2)}, u32[]{:S(2)}) %collective-permute-start.7) | collective-permute-done | bytes 98336 | tf_op jit(solution)/shard_map/ppermute | solution.py:158
  13.8 0.7 collective-permute-start.8
  14.5 0.7 collective-permute-start.4
  15.2 9.2 %collective-permute-start.9 = (bf16[256,384]{1,0:T(8,128)(2,1)S(1)}, bf16[256,384]{1,0:T(8,128)(2,1)S(1)}, u32[]{:S(2)}, u32[]{:S(2)}) collective-permute-start(bf16[256,384]{1,0:T(8,128)(2,1)S(1)} %collective-permute-done.8.refs_1_.refs_2_.refs_6_.refs_7_), channel_id=1, source_target_pairs={{0,1},{1,0},{2,3},{3,2},{4,5},{5,4},{6,7},{7,6},{8,9},{9,8},{10,11... | collective-permute-start | bytes 589832 | tf_op jit(solution)/shard_map/ppermute | solution.py:158
  24.4 0.7 collective-permute-start
  25.1 0.7 collective-permute-start.6
  25.8 5.0 %collective-permute-start.3 = (bf16[1536,128]{1,0:T(8,128)(2,1)S(1)}, bf16[1536,128]{1,0:T(8,128)(2,1)S(1)}, u32[]{:S(2)}, u32[]{:S(2)}) collective-permute-start(bf16[1536,128]{1,0:T(8,128)(2,1)S(1)} %get-tuple-element.14.lead_ref), channel_id=1, source_target_pairs={{0,1},{1,0},{2,3},{3,2},{4,5},{5,4},{6,7},{7,6},{8,9},{9,8},{10,11... | collective-permute-start | bytes 1179656 | tf_op jit(solution)/shard_map/ppermute | solution.py:158
  31.8 1.5 %collective-permute-start.10 = (bf16[128,256]{1,0:T(8,128)(2,1)S(1)}, bf16[128,256]{1,0:T(8,128)(2,1)S(1)}, u32[]{:S(2)}, u32[]{:S(2)}) collective-permute-start(bf16[128,256]{1,0:T(8,128)(2,1)S(1)} %shard_map.120.refs_0_), channel_id=1, source_target_pairs={{0,8},{4,12},{8,16},{12,20},{16,24},{20,28},{24,0},{28,4},{1,9},{5... | collective-permute-start | bytes 196616 | tf_op jit(solution)/shard_map/ppermute | solution.py:23
  33.3 1.5 %collective-permute-start.11 = (bf16[128,256]{1,0:T(8,128)(2,1)S(1)}, bf16[128,256]{1,0:T(8,128)(2,1)S(1)}, u32[]{:S(2)}, u32[]{:S(2)}) collective-permute-start(bf16[128,256]{1,0:T(8,128)(2,1)S(1)} %shard_map.120.refs_0_), channel_id=1, source_target_pairs={{0,16},{4,20},{8,24},{12,28},{16,0},{20,4},{24,8},{28,12},{1,17},{... | collective-permute-start | bytes 196616 | tf_op jit(solution)/shard_map/ppermute | solution.py:23
  34.8 2.2 %collective-permute-done.10.refs_1_.refs_5_ = bf16[128,256]{1,0:T(8,128)(2,1)S(1)} collective-permute-done((bf16[128,256]{1,0:T(8,128)(2,1)S(1)}, bf16[128,256]{1,0:T(8,128)(2,1)S(1)}, u32[]{:S(2)}, u32[]{:S(2)}) %collective-permute-start.10) | collective-permute-done | bytes 65568 | tf_op jit(solution)/shard_map/ppermute | solution.py:23
  37.0 6.0 %collective-permute-start.5 = (bf16[1536,128]{1,0:T(8,128)(2,1)S(1)}, bf16[1536,128]{1,0:T(8,128)(2,1)S(1)}, u32[]{:S(2)}, u32[]{:S(2)}) collective-permute-start(bf16[1536,128]{1,0:T(8,128)(2,1)S(1)} %get-tuple-element.15.trail_ref), channel_id=1, source_target_pairs={{0,1},{1,0},{2,3},{3,2},{4,5},{5,4},{6,7},{7,6},{8,9},{9,8},{10,11... | collective-permute-start | bytes 1179656 | tf_op jit(solution)/shard_map/ppermute | solution.py:158
  43.0 1.4 %collective-permute-start.12 = (bf16[128,256]{1,0:T(8,128)(2,1)S(1)}, bf16[128,256]{1,0:T(8,128)(2,1)S(1)}, u32[]{:S(2)}, u32[]{:S(2)}) collective-permute-start(bf16[128,256]{1,0:T(8,128)(2,1)S(1)} %shard_map.120.refs_0_), channel_id=1, source_target_pairs={{0,24},{4,28},{8,0},{12,4},{16,8},{20,12},{24,16},{28,20},{1,25},{... | collective-permute-start | bytes 196616 | tf_op jit(solution)/shard_map/ppermute | solution.py:23
  44.4 2.8 %collective-permute-done.12.refs_3_.refs_7_ = bf16[128,256]{1,0:T(8,128)(2,1)S(1)} collective-permute-done((bf16[128,256]{1,0:T(8,128)(2,1)S(1)}, bf16[128,256]{1,0:T(8,128)(2,1)S(1)}, u32[]{:S(2)}, u32[]{:S(2)}) %collective-permute-start.12) | collective-permute-done | bytes 65568 | tf_op jit(solution)/shard_map/ppermute | solution.py:23
  47.3 4.6 %collective-permute-start.1 = (bf16[1536,128]{1,0:T(8,128)(2,1)S(1)}, bf16[1536,128]{1,0:T(8,128)(2,1)S(1)}, u32[]{:S(2)}, u32[]{:S(2)}) collective-permute-start(bf16[1536,128]{1,0:T(8,128)(2,1)S(1)} %collective-permute-done.rest_0_.rest_1_), channel_id=1, source_target_pairs={{0,2},{1,0},{2,3},{3,1},{4,6},{5,4},{6,7},{7,5},{8,10},{9,8},{10,1... | collective-permute-start | bytes 1179656 | tf_op jit(solution)/shard_map/ppermute | solution.py:158
  51.9 1.2 collective-permute-start.15
  53.1 4.2 %shard_map.114 = (bf16[1536,1536]{1,0:T(8,128)(2,1)S(1)}, f32[1536,256]{1,0:T(8,128)S(1)}) custom-call(f32[1,1]{1,0:T(1,128)} %bitcast.6.low_ref, f32[1,1]{1,0:T(1,128)} %bitcast.11.high_ref, bf16[1536,128]{1,0:T(8,128)(2,1)S(1)} %copy-done.2, f32[1536,256]{1,0:T(8,128)S(1)} %gather_fusion, bf16[1536,128]{1,0:T(8,128)(2,1)S(1)} %get-tuple-element.14.lead_ref, ...), custom_call_target="tpu_custom_call" | custom-call | flops 1811939328 | bytes 8650752 | tf_op jit(solution)/shard_map/pallas_call | solution.py:55
  57.4 3.2 %shard_map.116.block_ref = bf16[1536,1536]{1,0:T(8,128)(2,1)S(1)} custom-call(s32[1,2]{1,0:T(1,128)S(1)} %copy-done.6, bf16[1536,128]{1,0:T(8,128)(2,1)S(1)} %copy-done.2, bf16[1536,128]{1,0:T(8,128)(2,1)S(1)} %collective-permute-done.2.rest_0_, bf16[1536,128]{1,0:T(8,128)(2,1)S(1)} %collective-permute-done.rest_0_.rest_1_), custom_call_target="tpu_custom_call" | custom-call | flops 603979776 | bytes 5505024 | tf_op jit(solution)/shard_map/pallas_call | solution.py:55
  60.6 2.4 %shard_map.117.rest_ref = f32[1536,256]{1,0:T(8,128)S(1)} custom-call(s32[1,2]{1,0:T(1,128)S(1)} %copy-done.6, bf16[1536,1536]{1,0:T(8,128)(2,1)S(1)} %shard_map.116.block_ref, f32[1536,256]{1,0:T(8,128)S(1)} %get-tuple-element.17.rest_ref, bf16[1536,128]{1,0:T(8,128)(2,1)S(1)} %collective-permute-done.3.refs_0_, ...), custom_call_target="tpu_custom_call" | custom-call | flops 1207959552 | bytes 8650752 | tf_op jit(solution)/shard_map/pallas_call | solution.py:55
  63.0 2.8 %collective-permute-done.1.rest_1_ = bf16[1536,128]{1,0:T(8,128)(2,1)S(1)} collective-permute-done((bf16[1536,128]{1,0:T(8,128)(2,1)S(1)}, bf16[1536,128]{1,0:T(8,128)(2,1)S(1)}, u32[]{:S(2)}, u32[]{:S(2)}) %collective-permute-start.1) | collective-permute-done | bytes 393248 | tf_op jit(solution)/shard_map/ppermute | solution.py:158
  65.8 3.2 %shard_map.115.block_ref = bf16[1536,1536]{1,0:T(8,128)(2,1)S(1)} custom-call(s32[1,2]{1,0:T(1,128)S(1)} %copy-done.6, bf16[1536,128]{1,0:T(8,128)(2,1)S(1)} %copy-done.2, bf16[1536,128]{1,0:T(8,128)(2,1)S(1)} %collective-permute-done.rest_0_.rest_1_, bf16[1536,128]{1,0:T(8,128)(2,1)S(1)} %collective-permute-done.1.rest_1_), custom_call_target="tpu_custom_call" | custom-call | flops 603979776 | bytes 5505024 | tf_op jit(solution)/shard_map/pallas_call | solution.py:55
  69.1 1.1 shard_map.122.coupled_ref
  70.1 4.1 %collective-permute-done.14.refs_1_ = bf16[1536,128]{1,0:T(8,128)(2,1)S(1)} collective-permute-done((bf16[1536,128]{1,0:T(8,128)(2,1)S(1)}, bf16[1536,128]{1,0:T(8,128)(2,1)S(1)}, u32[]{:S(2)}, u32[]{:S(2)}) %collective-permute-start.14) | collective-permute-done | bytes 393248 | tf_op jit(solution)/shard_map/ppermute | solution.py:158
  74.2 3.0 %shard_map.123 = (f32[1536,128]{1,0:T(8,128)S(1)}, bf16[1536,128]{1,0:T(8,128)(2,1)S(1)}, bf16[128,128]{1,0:T(8,128)(2,1)S(1)}) custom-call(s32[1,2]{1,0:T(1,128)S(1)} %copy-done.6, f32[1,1]{1,0:T(1,128)} %bitcast.7.low_ref, f32[1,1]{1,0:T(1,128)} %bitcast.12.high_ref, bf16[1536,1536]{1,0:T(8,128)(2,1)S(1)} %shard_map.115.block_ref, ...), custom_call_target="tpu_custom_call" | custom-call | flops 603979776 | bytes 7864320 | tf_op jit(solution)/shard_map/pallas_call | solution.py:55
  77.3 1.3 %collective-permute-done.15.refs_1_ = bf16[1536,128]{1,0:T(8,128)(2,1)S(1)} collective-permute-done((bf16[1536,128]{1,0:T(8,128)(2,1)S(1)}, bf16[1536,128]{1,0:T(8,128)(2,1)S(1)}, u32[]{:S(2)}, u32[]{:S(2)}) %collective-permute-start.15) | collective-permute-done | bytes 393248 | tf_op jit(solution)/shard_map/ppermute | solution.py:158
  78.6 3.1 %shard_map.124 = (f32[1536,128]{1,0:T(8,128)S(1)}, bf16[1536,128]{1,0:T(8,128)(2,1)S(1)}, bf16[128,256]{1,0:T(8,128)(2,1)S(1)}) custom-call(s32[1,2]{1,0:T(1,128)S(1)} %copy-done.6, f32[1,1]{1,0:T(1,128)} %bitcast.8.low_ref, f32[1,1]{1,0:T(1,128)} %bitcast.13.high_ref, bf16[1536,1536]{1,0:T(8,128)(2,1)S(1)} %shard_map.115.block_ref, ...), custom_call_target="tpu_custom_call" | custom-call | flops 603979776 | bytes 7864320 | tf_op jit(solution)/shard_map/pallas_call | solution.py:55
  81.7 3.8 %collective-permute-start.20 = (bf16[128,256]{1,0:T(8,128)(2,1)S(1)}, bf16[128,256]{1,0:T(8,128)(2,1)S(1)}, u32[]{:S(2)}, u32[]{:S(2)}) collective-permute-start(bf16[128,256]{1,0:T(8,128)(2,1)S(1)} %get-tuple-element.25.refs_0_.refs_10_), channel_id=1, source_target_pairs={{0,1},{1,0},{2,3},{3,2},{4,5},{5,4},{6,7},{7,6},{8,9},{9,8},{10,11... | collective-permute-start | bytes 196616 | tf_op jit(solution)/shard_map/ppermute | solution.py:158
  85.5 0.7 collective-permute-start.17
  86.2 1.6 %collective-permute-done.20.refs_1_.refs_0_ = bf16[128,256]{1,0:T(8,128)(2,1)S(1)} collective-permute-done((bf16[128,256]{1,0:T(8,128)(2,1)S(1)}, bf16[128,256]{1,0:T(8,128)(2,1)S(1)}, u32[]{:S(2)}, u32[]{:S(2)}) %collective-permute-start.20) | collective-permute-done | bytes 65568 | tf_op jit(solution)/shard_map/ppermute | solution.py:158
  87.8 0.7 collective-permute-start.21
  88.5 0.9 collective-permute-start.19
  89.4 12.3 %collective-permute-start.22 = (bf16[256,256]{1,0:T(8,128)(2,1)S(1)}, bf16[256,256]{1,0:T(8,128)(2,1)S(1)}, u32[]{:S(2)}, u32[]{:S(2)}) collective-permute-start(bf16[256,256]{1,0:T(8,128)(2,1)S(1)} %collective-permute-done.21.refs_1_.refs_2_), channel_id=1, source_target_pairs={{0,1},{1,0},{2,3},{3,2},{4,5},{5,4},{6,7},{7,6},{8,9},{9,8},{10,11... | collective-permute-start | bytes 393224 | tf_op jit(solution)/shard_map/ppermute | solution.py:158
  101.6 2.0 %collective-permute-start.16 = (bf16[1536,128]{1,0:T(8,128)(2,1)S(1)}, bf16[1536,128]{1,0:T(8,128)(2,1)S(1)}, u32[]{:S(2)}, u32[]{:S(2)}) collective-permute-start(bf16[1536,128]{1,0:T(8,128)(2,1)S(1)} %get-tuple-element.18.lead_ref), channel_id=1, source_target_pairs={{0,1},{1,0},{2,3},{3,2},{4,5},{5,4},{6,7},{7,6},{8,9},{9,8},{10,11... | collective-permute-start | bytes 1179656 | tf_op jit(solution)/shard_map/ppermute | solution.py:158
  103.6 2.3 %collective-permute-done.22.refs_3_.refs_4_ = bf16[256,256]{1,0:T(8,128)(2,1)S(1)} collective-permute-done((bf16[256,256]{1,0:T(8,128)(2,1)S(1)}, bf16[256,256]{1,0:T(8,128)(2,1)S(1)}, u32[]{:S(2)}, u32[]{:S(2)}) %collective-permute-start.22) | collective-permute-done | bytes 131104 | tf_op jit(solution)/shard_map/ppermute | solution.py:158
  106.2 1.5 %collective-permute-start.23 = (bf16[128,256]{1,0:T(8,128)(2,1)S(1)}, bf16[128,256]{1,0:T(8,128)(2,1)S(1)}, u32[]{:S(2)}, u32[]{:S(2)}) collective-permute-start(bf16[128,256]{1,0:T(8,128)(2,1)S(1)} %shard_map.128.refs_0_), channel_id=1, source_target_pairs={{0,8},{4,12},{8,16},{12,20},{16,24},{20,28},{24,0},{28,4},{1,9},{5... | collective-permute-start | bytes 196616 | tf_op jit(solution)/shard_map/ppermute | solution.py:23
  107.8 3.7 %collective-permute-done.23.refs_1_.refs_5_ = bf16[128,256]{1,0:T(8,128)(2,1)S(1)} collective-permute-done((bf16[128,256]{1,0:T(8,128)(2,1)S(1)}, bf16[128,256]{1,0:T(8,128)(2,1)S(1)}, u32[]{:S(2)}, u32[]{:S(2)}) %collective-permute-start.23) | collective-permute-done | bytes 65568 | tf_op jit(solution)/shard_map/ppermute | solution.py:23
  111.5 1.5 %collective-permute-start.24 = (bf16[128,256]{1,0:T(8,128)(2,1)S(1)}, bf16[128,256]{1,0:T(8,128)(2,1)S(1)}, u32[]{:S(2)}, u32[]{:S(2)}) collective-permute-start(bf16[128,256]{1,0:T(8,128)(2,1)S(1)} %shard_map.128.refs_0_), channel_id=1, source_target_pairs={{0,16},{4,20},{8,24},{12,28},{16,0},{20,4},{24,8},{28,12},{1,17},{... | collective-permute-start | bytes 196616 | tf_op jit(solution)/shard_map/ppermute | solution.py:23
  113.0 2.1 %collective-permute-start.28 = (bf16[1536,128]{1,0:T(8,128)(2,1)S(1)}, bf16[1536,128]{1,0:T(8,128)(2,1)S(1)}, u32[]{:S(2)}, u32[]{:S(2)}) collective-permute-start(bf16[1536,128]{1,0:T(8,128)(2,1)S(1)} %collective-permute-done.17.refs_1_.refs_0_), channel_id=1, source_target_pairs={{0,2},{1,0},{2,3},{3,1},{4,6},{5,4},{6,7},{7,5},{8,10},{9,8},{10,1... | collective-permute-start | bytes 1179656 | tf_op jit(solution)/shard_map/ppermute | solution.py:158
  115.7 1.5 %collective-permute-start.25 = (bf16[128,256]{1,0:T(8,128)(2,1)S(1)}, bf16[128,256]{1,0:T(8,128)(2,1)S(1)}, u32[]{:S(2)}, u32[]{:S(2)}) collective-permute-start(bf16[128,256]{1,0:T(8,128)(2,1)S(1)} %shard_map.128.refs_0_), channel_id=1, source_target_pairs={{0,24},{4,28},{8,0},{12,4},{16,8},{20,12},{24,16},{28,20},{1,25},{... | collective-permute-start | bytes 196616 | tf_op jit(solution)/shard_map/ppermute | solution.py:23
  117.3 2.1 %collective-permute-start.27 = (bf16[1536,128]{1,0:T(8,128)(2,1)S(1)}, bf16[1536,128]{1,0:T(8,128)(2,1)S(1)}, u32[]{:S(2)}, u32[]{:S(2)}) collective-permute-start(bf16[1536,128]{1,0:T(8,128)(2,1)S(1)} %collective-permute-done.19.refs_3_.refs_0_), channel_id=1, source_target_pairs={{0,2},{1,0},{2,3},{3,1},{4,6},{5,4},{6,7},{7,5},{8,10},{9,8},{10,1... | collective-permute-start | bytes 1179656 | tf_op jit(solution)/shard_map/ppermute | solution.py:158
  120.1 3.0 %shard_map.125 = (f32[1536,256]{1,0:T(8,128)}, f32[1536,256]{1,0:T(8,128)S(1)}) custom-call(f32[1,1]{1,0:T(1,128)} %bitcast.9.low_ref, f32[1,1]{1,0:T(1,128)} %bitcast.14.high_ref, bf16[1536,1536]{1,0:T(8,128)(2,1)S(1)} %get-tuple-element.16.block_ref, bf16[1536,128]{1,0:T(8,128)(2,1)S(1)} %get-tuple-element.18.lead_ref, ...), custom_call_target="tpu_custom_call" | custom-call | flops 1207959552 | bytes 11796480 | tf_op jit(solution)/shard_map/pallas_call | solution.py:55
  123.1 2.4 %shard_map.126.rest_ref = f32[1536,256]{1,0:T(8,128)S(1)} custom-call(s32[1,2]{1,0:T(1,128)S(1)} %copy-done.6, bf16[1536,1536]{1,0:T(8,128)(2,1)S(1)} %shard_map.116.block_ref, f32[1536,256]{1,0:T(8,128)S(1)} %get-tuple-element.24.rest_ref, bf16[1536,128]{1,0:T(8,128)(2,1)S(1)} %collective-permute-done.16.refs_0_, ...), custom_call_target="tpu_custom_call" | custom-call | flops 1207959552 | bytes 8650752 | tf_op jit(solution)/shard_map/pallas_call | solution.py:55
  125.5 1.1 shard_map.130.coupled_ref
  126.7 2.8 %shard_map.131.refs_2_ = f32[1536,256]{1,0:T(8,128)} custom-call(s32[1,2]{1,0:T(1,128)S(1)} %copy-done.6, bf16[1536,1536]{1,0:T(8,128)(2,1)S(1)} %shard_map.115.block_ref, f32[1536,256]{1,0:T(8,128)S(1)} %shard_map.126.rest_ref, bf16[1536,128]{1,0:T(8,128)(2,1)S(1)} %copy-done.1, bf16[128,256]{1,0:T(8,128)(2,1)S(1)} %shard_map.130.coupled_ref, ...), custom_call_target="tpu_custom_call" | custom-call | flops 603979776 | bytes 6684672 | tf_op jit(solution)/shard_map/pallas_call | solution.py:55
  130.1 2.8 %shard_map.132 = f32[1536,256]{1,0:T(8,128)} custom-call(s32[1,2]{1,0:T(1,128)S(1)} %copy-done.6, bf16[1536,1536]{1,0:T(8,128)(2,1)S(1)} %shard_map.115.block_ref, f32[1536,256]{1,0:T(8,128)S(1)} %shard_map.126.rest_ref, bf16[1536,128]{1,0:T(8,128)(2,1)S(1)} %copy-done.1, ...), custom_call_target="tpu_custom_call", output_to_operand_aliasing={{}: (7, {})} | custom-call | flops 603979776 | bytes 6684672 | tf_op jit(solution)/shard_map/pallas_call | solution.py:55
  (47 shorter events, 4.1 us)
Async XLA Ops:
  0.6 2.2 %copy-start = (f32[1536,256]{1,0:T(8,128)S(1)}, f32[1536,256]{1,0:T(8,128)}, u32[]{:S(2)}) copy-start(f32[1536,256]{1,0:T(8,128)} %param.11) | copy-start | bytes 4718596
  6.5 1.0 copy-start.1
  6.5 1.0 copy-start.5
  6.5 17.9 %copy-start.2 = (bf16[1536,128]{1,0:T(8,128)(2,1)S(1)}, bf16[1536,128]{1,0:T(8,128)(2,1)}, u32[]{:S(2)}) copy-start(bf16[1536,128]{1,0:T(8,128)(2,1)} %points_ref.5) | copy-start | bytes 1179652
  7.9 5.9 %collective-permute-start.7 = (bf16[128,384]{1,0:T(8,128)(2,1)S(1)}, bf16[128,384]{1,0:T(8,128)(2,1)S(1)}, u32[]{:S(2)}, u32[]{:S(2)}) collective-permute-start(bf16[128,384]{1,0:T(8,128)(2,1)S(1)} %shard_map.118.refs_0_.refs_10_.refs_11_), channel_id=1, source_target_pairs={{0,1},{1,0},{2,3},{3,2},{4,5},{5,4},{6,7},{7,6},{8,9},{9,8},{10,11... | collective-permute-start | bytes 294920 | tf_op jit(solution)/shard_map/ppermute | solution.py:158
  13.8 1.4 %collective-permute-start.8 = (bf16[256,384]{1,0:T(8,128)(2,1)S(1)}, bf16[256,384]{1,0:T(8,128)(2,1)S(1)}, u32[]{:S(2)}, u32[]{:S(2)}) collective-permute-start(bf16[256,384]{1,0:T(8,128)(2,1)S(1)} %shard_map.119), channel_id=1, source_target_pairs={{0,0},{1,2},{2,1},{3,3},{4,4},{5,6},{6,5},{7,7},{8,8},{9,10},{10,9... | collective-permute-start | bytes 589832 | tf_op jit(solution)/shard_map/ppermute | solution.py:158
  14.5 17.2 %collective-permute-start.4 = (bf16[1536,128]{1,0:T(8,128)(2,1)S(1)}, bf16[1536,128]{1,0:T(8,128)(2,1)S(1)}, u32[]{:S(2)}, u32[]{:S(2)}) collective-permute-start(bf16[1536,128]{1,0:T(8,128)(2,1)S(1)} %get-tuple-element.14.lead_ref), channel_id=1, source_target_pairs={{0,0},{1,2},{2,1},{3,3},{4,4},{5,6},{6,5},{7,7},{8,8},{9,10},{10,9... | collective-permute-start | bytes 1179656 | tf_op jit(solution)/shard_map/ppermute | solution.py:158
  15.2 15.6 %collective-permute-start.9 = (bf16[256,384]{1,0:T(8,128)(2,1)S(1)}, bf16[256,384]{1,0:T(8,128)(2,1)S(1)}, u32[]{:S(2)}, u32[]{:S(2)}) collective-permute-start(bf16[256,384]{1,0:T(8,128)(2,1)S(1)} %collective-permute-done.8.refs_1_.refs_2_.refs_6_.refs_7_), channel_id=1, source_target_pairs={{0,1},{1,0},{2,3},{3,2},{4,5},{5,4},{6,7},{7,6},{8,9},{9,8},{10,11... | collective-permute-start | bytes 589832 | tf_op jit(solution)/shard_map/ppermute | solution.py:158
  24.4 8.9 %collective-permute-start = (bf16[1536,128]{1,0:T(8,128)(2,1)S(1)}, bf16[1536,128]{1,0:T(8,128)(2,1)S(1)}, u32[]{:S(2)}, u32[]{:S(2)}) collective-permute-start(bf16[1536,128]{1,0:T(8,128)(2,1)S(1)} %copy-done.2), channel_id=1, source_target_pairs={{0,0},{1,2},{2,1},{3,3},{4,4},{5,6},{6,5},{7,7},{8,8},{9,10},{10,9... | collective-permute-start | bytes 1179656 | tf_op jit(solution)/shard_map/ppermute | solution.py:158
  25.1 26.7 %collective-permute-start.6 = (bf16[1536,128]{1,0:T(8,128)(2,1)S(1)}, bf16[1536,128]{1,0:T(8,128)(2,1)S(1)}, u32[]{:S(2)}, u32[]{:S(2)}) collective-permute-start(bf16[1536,128]{1,0:T(8,128)(2,1)S(1)} %get-tuple-element.15.trail_ref), channel_id=1, source_target_pairs={{0,0},{1,2},{2,1},{3,3},{4,4},{5,6},{6,5},{7,7},{8,8},{9,10},{10,9... | collective-permute-start | bytes 1179656 | tf_op jit(solution)/shard_map/ppermute | solution.py:158
  25.8 26.1 %collective-permute-start.3 = (bf16[1536,128]{1,0:T(8,128)(2,1)S(1)}, bf16[1536,128]{1,0:T(8,128)(2,1)S(1)}, u32[]{:S(2)}, u32[]{:S(2)}) collective-permute-start(bf16[1536,128]{1,0:T(8,128)(2,1)S(1)} %get-tuple-element.14.lead_ref), channel_id=1, source_target_pairs={{0,1},{1,0},{2,3},{3,2},{4,5},{5,4},{6,7},{7,6},{8,9},{9,8},{10,11... | collective-permute-start | bytes 1179656 | tf_op jit(solution)/shard_map/ppermute | solution.py:158
  30.8 22.3 %collective-permute-start.2 = (bf16[1536,128]{1,0:T(8,128)(2,1)S(1)}, bf16[1536,128]{1,0:T(8,128)(2,1)S(1)}, u32[]{:S(2)}, u32[]{:S(2)}) collective-permute-start(bf16[1536,128]{1,0:T(8,128)(2,1)S(1)} %copy-done.2), channel_id=1, source_target_pairs={{0,1},{1,0},{2,3},{3,2},{4,5},{5,4},{6,7},{7,6},{8,9},{9,8},{10,11... | collective-permute-start | bytes 1179656 | tf_op jit(solution)/shard_map/ppermute | solution.py:158
  31.8 5.2 %collective-permute-start.10 = (bf16[128,256]{1,0:T(8,128)(2,1)S(1)}, bf16[128,256]{1,0:T(8,128)(2,1)S(1)}, u32[]{:S(2)}, u32[]{:S(2)}) collective-permute-start(bf16[128,256]{1,0:T(8,128)(2,1)S(1)} %shard_map.120.refs_0_), channel_id=1, source_target_pairs={{0,8},{4,12},{8,16},{12,20},{16,24},{20,28},{24,0},{28,4},{1,9},{5... | collective-permute-start | bytes 196616 | tf_op jit(solution)/shard_map/ppermute | solution.py:23
  33.3 9.7 %collective-permute-start.11 = (bf16[128,256]{1,0:T(8,128)(2,1)S(1)}, bf16[128,256]{1,0:T(8,128)(2,1)S(1)}, u32[]{:S(2)}, u32[]{:S(2)}) collective-permute-start(bf16[128,256]{1,0:T(8,128)(2,1)S(1)} %shard_map.120.refs_0_), channel_id=1, source_target_pairs={{0,16},{4,20},{8,24},{12,28},{16,0},{20,4},{24,8},{28,12},{1,17},{... | collective-permute-start | bytes 196616 | tf_op jit(solution)/shard_map/ppermute | solution.py:23
  37.0 23.6 %collective-permute-start.5 = (bf16[1536,128]{1,0:T(8,128)(2,1)S(1)}, bf16[1536,128]{1,0:T(8,128)(2,1)S(1)}, u32[]{:S(2)}, u32[]{:S(2)}) collective-permute-start(bf16[1536,128]{1,0:T(8,128)(2,1)S(1)} %get-tuple-element.15.trail_ref), channel_id=1, source_target_pairs={{0,1},{1,0},{2,3},{3,2},{4,5},{5,4},{6,7},{7,6},{8,9},{9,8},{10,11... | collective-permute-start | bytes 1179656 | tf_op jit(solution)/shard_map/ppermute | solution.py:158
  43.0 4.3 %collective-permute-start.12 = (bf16[128,256]{1,0:T(8,128)(2,1)S(1)}, bf16[128,256]{1,0:T(8,128)(2,1)S(1)}, u32[]{:S(2)}, u32[]{:S(2)}) collective-permute-start(bf16[128,256]{1,0:T(8,128)(2,1)S(1)} %shard_map.120.refs_0_), channel_id=1, source_target_pairs={{0,24},{4,28},{8,0},{12,4},{16,8},{20,12},{24,16},{28,20},{1,25},{... | collective-permute-start | bytes 196616 | tf_op jit(solution)/shard_map/ppermute | solution.py:23
  47.3 18.6 %collective-permute-start.1 = (bf16[1536,128]{1,0:T(8,128)(2,1)S(1)}, bf16[1536,128]{1,0:T(8,128)(2,1)S(1)}, u32[]{:S(2)}, u32[]{:S(2)}) collective-permute-start(bf16[1536,128]{1,0:T(8,128)(2,1)S(1)} %collective-permute-done.rest_0_.rest_1_), channel_id=1, source_target_pairs={{0,2},{1,0},{2,3},{3,1},{4,6},{5,4},{6,7},{7,5},{8,10},{9,8},{10,1... | collective-permute-start | bytes 1179656 | tf_op jit(solution)/shard_map/ppermute | solution.py:158
  51.8 22.4 %collective-permute-start.14 = (bf16[1536,128]{1,0:T(8,128)(2,1)S(1)}, bf16[1536,128]{1,0:T(8,128)(2,1)S(1)}, u32[]{:S(2)}, u32[]{:S(2)}) collective-permute-start(bf16[1536,128]{1,0:T(8,128)(2,1)S(1)} %collective-permute-done.4.refs_1_.refs_0_), channel_id=1, source_target_pairs={{0,2},{1,0},{2,3},{3,1},{4,6},{5,4},{6,7},{7,5},{8,10},{9,8},{10,1... | collective-permute-start | bytes 1179656 | tf_op jit(solution)/shard_map/ppermute | solution.py:158
  51.9 26.7 %collective-permute-start.15 = (bf16[1536,128]{1,0:T(8,128)(2,1)S(1)}, bf16[1536,128]{1,0:T(8,128)(2,1)S(1)}, u32[]{:S(2)}, u32[]{:S(2)}) collective-permute-start(bf16[1536,128]{1,0:T(8,128)(2,1)S(1)} %collective-permute-done.6.refs_3_.refs_0_), channel_id=1, source_target_pairs={{0,2},{1,0},{2,3},{3,1},{4,6},{5,4},{6,7},{7,5},{8,10},{9,8},{10,1... | collective-permute-start | bytes 1179656 | tf_op jit(solution)/shard_map/ppermute | solution.py:158
  53.1 15.9 %collective-permute-start.13 = (bf16[512,256]{1,0:T(8,128)(2,1)S(1)}, bf16[512,256]{1,0:T(8,128)(2,1)S(1)}, u32[]{:S(2)}, u32[]{:S(2)}) collective-permute-start(bf16[512,256]{1,0:T(8,128)(2,1)S(1)} %shard_map.121), channel_id=1, source_target_pairs={{0,4},{4,0},{8,12},{12,8},{16,20},{20,16},{24,28},{28,24},{1,5},{5... | collective-permute-start | bytes 786440 | tf_op jit(solution)/shard_map/ppermute | solution.py:501
  53.1 4.2 %copy-start.6 = (s32[1,2]{1,0:T(1,128)S(1)}, s32[1,2]{1,0:T(1,128)}, u32[]{:S(2)}) copy-start(s32[1,2]{1,0:T(1,128)} %near_ref.19) | copy-start | bytes 28
  63.0 6.0 %copy-start.3 = (bf16[1,8,128,128]{3,2,1,0:T(8,128)(2,1)S(1)}, bf16[1,8,128,128]{3,2,1,0:T(8,128)(2,1)}, u32[]{:S(2)}) copy-start(bf16[1,8,128,128]{3,2,1,0:T(8,128)(2,1)} %param.17) | copy-start | bytes 786436
  63.0 6.0 %copy-start.4 = (bf16[1,4,128,128]{3,2,1,0:T(8,128)(2,1)S(1)}, bf16[1,4,128,128]{3,2,1,0:T(8,128)(2,1)}, u32[]{:S(2)}) copy-start(bf16[1,4,128,128]{3,2,1,0:T(8,128)(2,1)} %param.15) | copy-start | bytes 393220
  81.7 6.1 %collective-permute-start.20 = (bf16[128,256]{1,0:T(8,128)(2,1)S(1)}, bf16[128,256]{1,0:T(8,128)(2,1)S(1)}, u32[]{:S(2)}, u32[]{:S(2)}) collective-permute-start(bf16[128,256]{1,0:T(8,128)(2,1)S(1)} %get-tuple-element.25.refs_0_.refs_10_), channel_id=1, source_target_pairs={{0,1},{1,0},{2,3},{3,2},{4,5},{5,4},{6,7},{7,6},{8,9},{9,8},{10,11... | collective-permute-start | bytes 196616 | tf_op jit(solution)/shard_map/ppermute | solution.py:158
  85.5 27.4 %collective-permute-start.17 = (bf16[1536,128]{1,0:T(8,128)(2,1)S(1)}, bf16[1536,128]{1,0:T(8,128)(2,1)S(1)}, u32[]{:S(2)}, u32[]{:S(2)}) collective-permute-start(bf16[1536,128]{1,0:T(8,128)(2,1)S(1)} %get-tuple-element.18.lead_ref), channel_id=1, source_target_pairs={{0,0},{1,2},{2,1},{3,3},{4,4},{5,6},{6,5},{7,7},{8,8},{9,10},{10,9... | collective-permute-start | bytes 1179656 | tf_op jit(solution)/shard_map/ppermute | solution.py:158
  87.8 1.6 %collective-permute-start.21 = (bf16[256,256]{1,0:T(8,128)(2,1)S(1)}, bf16[256,256]{1,0:T(8,128)(2,1)S(1)}, u32[]{:S(2)}, u32[]{:S(2)}) collective-permute-start(bf16[256,256]{1,0:T(8,128)(2,1)S(1)} %shard_map.127), channel_id=1, source_target_pairs={{0,0},{1,2},{2,1},{3,3},{4,4},{5,6},{6,5},{7,7},{8,8},{9,10},{10,9... | collective-permute-start | bytes 393224 | tf_op jit(solution)/shard_map/ppermute | solution.py:158
  88.5 28.8 %collective-permute-start.19 = (bf16[1536,128]{1,0:T(8,128)(2,1)S(1)}, bf16[1536,128]{1,0:T(8,128)(2,1)S(1)}, u32[]{:S(2)}, u32[]{:S(2)}) collective-permute-start(bf16[1536,128]{1,0:T(8,128)(2,1)S(1)} %get-tuple-element.20.trail_ref), channel_id=1, source_target_pairs={{0,0},{1,2},{2,1},{3,3},{4,4},{5,6},{6,5},{7,7},{8,8},{9,10},{10,9... | collective-permute-start | bytes 1179656 | tf_op jit(solution)/shard_map/ppermute | solution.py:158
  89.4 16.6 %collective-permute-start.22 = (bf16[256,256]{1,0:T(8,128)(2,1)S(1)}, bf16[256,256]{1,0:T(8,128)(2,1)S(1)}, u32[]{:S(2)}, u32[]{:S(2)}) collective-permute-start(bf16[256,256]{1,0:T(8,128)(2,1)S(1)} %collective-permute-done.21.refs_1_.refs_2_), channel_id=1, source_target_pairs={{0,1},{1,0},{2,3},{3,2},{4,5},{5,4},{6,7},{7,6},{8,9},{9,8},{10,11... | collective-permute-start | bytes 393224 | tf_op jit(solution)/shard_map/ppermute | solution.py:158
  101.6 21.5 %collective-permute-start.18 = (bf16[1536,128]{1,0:T(8,128)(2,1)S(1)}, bf16[1536,128]{1,0:T(8,128)(2,1)S(1)}, u32[]{:S(2)}, u32[]{:S(2)}) collective-permute-start(bf16[1536,128]{1,0:T(8,128)(2,1)S(1)} %get-tuple-element.20.trail_ref), channel_id=1, source_target_pairs={{0,1},{1,0},{2,3},{3,2},{4,5},{5,4},{6,7},{7,6},{8,9},{9,8},{10,11... | collective-permute-start | bytes 1179656 | tf_op jit(solution)/shard_map/ppermute | solution.py:158
  101.6 21.5 %collective-permute-start.16 = (bf16[1536,128]{1,0:T(8,128)(2,1)S(1)}, bf16[1536,128]{1,0:T(8,128)(2,1)S(1)}, u32[]{:S(2)}, u32[]{:S(2)}) collective-permute-start(bf16[1536,128]{1,0:T(8,128)(2,1)S(1)} %get-tuple-element.18.lead_ref), channel_id=1, source_target_pairs={{0,1},{1,0},{2,3},{3,2},{4,5},{5,4},{6,7},{7,6},{8,9},{9,8},{10,11... | collective-permute-start | bytes 1179656 | tf_op jit(solution)/shard_map/ppermute | solution.py:158
  106.2 5.2 %collective-permute-start.23 = (bf16[128,256]{1,0:T(8,128)(2,1)S(1)}, bf16[128,256]{1,0:T(8,128)(2,1)S(1)}, u32[]{:S(2)}, u32[]{:S(2)}) collective-permute-start(bf16[128,256]{1,0:T(8,128)(2,1)S(1)} %shard_map.128.refs_0_), channel_id=1, source_target_pairs={{0,8},{4,12},{8,16},{12,20},{16,24},{20,28},{24,0},{28,4},{1,9},{5... | collective-permute-start | bytes 196616 | tf_op jit(solution)/shard_map/ppermute | solution.py:23
  111.5 4.3 %collective-permute-start.24 = (bf16[128,256]{1,0:T(8,128)(2,1)S(1)}, bf16[128,256]{1,0:T(8,128)(2,1)S(1)}, u32[]{:S(2)}, u32[]{:S(2)}) collective-permute-start(bf16[128,256]{1,0:T(8,128)(2,1)S(1)} %shard_map.128.refs_0_), channel_id=1, source_target_pairs={{0,16},{4,20},{8,24},{12,28},{16,0},{20,4},{24,8},{28,12},{1,17},{... | collective-permute-start | bytes 196616 | tf_op jit(solution)/shard_map/ppermute | solution.py:23
  113.0 13.7 %collective-permute-start.28 = (bf16[1536,128]{1,0:T(8,128)(2,1)S(1)}, bf16[1536,128]{1,0:T(8,128)(2,1)S(1)}, u32[]{:S(2)}, u32[]{:S(2)}) collective-permute-start(bf16[1536,128]{1,0:T(8,128)(2,1)S(1)} %collective-permute-done.17.refs_1_.refs_0_), channel_id=1, source_target_pairs={{0,2},{1,0},{2,3},{3,1},{4,6},{5,4},{6,7},{7,5},{8,10},{9,8},{10,1... | collective-permute-start | bytes 1179656 | tf_op jit(solution)/shard_map/ppermute | solution.py:158
  115.7 4.3 %collective-permute-start.25 = (bf16[128,256]{1,0:T(8,128)(2,1)S(1)}, bf16[128,256]{1,0:T(8,128)(2,1)S(1)}, u32[]{:S(2)}, u32[]{:S(2)}) collective-permute-start(bf16[128,256]{1,0:T(8,128)(2,1)S(1)} %shard_map.128.refs_0_), channel_id=1, source_target_pairs={{0,24},{4,28},{8,0},{12,4},{16,8},{20,12},{24,16},{28,20},{1,25},{... | collective-permute-start | bytes 196616 | tf_op jit(solution)/shard_map/ppermute | solution.py:23
  117.3 12.8 %collective-permute-start.27 = (bf16[1536,128]{1,0:T(8,128)(2,1)S(1)}, bf16[1536,128]{1,0:T(8,128)(2,1)S(1)}, u32[]{:S(2)}, u32[]{:S(2)}) collective-permute-start(bf16[1536,128]{1,0:T(8,128)(2,1)S(1)} %collective-permute-done.19.refs_3_.refs_0_), channel_id=1, source_target_pairs={{0,2},{1,0},{2,3},{3,1},{4,6},{5,4},{6,7},{7,5},{8,10},{9,8},{10,1... | collective-permute-start | bytes 1179656 | tf_op jit(solution)/shard_map/ppermute | solution.py:158
  120.0 5.5 %collective-permute-start.26 = (bf16[512,256]{1,0:T(8,128)(2,1)S(1)}, bf16[512,256]{1,0:T(8,128)(2,1)S(1)}, u32[]{:S(2)}, u32[]{:S(2)}) collective-permute-start(bf16[512,256]{1,0:T(8,128)(2,1)S(1)} %shard_map.129), channel_id=1, source_target_pairs={{0,4},{4,0},{8,12},{12,8},{16,20},{20,16},{24,28},{28,24},{1,5},{5... | collective-permute-start | bytes 786440 | tf_op jit(solution)/shard_map/ppermute | solution.py:501

commit v3 on v2

--- a/solution.py
+++ b/solution.py
@@ -1,4 +1,3 @@
-import functools
 import math
 
 import jax
@@ -380,96 +379,196 @@
     )
 
 
-def final(column, near, block, rest, candidates, bases, coupled, written=()):
+def write_tiles(steps, tile, result, out_ref, columns, sems):
+    copies = []
+    for k, (first, count) in enumerate(steps):
+        at = pl.ds(first, count)
+        result[at, :] = tile(at)
+        copies.append(pltpu.make_async_copy(result.at[at, :], out_ref.at[at, columns], sems.at[k]))
+        copies[-1].start()
+    for started in copies:
+        started.wait()
+
+
+def final_lead(near, block, rest, candidates, bases, coupled):
     rows, width = rest.shape
     half = width // 2
     members = lax.axis_size("member")
     count = len(candidates)
     tile_rows = tile_of(rows)
-    columns = pl.ds(column * half, half)
+    steps = [(k, tile_rows) for k in range(0, rows, tile_rows)]
 
     def body(near_ref, block_ref, rest_ref, bases_ref, coupled_ref, *refs):
+        others, (out_ref, trail_ref, result, sems) = refs[:count], refs[count:]
+
+        def use(slot_b):
+            def tile(at):
+                other = rest_ref[at, :] - dot(bases_ref[at, :], coupled_ref[...])
+                trail_ref[at, :] = other[:, half:]
+                return other[:, :half] - slot_b(at)
+
+            write_tiles(steps, tile, result, out_ref, pl.ds(0, half), sems)
+
+        with_slot_b(near_ref, members, block_ref, others, use)
+
+    return call(
+        body, (shape(F32, rows, width), shape(F32, rows, half)),
+        (near, block, rest, bases, coupled, *candidates), scalars=1, out_specs=(ANY_SPEC, VMEM_SPEC),
+        scratch=[VMEM((rows, half), F32), pltpu.SemaphoreType.DMA((len(steps),))],
+        flops=2 * rows * rows * half, bytes_=rows * rows * 2 + rows * half * 10,
+    )
+
+
+def trail_part(near, block, trail, inner, piece):
+    rows, half = trail.shape
+    members = lax.axis_size("member")
+    cut = piece.shape[0]
+
+    def body(near_ref, block_ref, trail_ref, inner_ref, piece_ref, out_ref):
+        choice = slots(near_ref, members)[1]
+
+        @pl.when(choice == 0)
+        def _():
+            def tile(at):
+                out_ref[at, :] = trail_ref[at, :] - dot(block_ref[at, :], inner_ref[...])
+
+            over_tiles(rows, tile)
+
+        @pl.when(choice != 0)
+        def _():
+            def tile(at):
+                out_ref[at, :] = trail_ref[at, :] - dot(block_ref[at, :cut], piece_ref[...])
+
+            over_tiles(rows, tile)
+
+    return call(
+        body, shape(F32, rows, half), (near, block, trail, inner, piece), scalars=1,
+        flops=2 * rows * cut * half, bytes_=rows * cut * 2 + rows * half * 8,
+    )
+
+
+def final_trail(near, block, trail, candidates, first, written):
+    rows, half = trail.shape
+    members = lax.axis_size("member")
+    count = len(candidates)
+    tile_rows = tile_of(rows)
+    steps = [(k, tile_rows) for k in range(0, rows, tile_rows)]
+
+    def body(near_ref, block_ref, trail_ref, *refs):
         others, (out_ref, result, sems) = refs[:count], refs[-3:]
 
         def use(slot_b):
-            copies = []
-            for k in range(rows // tile_rows):
-                at = pl.ds(k * tile_rows, tile_rows)
-                result[at, :] = (
-                    rest_ref[at, columns] - slot_b(at) - dot(bases_ref[at, :], coupled_ref[:, columns]))
-                copies.append(pltpu.make_async_copy(result.at[at, :], out_ref.at[at, columns], sems.at[k]))
-                copies[-1].start()
-            for started in copies:
-                started.wait()
-
-        with_slot_b(near_ref, members, block_ref, others, use)
-
-    return call(
-        body, shape(F32, rows, width), (near, block, rest, bases, coupled, *candidates, *written),
-        in_specs=[SMEM_SPEC] + [VMEM_SPEC] * (4 + count) + [ANY_SPEC] * len(written), out_specs=ANY_SPEC,
-        scratch=[VMEM((rows, half), F32), pltpu.SemaphoreType.DMA((rows // tile_rows,))],
+            def tile(at):
+                return trail_ref[at, :] - slot_b(at)
+
+            write_tiles(steps, tile, result, out_ref, pl.ds(half, half), sems)
+
+        if first is None:
+            with_slot_b(near_ref, members, block_ref, others, use)
+        else:
+            late = slots(near_ref, members)[1] != 0
+            pl.when(late)(lambda: use(lambda at: dot(block_ref[at, first:], others[0][...])))
+            pl.when(jnp.logical_not(late))(lambda: use(lambda at: 0.0))
+
+    return call(
+        body, shape(F32, *written.shape), (near, block, trail, *candidates, written),
+        in_specs=[SMEM_SPEC] + [VMEM_SPEC] * (2 + count) + [ANY_SPEC], out_specs=ANY_SPEC,
+        scratch=[VMEM((rows, half), F32), pltpu.SemaphoreType.DMA((len(steps),))],
         flops=2 * rows * rows * half, bytes_=rows * rows * 2 + rows * half * 10,
-        aliases={5 + count: 0} if written else {},
-    )
-
-
-def pair_mate(member):
-    return member + 1 - 2 * lax.rem(member, 2)
-
-
-def gather_messages(message):
-    members = lax.axis_size("member")
-    rank = message.shape[0]
+        aliases={3 + count: 0},
+    )
+
+
+def merge_all(message, first, rank):
+    members = lax.axis_size("member")
+    width = first["own"].shape[1] - rank if first else message.shape[1] - rank
     if not paired(members):
         others = around(message, "member")
-        sources = [functools.partial(lambda k, m: lax.rem(m + (members - k), members), k)
-                   for k in range(1, members)]
-        return [(other, 0) for other in others], sources
-    mate = permute(message, mates(members))
+        state = {"own": message, "others": others}
+        first = first or state
+        merged = merge_ring(state, first, rank, width)
+        return state, merged
+    down = mates(members)
+    up = mates(members)
+    mate = permute(message, down)
     pair = pack((message, mate))
     crossed = permute(pair, [(i, beside_pair(i, members)) for i in range(members)])
-    handed = permute(crossed, mates(members))
-    return [(mate, 0), (crossed, 0), (crossed, rank), (handed, 0), (handed, rank)], None
-
-
-def message_views(refs, spots, rank, sources, members):
+    state = {"own": message, "pair": pair, "crossed": crossed}
+    first = first or state
+    summed = merge_line(state, first, rank, width)
+    handed = permute(summed, up)
+    state["handed"] = handed
+    return state, choose(summed, handed, width)
+
+
+def merge_ring(state, first, rank, width):
+    count = len(state["others"]) + 1
+
+    def body(*refs):
+        total = jnp.zeros((rank, width), F32)
+        for coeff, carried in zip(refs[:count], refs[count:-1]):
+            total = total + dot_tn(carried[:, width:], coeff[:, :width])
+        refs[-1][...] = total.astype(BF16)
+
+    args = (state["own"], *state["others"], first["own"], *first["others"])
+    return call(
+        body, shape(BF16, rank, width), args,
+        flops=2 * rank * rank * width * count, bytes_=rank * width * 4 * count,
+    )
+
+
+def merge_line(state, first, rank, width):
+    def body(pair_ref, crossed_ref, first_pair_ref, first_crossed_ref, out_ref):
+        total = jnp.zeros((rank, width), F32)
+        for coeffs, carried in ((pair_ref, first_pair_ref), (crossed_ref, first_crossed_ref)):
+            for rows in (slice(0, rank), slice(rank, 2 * rank)):
+                total = total + dot_tn(carried[rows, width:], coeffs[rows, :width])
+        out_ref[:, :width] = total.astype(BF16)
+        out_ref[:, width:] = crossed_ref[rank:, :width]
+
+    return call(
+        body, shape(BF16, rank, 2 * width),
+        (state["pair"], state["crossed"], first["pair"], first["crossed"]),
+        flops=8 * rank * rank * width, bytes_=rank * width * 16,
+    )
+
+
+def choose(summed, handed, width):
+    members = lax.axis_size("member")
+
+    def body(summed_ref, handed_ref, out_ref):
+        end = at_end(lax.axis_index("member"), members)
+        out_ref[...] = jnp.where(end, handed_ref[:, :width], summed_ref[:, :width])
+
+    return call(
+        body, shape(BF16, summed.shape[0], width), (summed, handed),
+        bytes_=summed.shape[0] * width * 6,
+    )
+
+
+def coupled_arrays(state):
+    if "others" in state:
+        return tuple(state["others"])
+    return state["pair"], state["crossed"], state["handed"]
+
+
+def coupled_views(refs, rank, width):
+    members = lax.axis_size("member")
     member = lax.axis_index("member")
-    if sources is not None:
-        return [(source(member), ref[row : row + rank, :]) for (ref, row), source in zip(
-            zip(refs, [row for _, row in spots]), sources)]
+    if not paired(members):
+        return [(lax.rem(member + (members - 1 - k), members), ref[:, :width]) for k, ref in enumerate(refs)]
+    pair_ref, crossed_ref, handed_ref = refs
+    lower = member < members // 2
+    far_end = jnp.where(lower, members - 1, 0)
+    far_middle = jnp.where(lower, members // 2, members // 2 - 1)
+    own_end = members - 1 - far_end
     end = at_end(member, members)
-    near_end = jnp.where(member < members // 2, members // 2, members // 2 - 1)
-    views = [(pair_mate(member), refs[0][...])]
-    for k, number in enumerate((near_end, pair_mate(near_end))):
-        rows = slice(k * rank, (k + 1) * rank)
-        views.append((number, jnp.where(end, refs[3][rows, :], refs[1][rows, :])))
-    return views
-
-
-def merge(own, messages, first_own, first_messages):
-    rank = own.shape[0]
-    width = first_own.shape[1] - rank
-    spots, sources = messages
-    first_spots, _ = first_messages
-    members = lax.axis_size("member")
-    count = len(spots)
-
-    def body(*refs):
-        coeffs, firsts, out_ref = refs[:count], refs[count : 2 * count], refs[-1]
-        own_ref, first_own_ref = refs[2 * count], refs[2 * count + 1]
-        total = dot_tn(first_own_ref[:, width:], own_ref[:, :width])
-        for (_, coeff), (_, carried) in zip(
-            message_views(coeffs, spots, rank, sources, members),
-            message_views(firsts, first_spots, rank, sources, members),
-        ):
-            total = total + dot_tn(carried[:, width:], coeff[:, :width])
-        out_ref[...] = total.astype(BF16)
-
-    args = (*[array for array, _ in spots], *[array for array, _ in first_spots], own, first_own)
-    return call(
-        body, shape(BF16, rank, width), args,
-        flops=2 * rank * rank * width * (count + 1), bytes_=rank * width * 2 * (2 * count + 3),
-    )
+    from_far_end = jnp.where(end, handed_ref[:, width:], crossed_ref[rank:, :width])
+    return [
+        (jnp.where(end, far_middle, own_end), pair_ref[rank:, :width]),
+        (far_middle, crossed_ref[:rank, :width]),
+        (far_end, from_far_end),
+    ]
 
 
 def pack(blocks):
@@ -510,8 +609,8 @@
     inner = inner_of(groups)
     packed = () if beside is None else (beside,)
 
-    spots, sources = messages
-    count = len(spots)
+    arrays = coupled_arrays(messages)
+    count = len(arrays)
 
     def body(near_ref, couplings_ref, transfer_ref, cross_ref, *refs):
         coeffs, others, out_ref = refs[:count], refs[count:-1], refs[-1]
@@ -526,12 +625,12 @@
                 source = lax.rem(side + (groups - k * inner), groups)
                 crossed = crossed + dot(cross_ref[source], others[-1][k * rank : (k + 1) * rank, :])
         within = dot(transfer_ref[...], crossed.astype(BF16))
-        for source, coeff in message_views(coeffs, spots, rank, sources, members):
+        for source, coeff in coupled_views(coeffs, rank, width):
             far = (source != near_ref[0, 0]) & (source != near_ref[0, 1])
-            within = within + jnp.where(far, 1.0, 0.0) * dot(couplings_ref[source], coeff[:, :width])
+            within = within + jnp.where(far, 1.0, 0.0) * dot(couplings_ref[source], coeff)
         out_ref[...] = within.astype(BF16)
 
-    args = (near, couplings, transfer, cross, *[array for array, _ in spots], *merged, *packed)
+    args = (near, couplings, transfer, cross, *arrays, *merged, *packed)
     return call(
         body, shape(BF16, rank, width), args, scalars=1,
         flops=2 * rank * rank * width * (members + groups), bytes_=rank * width * 2 * (members + groups) * 2,
@@ -586,11 +685,11 @@
     ordered = take_rows(right_sides, leaf_order[0])
     lead, trail = start_rows(ordered, low, high)
     message = start_message(lead, trail, bases, transfer)
-    messages = gather_messages(message)
+    rank = transfer.shape[0]
+    messages, merged = merge_all(message, None, rank)
     lead_a, lead_b = moved(lead)
     trail_a, trail_b = moved(trail)
     own_block, rest = self_first(points, ordered, lead, trail, low, high)
-    merged = merge(message, messages, message, messages)
     merged, beside = all_merged(merged)
     rest = subtract_near(near, block_a, rest, lead_a, trail_a)
     coupled = couple(near, couplings, transfer, cross, messages, merged, beside)
@@ -598,16 +697,26 @@
     first_trail, trail, coeff = turn(
         1, near, block_b, rest, trail_b, bases, coupled, ordered, low, high, (coeff,))
 
-    coeffs = gather_messages(coeff)
+    coeffs, merged = merge_all(coeff, messages, rank)
     lead_a, lead_b = moved(lead)
-    trail_a, trail_b = moved(trail)
+    if line:
+        inner, outer = hop(trail)
+        trail_a = (outer, inner)
+        cut = 2 * trail.shape[0] // 3 if trail.shape[0] % 384 == 0 else trail.shape[0] // 2
+        early = across(inner[:cut])
+        late = across(inner[cut:])
+    else:
+        trail_a, trail_b = moved(trail)
     solution_rows, rest = self_second(own_block, lead, trail, first_lead, first_trail, ordered, low, high)
-    merged = merge(coeff, coeffs, message, messages)
     merged, beside = all_merged(merged)
     rest = subtract_near(near, block_a, rest, lead_a, trail_a)
     coupled = couple(near, couplings, transfer, cross, coeffs, merged, beside)
-    residual = final(0, near, block_b, rest, lead_b, bases, coupled)
-    residual = final(1, near, block_b, rest, trail_b, bases, coupled, (residual,))
+    residual, rest = final_lead(near, block_b, rest, lead_b, bases, coupled)
+    if line:
+        rest = trail_part(near, block_b, rest, inner, early)
+        residual = final_trail(near, block_b, rest, (late,), cut, residual)
+    else:
+        residual = final_trail(near, block_b, rest, trail_b, None, residual)
     return solution_rows, residual
 
 

time: 133 us -> 136 us (1.023)
    ppermute x6, waiting for transfers between devices: 10 us -> 11.8 us  [cycle(): lax.ppermute(array, axis, [(i, (i + by) % count) for i in range(count)])]
    pallas_call x20 -> x23, Pallas kernels: 33.6 us -> 34.8 us  [call(): pl.pallas_call(body, out_shape=out, in_specs=in_specs or [SMEM_SPEC] * sc...]
    ppermute x21 -> x22, waiting for transfers between devices: 15.6 us -> 15 us  [permute(): return lax.ppermute(block, 'member', pairs)]
    ppermute x21 -> x22, starting transfers between devices: 57 us -> 56.6 us  [permute(): return lax.ppermute(block, 'member', pairs)]
  transfers between devices with their start and end apart: 29 -> 30, of which waited for: 12 -> 12; matrix products, arithmetic and copies ran while one was open for 0% -> 0% of each run, Pallas kernels for 20% -> 22%
where the time goes in v3:
time: 136 us; the launch traced here: 135 us
  starting transfers between devices  65.9 us (48%)
  Pallas kernels  34.8 us (26%)
  waiting for transfers between devices  26.8 us (20%)
  local copies, waits for them, and re-layouts  4.5 us (3%)
  between operations  2.54 us (2%)
    ppermute x22, starting transfers between devices, permute(): return lax.ppermute(block, 'member', pairs)  56.6 us
    pallas_call x23, Pallas kernels, call(): pl.pallas_call(body, out_shape=out, in_specs=in_specs or [SMEM_SPEC] * sc...  34.8 us
    ppermute x22, waiting for transfers between devices, permute(): return lax.ppermute(block, 'member', pairs)  15 us
    ppermute x6, waiting for transfers between devices, cycle(): lax.ppermute(array, axis, [(i, (i + by) % count) for i in range(count)])  11.8 us
    ppermute x6, starting transfers between devices, cycle(): lax.ppermute(array, axis, [(i, (i + by) % count) for i in range(count)])  9.17 us
    gather x1, local copies, waits for them, and re-layouts, take_rows(): lax.gather(rows, order[:, None], dims, (1, rows.shape[1]), unique_indices...  3.66 us
  transfers between devices with their start and end apart: 30, of which 12 were waited for; matrix products, arithmetic and copies ran while one was open for 0% of the time, Pallas kernels for 22%

profile of v3, /device:TPU:0, one launch (start us, length us, event | category | flops | bytes accessed | tf_op | source)
XLA Modules:
  0.0 135.3 jit_solution(14908631560852178070)
XLA Ops:
  0.6 0.8 reduce
  2.8 3.7 %gather_fusion = f32[1536,256]{1,0:T(8,128)S(1)} fusion(f32[1536,256]{1,0:T(8,128)S(1)} %copy-done, s32[2048]{0:T(1024)S(1)} %pad_clamp_fusion), kind=kCustom, calls=%fused_computation | custom fusion | bytes 3151872 | tf_op jit(solution)/shard_map/gather | solution.py:649
  6.7 0.8 copy-done.1
  7.9 3.1 %collective-permute-start.7 = (bf16[128,384]{1,0:T(8,128)(2,1)S(1)}, bf16[128,384]{1,0:T(8,128)(2,1)S(1)}, u32[]{:S(2)}, u32[]{:S(2)}) collective-permute-start(bf16[128,384]{1,0:T(8,128)(2,1)S(1)} %shard_map.118.refs_0_), channel_id=1, source_target_pairs={{0,1},{1,0},{2,3},{3,2},{4,5},{5,4},{6,7},{7,6},{8,9},{9,8},{10,11... | collective-permute-start | bytes 294920 | tf_op jit(solution)/shard_map/ppermute | solution.py:157
  11.0 2.8 %collective-permute-done.7.refs_1_ = bf16[128,384]{1,0:T(8,128)(2,1)S(1)} collective-permute-done((bf16[128,384]{1,0:T(8,128)(2,1)S(1)}, bf16[128,384]{1,0:T(8,128)(2,1)S(1)}, u32[]{:S(2)}, u32[]{:S(2)}) %collective-permute-start.7) | collective-permute-done | bytes 98336 | tf_op jit(solution)/shard_map/ppermute | solution.py:157
  14.5 0.7 collective-permute-start.4
  15.2 0.7 collective-permute-start
  16.2 9.2 %collective-permute-start.9 = (bf16[128,512]{1,0:T(8,128)(2,1)S(1)}, bf16[128,512]{1,0:T(8,128)(2,1)S(1)}, u32[]{:S(2)}, u32[]{:S(2)}) collective-permute-start(bf16[128,512]{1,0:T(8,128)(2,1)S(1)} %shard_map.120.summed_ref), channel_id=1, source_target_pairs={{0,1},{1,0},{2,3},{3,2},{4,5},{5,4},{6,7},{7,6},{8,9},{9,8},{10,11... | collective-permute-start | bytes 393224 | tf_op jit(solution)/shard_map/ppermute | solution.py:157
  25.4 0.7 collective-permute-start.6
  26.0 3.2 %collective-permute-start.3 = (bf16[1536,128]{1,0:T(8,128)(2,1)S(1)}, bf16[1536,128]{1,0:T(8,128)(2,1)S(1)}, u32[]{:S(2)}, u32[]{:S(2)}) collective-permute-start(bf16[1536,128]{1,0:T(8,128)(2,1)S(1)} %get-tuple-element.16.lead_ref), channel_id=1, source_target_pairs={{0,1},{1,0},{2,3},{3,2},{4,5},{5,4},{6,7},{7,6},{8,9},{9,8},{10,11... | collective-permute-start | bytes 1179656 | tf_op jit(solution)/shard_map/ppermute | solution.py:157
  29.7 2.0 %collective-permute-start.2 = (bf16[1536,128]{1,0:T(8,128)(2,1)S(1)}, bf16[1536,128]{1,0:T(8,128)(2,1)S(1)}, u32[]{:S(2)}, u32[]{:S(2)}) collective-permute-start(bf16[1536,128]{1,0:T(8,128)(2,1)S(1)} %copy-done.2), channel_id=1, source_target_pairs={{0,1},{1,0},{2,3},{3,2},{4,5},{5,4},{6,7},{7,6},{8,9},{9,8},{10,11... | collective-permute-start | bytes 1179656 | tf_op jit(solution)/shard_map/ppermute | solution.py:157
  31.8 1.5 %collective-permute-start.10 = (bf16[128,256]{1,0:T(8,128)(2,1)S(1)}, bf16[128,256]{1,0:T(8,128)(2,1)S(1)}, u32[]{:S(2)}, u32[]{:S(2)}) collective-permute-start(bf16[128,256]{1,0:T(8,128)(2,1)S(1)} %shard_map.121.refs_0_), channel_id=1, source_target_pairs={{0,8},{4,12},{8,16},{12,20},{16,24},{20,28},{24,0},{28,4},{1,9},{5... | collective-permute-start | bytes 196616 | tf_op jit(solution)/shard_map/ppermute | solution.py:22
  33.3 1.5 %collective-permute-start.11 = (bf16[128,256]{1,0:T(8,128)(2,1)S(1)}, bf16[128,256]{1,0:T(8,128)(2,1)S(1)}, u32[]{:S(2)}, u32[]{:S(2)}) collective-permute-start(bf16[128,256]{1,0:T(8,128)(2,1)S(1)} %shard_map.121.refs_0_), channel_id=1, source_target_pairs={{0,16},{4,20},{8,24},{12,28},{16,0},{20,4},{24,8},{28,12},{1,17},{... | collective-permute-start | bytes 196616 | tf_op jit(solution)/shard_map/ppermute | solution.py:22
  34.8 2.2 %collective-permute-done.10.refs_1_.refs_3_ = bf16[128,256]{1,0:T(8,128)(2,1)S(1)} collective-permute-done((bf16[128,256]{1,0:T(8,128)(2,1)S(1)}, bf16[128,256]{1,0:T(8,128)(2,1)S(1)}, u32[]{:S(2)}, u32[]{:S(2)}) %collective-permute-start.10) | collective-permute-done | bytes 65568 | tf_op jit(solution)/shard_map/ppermute | solution.py:22
  37.0 6.0 %collective-permute-start.5 = (bf16[1536,128]{1,0:T(8,128)(2,1)S(1)}, bf16[1536,128]{1,0:T(8,128)(2,1)S(1)}, u32[]{:S(2)}, u32[]{:S(2)}) collective-permute-start(bf16[1536,128]{1,0:T(8,128)(2,1)S(1)} %get-tuple-element.17.trail_ref), channel_id=1, source_target_pairs={{0,1},{1,0},{2,3},{3,2},{4,5},{5,4},{6,7},{7,6},{8,9},{9,8},{10,11... | collective-permute-start | bytes 1179656 | tf_op jit(solution)/shard_map/ppermute | solution.py:157
  43.0 1.4 %collective-permute-start.12 = (bf16[128,256]{1,0:T(8,128)(2,1)S(1)}, bf16[128,256]{1,0:T(8,128)(2,1)S(1)}, u32[]{:S(2)}, u32[]{:S(2)}) collective-permute-start(bf16[128,256]{1,0:T(8,128)(2,1)S(1)} %shard_map.121.refs_0_), channel_id=1, source_target_pairs={{0,24},{4,28},{8,0},{12,4},{16,8},{20,12},{24,16},{28,20},{1,25},{... | collective-permute-start | bytes 196616 | tf_op jit(solution)/shard_map/ppermute | solution.py:22
  44.4 2.8 %collective-permute-done.12.refs_3_.refs_5_ = bf16[128,256]{1,0:T(8,128)(2,1)S(1)} collective-permute-done((bf16[128,256]{1,0:T(8,128)(2,1)S(1)}, bf16[128,256]{1,0:T(8,128)(2,1)S(1)}, u32[]{:S(2)}, u32[]{:S(2)}) %collective-permute-start.12) | collective-permute-done | bytes 65568 | tf_op jit(solution)/shard_map/ppermute | solution.py:22
  47.3 4.6 %collective-permute-start.1 = (bf16[1536,128]{1,0:T(8,128)(2,1)S(1)}, bf16[1536,128]{1,0:T(8,128)(2,1)S(1)}, u32[]{:S(2)}, u32[]{:S(2)}) collective-permute-start(bf16[1536,128]{1,0:T(8,128)(2,1)S(1)} %collective-permute-done.rest_0_.rest_1_), channel_id=1, source_target_pairs={{0,2},{1,0},{2,3},{3,1},{4,6},{5,4},{6,7},{7,5},{8,10},{9,8},{10,1... | collective-permute-start | bytes 1179656 | tf_op jit(solution)/shard_map/ppermute | solution.py:157
  51.9 1.2 collective-permute-start.15
  53.1 4.2 %shard_map.114 = (bf16[1536,1536]{1,0:T(8,128)(2,1)S(1)}, f32[1536,256]{1,0:T(8,128)S(1)}) custom-call(f32[1,1]{1,0:T(1,128)} %bitcast.6.low_ref, f32[1,1]{1,0:T(1,128)} %bitcast.11.high_ref, bf16[1536,128]{1,0:T(8,128)(2,1)S(1)} %copy-done.2, f32[1536,256]{1,0:T(8,128)S(1)} %gather_fusion, bf16[1536,128]{1,0:T(8,128)(2,1)S(1)} %get-tuple-element.16.lead_ref, ...), custom_call_target="tpu_custom_call" | custom-call | flops 1811939328 | bytes 8650752 | tf_op jit(solution)/shard_map/pallas_call | solution.py:54
  57.4 3.2 %shard_map.116.block_ref = bf16[1536,1536]{1,0:T(8,128)(2,1)S(1)} custom-call(s32[1,2]{1,0:T(1,128)S(1)} %copy-done.6, bf16[1536,128]{1,0:T(8,128)(2,1)S(1)} %copy-done.2, bf16[1536,128]{1,0:T(8,128)(2,1)S(1)} %collective-permute-done.2.rest_0_, bf16[1536,128]{1,0:T(8,128)(2,1)S(1)} %collective-permute-done.rest_0_.rest_1_), custom_call_target="tpu_custom_call" | custom-call | flops 603979776 | bytes 5505024 | tf_op jit(solution)/shard_map/pallas_call | solution.py:54
  60.6 2.4 %shard_map.117.rest_ref = f32[1536,256]{1,0:T(8,128)S(1)} custom-call(s32[1,2]{1,0:T(1,128)S(1)} %copy-done.6, bf16[1536,1536]{1,0:T(8,128)(2,1)S(1)} %shard_map.116.block_ref, f32[1536,256]{1,0:T(8,128)S(1)} %get-tuple-element.19.rest_ref, bf16[1536,128]{1,0:T(8,128)(2,1)S(1)} %collective-permute-done.3.refs_0_, ...), custom_call_target="tpu_custom_call" | custom-call | flops 1207959552 | bytes 8650752 | tf_op jit(solution)/shard_map/pallas_call | solution.py:54
  63.1 1.1 shard_map.123.coupled_ref
  64.5 3.2 %shard_map.115.block_ref = bf16[1536,1536]{1,0:T(8,128)(2,1)S(1)} custom-call(s32[1,2]{1,0:T(1,128)S(1)} %copy-done.6, bf16[1536,128]{1,0:T(8,128)(2,1)S(1)} %copy-done.2, bf16[1536,128]{1,0:T(8,128)(2,1)S(1)} %collective-permute-done.rest_0_.rest_1_, bf16[1536,128]{1,0:T(8,128)(2,1)S(1)} %collective-permute-done.1.rest_1_), custom_call_target="tpu_custom_call" | custom-call | flops 603979776 | bytes 5505024 | tf_op jit(solution)/shard_map/pallas_call | solution.py:54
  67.7 5.2 %collective-permute-done.14.refs_1_ = bf16[1536,128]{1,0:T(8,128)(2,1)S(1)} collective-permute-done((bf16[1536,128]{1,0:T(8,128)(2,1)S(1)}, bf16[1536,128]{1,0:T(8,128)(2,1)S(1)}, u32[]{:S(2)}, u32[]{:S(2)}) %collective-permute-start.14) | collective-permute-done | bytes 393248 | tf_op jit(solution)/shard_map/ppermute | solution.py:157
  72.9 3.0 %shard_map.124 = (f32[1536,128]{1,0:T(8,128)S(1)}, bf16[1536,128]{1,0:T(8,128)(2,1)S(1)}, bf16[128,128]{1,0:T(8,128)(2,1)S(1)}) custom-call(s32[1,2]{1,0:T(1,128)S(1)} %copy-done.6, f32[1,1]{1,0:T(1,128)} %bitcast.7.low_ref, f32[1,1]{1,0:T(1,128)} %bitcast.12.high_ref, bf16[1536,1536]{1,0:T(8,128)(2,1)S(1)} %shard_map.115.block_ref, ...), custom_call_target="tpu_custom_call" | custom-call | flops 603979776 | bytes 7864320 | tf_op jit(solution)/shard_map/pallas_call | solution.py:54
  76.0 2.3 %collective-permute-done.15.refs_1_ = bf16[1536,128]{1,0:T(8,128)(2,1)S(1)} collective-permute-done((bf16[1536,128]{1,0:T(8,128)(2,1)S(1)}, bf16[1536,128]{1,0:T(8,128)(2,1)S(1)}, u32[]{:S(2)}, u32[]{:S(2)}) %collective-permute-start.15) | collective-permute-done | bytes 393248 | tf_op jit(solution)/shard_map/ppermute | solution.py:157
  78.2 3.1 %shard_map.125 = (f32[1536,128]{1,0:T(8,128)S(1)}, bf16[1536,128]{1,0:T(8,128)(2,1)S(1)}, bf16[128,256]{1,0:T(8,128)(2,1)S(1)}) custom-call(s32[1,2]{1,0:T(1,128)S(1)} %copy-done.6, f32[1,1]{1,0:T(1,128)} %bitcast.8.low_ref, f32[1,1]{1,0:T(1,128)} %bitcast.13.high_ref, bf16[1536,1536]{1,0:T(8,128)(2,1)S(1)} %shard_map.115.block_ref, ...), custom_call_target="tpu_custom_call" | custom-call | flops 603979776 | bytes 7864320 | tf_op jit(solution)/shard_map/pallas_call | solution.py:54
  81.3 2.8 %collective-permute-start.20 = (bf16[128,256]{1,0:T(8,128)(2,1)S(1)}, bf16[128,256]{1,0:T(8,128)(2,1)S(1)}, u32[]{:S(2)}, u32[]{:S(2)}) collective-permute-start(bf16[128,256]{1,0:T(8,128)(2,1)S(1)} %get-tuple-element.27.refs_0_), channel_id=1, source_target_pairs={{0,1},{1,0},{2,3},{3,2},{4,5},{5,4},{6,7},{7,6},{8,9},{9,8},{10,11... | collective-permute-start | bytes 196616 | tf_op jit(solution)/shard_map/ppermute | solution.py:157
  84.1 0.7 collective-permute-start.17
  84.8 1.6 %collective-permute-done.20.refs_1_ = bf16[128,256]{1,0:T(8,128)(2,1)S(1)} collective-permute-done((bf16[128,256]{1,0:T(8,128)(2,1)S(1)}, bf16[128,256]{1,0:T(8,128)(2,1)S(1)}, u32[]{:S(2)}, u32[]{:S(2)}) %collective-permute-start.20) | collective-permute-done | bytes 65568 | tf_op jit(solution)/shard_map/ppermute | solution.py:157
  87.0 0.9 collective-permute-start.19
  88.2 12.9 %collective-permute-start.22 = (bf16[128,512]{1,0:T(8,128)(2,1)S(1)}, bf16[128,512]{1,0:T(8,128)(2,1)S(1)}, u32[]{:S(2)}, u32[]{:S(2)}) collective-permute-start(bf16[128,512]{1,0:T(8,128)(2,1)S(1)} %shard_map.129.summed_ref), channel_id=1, source_target_pairs={{0,1},{1,0},{2,3},{3,2},{4,5},{5,4},{6,7},{7,6},{8,9},{9,8},{10,11... | collective-permute-start | bytes 393224 | tf_op jit(solution)/shard_map/ppermute | solution.py:157
  101.2 1.9 %collective-permute-start.16 = (bf16[1536,128]{1,0:T(8,128)(2,1)S(1)}, bf16[1536,128]{1,0:T(8,128)(2,1)S(1)}, u32[]{:S(2)}, u32[]{:S(2)}) collective-permute-start(bf16[1536,128]{1,0:T(8,128)(2,1)S(1)} %get-tuple-element.20.lead_ref), channel_id=1, source_target_pairs={{0,1},{1,0},{2,3},{3,2},{4,5},{5,4},{6,7},{7,6},{8,9},{9,8},{10,11... | collective-permute-start | bytes 1179656 | tf_op jit(solution)/shard_map/ppermute | solution.py:157
  103.1 2.3 %collective-permute-done.22.handed_ref.refs_2_ = bf16[128,512]{1,0:T(8,128)(2,1)S(1)} collective-permute-done((bf16[128,512]{1,0:T(8,128)(2,1)S(1)}, bf16[128,512]{1,0:T(8,128)(2,1)S(1)}, u32[]{:S(2)}, u32[]{:S(2)}) %collective-permute-start.22) | collective-permute-done | bytes 131104 | tf_op jit(solution)/shard_map/ppermute | solution.py:157
  105.5 1.6 %collective-permute-start.23 = (bf16[128,256]{1,0:T(8,128)(2,1)S(1)}, bf16[128,256]{1,0:T(8,128)(2,1)S(1)}, u32[]{:S(2)}, u32[]{:S(2)}) collective-permute-start(bf16[128,256]{1,0:T(8,128)(2,1)S(1)} %shard_map.130.refs_0_), channel_id=1, source_target_pairs={{0,8},{4,12},{8,16},{12,20},{16,24},{20,28},{24,0},{28,4},{1,9},{5... | collective-permute-start | bytes 196616 | tf_op jit(solution)/shard_map/ppermute | solution.py:22
  107.0 3.7 %collective-permute-done.23.refs_1_.refs_3_ = bf16[128,256]{1,0:T(8,128)(2,1)S(1)} collective-permute-done((bf16[128,256]{1,0:T(8,128)(2,1)S(1)}, bf16[128,256]{1,0:T(8,128)(2,1)S(1)}, u32[]{:S(2)}, u32[]{:S(2)}) %collective-permute-start.23) | collective-permute-done | bytes 65568 | tf_op jit(solution)/shard_map/ppermute | solution.py:22
  110.7 1.5 %collective-permute-start.24 = (bf16[128,256]{1,0:T(8,128)(2,1)S(1)}, bf16[128,256]{1,0:T(8,128)(2,1)S(1)}, u32[]{:S(2)}, u32[]{:S(2)}) collective-permute-start(bf16[128,256]{1,0:T(8,128)(2,1)S(1)} %shard_map.130.refs_0_), channel_id=1, source_target_pairs={{0,16},{4,20},{8,24},{12,28},{16,0},{20,4},{24,8},{28,12},{1,17},{... | collective-permute-start | bytes 196616 | tf_op jit(solution)/shard_map/ppermute | solution.py:22
  112.2 2.3 %collective-permute-start.27 = (bf16[1536,128]{1,0:T(8,128)(2,1)S(1)}, bf16[1536,128]{1,0:T(8,128)(2,1)S(1)}, u32[]{:S(2)}, u32[]{:S(2)}) collective-permute-start(bf16[1536,128]{1,0:T(8,128)(2,1)S(1)} %collective-permute-done.17.refs_1_.refs_0_), channel_id=1, source_target_pairs={{0,2},{1,0},{2,3},{3,1},{4,6},{5,4},{6,7},{7,5},{8,10},{9,8},{10,1... | collective-permute-start | bytes 1179656 | tf_op jit(solution)/shard_map/ppermute | solution.py:157
  115.0 1.6 %collective-permute-start.25 = (bf16[128,256]{1,0:T(8,128)(2,1)S(1)}, bf16[128,256]{1,0:T(8,128)(2,1)S(1)}, u32[]{:S(2)}, u32[]{:S(2)}) collective-permute-start(bf16[128,256]{1,0:T(8,128)(2,1)S(1)} %shard_map.130.refs_0_), channel_id=1, source_target_pairs={{0,24},{4,28},{8,0},{12,4},{16,8},{20,12},{24,16},{28,20},{1,25},{... | collective-permute-start | bytes 196616 | tf_op jit(solution)/shard_map/ppermute | solution.py:22
  116.5 2.7 %collective-permute-done.25.refs_3_.refs_5_ = bf16[128,256]{1,0:T(8,128)(2,1)S(1)} collective-permute-done((bf16[128,256]{1,0:T(8,128)(2,1)S(1)}, bf16[128,256]{1,0:T(8,128)(2,1)S(1)}, u32[]{:S(2)}, u32[]{:S(2)}) %collective-permute-start.25) | collective-permute-done | bytes 65568 | tf_op jit(solution)/shard_map/ppermute | solution.py:22
  119.4 2.3 %collective-permute-start.28 = (bf16[1024,128]{1,0:T(8,128)(2,1)S(1)}, bf16[1024,128]{1,0:T(8,128)(2,1)S(1)}, u32[]{:S(2)}, u32[]{:S(2)}) collective-permute-start(bf16[1024,128]{1,0:T(8,128)(2,1)S(1)} %slice.10), channel_id=1, source_target_pairs={{0,2},{1,0},{2,3},{3,1},{4,6},{5,4},{6,7},{7,5},{8,10},{9,8},{10,1... | collective-permute-start | bytes 786440 | tf_op jit(solution)/shard_map/ppermute | solution.py:157
  121.7 3.0 %shard_map.126 = (f32[1536,256]{1,0:T(8,128)}, f32[1536,256]{1,0:T(8,128)S(1)}) custom-call(f32[1,1]{1,0:T(1,128)} %bitcast.9.low_ref, f32[1,1]{1,0:T(1,128)} %bitcast.14.high_ref, bf16[1536,1536]{1,0:T(8,128)(2,1)S(1)} %get-tuple-element.18.block_ref, bf16[1536,128]{1,0:T(8,128)(2,1)S(1)} %get-tuple-element.20.lead_ref, ...), custom_call_target="tpu_custom_call" | custom-call | flops 1207959552 | bytes 11796480 | tf_op jit(solution)/shard_map/pallas_call | solution.py:54
  124.8 2.4 %shard_map.127.rest_ref = f32[1536,256]{1,0:T(8,128)S(1)} custom-call(s32[1,2]{1,0:T(1,128)S(1)} %copy-done.6, bf16[1536,1536]{1,0:T(8,128)(2,1)S(1)} %shard_map.116.block_ref, f32[1536,256]{1,0:T(8,128)S(1)} %get-tuple-element.26.rest_ref, bf16[1536,128]{1,0:T(8,128)(2,1)S(1)} %collective-permute-done.16.refs_0_, ...), custom_call_target="tpu_custom_call" | custom-call | flops 1207959552 | bytes 8650752 | tf_op jit(solution)/shard_map/pallas_call | solution.py:54
  127.3 1.1 shard_map.132.coupled_ref
  128.4 3.0 %shard_map.133 = (f32[1536,256]{1,0:T(8,128)}, f32[1536,128]{1,0:T(8,128)S(1)}) custom-call(s32[1,2]{1,0:T(1,128)S(1)} %copy-done.6, bf16[1536,1536]{1,0:T(8,128)(2,1)S(1)} %shard_map.115.block_ref, f32[1536,256]{1,0:T(8,128)S(1)} %shard_map.127.rest_ref, bf16[1536,128]{1,0:T(8,128)(2,1)S(1)} %copy-done.1, bf16[128,256]{1,0:T(8,128)(2,1)S(1)} %shard_map.132.coupled_ref, ...), custom_call_target="tpu_custom_call" | custom-call | flops 603979776 | bytes 6684672 | tf_op jit(solution)/shard_map/pallas_call | solution.py:54
  131.3 1.9 %shard_map.134.trail_ref = f32[1536,128]{1,0:T(8,128)S(1)} custom-call(s32[1,2]{1,0:T(1,128)S(1)} %copy-done.6, bf16[1536,1536]{1,0:T(8,128)(2,1)S(1)} %shard_map.115.block_ref, f32[1536,128]{1,0:T(8,128)S(1)} %get-tuple-element.28.trail_ref, bf16[1536,128]{1,0:T(8,128)(2,1)S(1)} %collective-permute-done.19.refs_3_.inner_ref, ...), custom_call_target="tpu_custom_call" | custom-call | flops 402653184 | bytes 4718592 | tf_op jit(solution)/shard_map/pallas_call | solution.py:54
  133.2 1.9 %shard_map.135 = f32[1536,256]{1,0:T(8,128)} custom-call(s32[1,2]{1,0:T(1,128)S(1)} %copy-done.6, bf16[1536,1536]{1,0:T(8,128)(2,1)S(1)} %shard_map.115.block_ref, f32[1536,128]{1,0:T(8,128)S(1)} %shard_map.134.trail_ref, bf16[512,128]{1,0:T(8,128)(2,1)S(1)} %collective-permute-done.29.refs_0_, ...), custom_call_target="tpu_custom_call", output_to_operand_aliasing={{}: (4, {})} | custom-call | flops 603979776 | bytes 6684672 | tf_op jit(solution)/shard_map/pallas_call | solution.py:54
  (54 shorter events, 4.2 us)
Async XLA Ops:
  0.6 2.2 %copy-start = (f32[1536,256]{1,0:T(8,128)S(1)}, f32[1536,256]{1,0:T(8,128)}, u32[]{:S(2)}) copy-start(f32[1536,256]{1,0:T(8,128)} %param.11) | copy-start | bytes 4718596
  6.5 1.0 copy-start.1
  6.5 1.0 copy-start.5
  6.5 8.7 %copy-start.2 = (bf16[1536,128]{1,0:T(8,128)(2,1)S(1)}, bf16[1536,128]{1,0:T(8,128)(2,1)}, u32[]{:S(2)}) copy-start(bf16[1536,128]{1,0:T(8,128)(2,1)} %points_ref.5) | copy-start | bytes 1179652
  7.9 5.9 %collective-permute-start.7 = (bf16[128,384]{1,0:T(8,128)(2,1)S(1)}, bf16[128,384]{1,0:T(8,128)(2,1)S(1)}, u32[]{:S(2)}, u32[]{:S(2)}) collective-permute-start(bf16[128,384]{1,0:T(8,128)(2,1)S(1)} %shard_map.118.refs_0_), channel_id=1, source_target_pairs={{0,1},{1,0},{2,3},{3,2},{4,5},{5,4},{6,7},{7,6},{8,9},{9,8},{10,11... | collective-permute-start | bytes 294920 | tf_op jit(solution)/shard_map/ppermute | solution.py:157
  13.8 2.1 %collective-permute-start.8 = (bf16[256,384]{1,0:T(8,128)(2,1)S(1)}, bf16[256,384]{1,0:T(8,128)(2,1)S(1)}, u32[]{:S(2)}, u32[]{:S(2)}) collective-permute-start(bf16[256,384]{1,0:T(8,128)(2,1)S(1)} %shard_map.119.pair_ref.first_pair_ref.refs_0_), channel_id=1, source_target_pairs={{0,0},{1,2},{2,1},{3,3},{4,4},{5,6},{6,5},{7,7},{8,8},{9,10},{10,9... | collective-permute-start | bytes 589832 | tf_op jit(solution)/shard_map/ppermute | solution.py:157
  14.5 17.2 %collective-permute-start.4 = (bf16[1536,128]{1,0:T(8,128)(2,1)S(1)}, bf16[1536,128]{1,0:T(8,128)(2,1)S(1)}, u32[]{:S(2)}, u32[]{:S(2)}) collective-permute-start(bf16[1536,128]{1,0:T(8,128)(2,1)S(1)} %get-tuple-element.16.lead_ref), channel_id=1, source_target_pairs={{0,0},{1,2},{2,1},{3,3},{4,4},{5,6},{6,5},{7,7},{8,8},{9,10},{10,9... | collective-permute-start | bytes 1179656 | tf_op jit(solution)/shard_map/ppermute | solution.py:157
  15.2 18.1 %collective-permute-start = (bf16[1536,128]{1,0:T(8,128)(2,1)S(1)}, bf16[1536,128]{1,0:T(8,128)(2,1)S(1)}, u32[]{:S(2)}, u32[]{:S(2)}) collective-permute-start(bf16[1536,128]{1,0:T(8,128)(2,1)S(1)} %copy-done.2), channel_id=1, source_target_pairs={{0,0},{1,2},{2,1},{3,3},{4,4},{5,6},{6,5},{7,7},{8,8},{9,10},{10,9... | collective-permute-start | bytes 1179656 | tf_op jit(solution)/shard_map/ppermute | solution.py:157
  16.2 13.5 %collective-permute-start.9 = (bf16[128,512]{1,0:T(8,128)(2,1)S(1)}, bf16[128,512]{1,0:T(8,128)(2,1)S(1)}, u32[]{:S(2)}, u32[]{:S(2)}) collective-permute-start(bf16[128,512]{1,0:T(8,128)(2,1)S(1)} %shard_map.120.summed_ref), channel_id=1, source_target_pairs={{0,1},{1,0},{2,3},{3,2},{4,5},{5,4},{6,7},{7,6},{8,9},{9,8},{10,11... | collective-permute-start | bytes 393224 | tf_op jit(solution)/shard_map/ppermute | solution.py:157
  25.4 26.5 %collective-permute-start.6 = (bf16[1536,128]{1,0:T(8,128)(2,1)S(1)}, bf16[1536,128]{1,0:T(8,128)(2,1)S(1)}, u32[]{:S(2)}, u32[]{:S(2)}) collective-permute-start(bf16[1536,128]{1,0:T(8,128)(2,1)S(1)} %get-tuple-element.17.trail_ref), channel_id=1, source_target_pairs={{0,0},{1,2},{2,1},{3,3},{4,4},{5,6},{6,5},{7,7},{8,8},{9,10},{10,9... | collective-permute-start | bytes 1179656 | tf_op jit(solution)/shard_map/ppermute | solution.py:157
  26.0 25.9 %collective-permute-start.3 = (bf16[1536,128]{1,0:T(8,128)(2,1)S(1)}, bf16[1536,128]{1,0:T(8,128)(2,1)S(1)}, u32[]{:S(2)}, u32[]{:S(2)}) collective-permute-start(bf16[1536,128]{1,0:T(8,128)(2,1)S(1)} %get-tuple-element.16.lead_ref), channel_id=1, source_target_pairs={{0,1},{1,0},{2,3},{3,2},{4,5},{5,4},{6,7},{7,6},{8,9},{9,8},{10,11... | collective-permute-start | bytes 1179656 | tf_op jit(solution)/shard_map/ppermute | solution.py:157
  29.7 23.4 %collective-permute-start.2 = (bf16[1536,128]{1,0:T(8,128)(2,1)S(1)}, bf16[1536,128]{1,0:T(8,128)(2,1)S(1)}, u32[]{:S(2)}, u32[]{:S(2)}) collective-permute-start(bf16[1536,128]{1,0:T(8,128)(2,1)S(1)} %copy-done.2), channel_id=1, source_target_pairs={{0,1},{1,0},{2,3},{3,2},{4,5},{5,4},{6,7},{7,6},{8,9},{9,8},{10,11... | collective-permute-start | bytes 1179656 | tf_op jit(solution)/shard_map/ppermute | solution.py:157
  31.8 5.2 %collective-permute-start.10 = (bf16[128,256]{1,0:T(8,128)(2,1)S(1)}, bf16[128,256]{1,0:T(8,128)(2,1)S(1)}, u32[]{:S(2)}, u32[]{:S(2)}) collective-permute-start(bf16[128,256]{1,0:T(8,128)(2,1)S(1)} %shard_map.121.refs_0_), channel_id=1, source_target_pairs={{0,8},{4,12},{8,16},{12,20},{16,24},{20,28},{24,0},{28,4},{1,9},{5... | collective-permute-start | bytes 196616 | tf_op jit(solution)/shard_map/ppermute | solution.py:22
  33.3 9.7 %collective-permute-start.11 = (bf16[128,256]{1,0:T(8,128)(2,1)S(1)}, bf16[128,256]{1,0:T(8,128)(2,1)S(1)}, u32[]{:S(2)}, u32[]{:S(2)}) collective-permute-start(bf16[128,256]{1,0:T(8,128)(2,1)S(1)} %shard_map.121.refs_0_), channel_id=1, source_target_pairs={{0,16},{4,20},{8,24},{12,28},{16,0},{20,4},{24,8},{28,12},{1,17},{... | collective-permute-start | bytes 196616 | tf_op jit(solution)/shard_map/ppermute | solution.py:22
  37.0 23.6 %collective-permute-start.5 = (bf16[1536,128]{1,0:T(8,128)(2,1)S(1)}, bf16[1536,128]{1,0:T(8,128)(2,1)S(1)}, u32[]{:S(2)}, u32[]{:S(2)}) collective-permute-start(bf16[1536,128]{1,0:T(8,128)(2,1)S(1)} %get-tuple-element.17.trail_ref), channel_id=1, source_target_pairs={{0,1},{1,0},{2,3},{3,2},{4,5},{5,4},{6,7},{7,6},{8,9},{9,8},{10,11... | collective-permute-start | bytes 1179656 | tf_op jit(solution)/shard_map/ppermute | solution.py:157
  43.0 4.3 %collective-permute-start.12 = (bf16[128,256]{1,0:T(8,128)(2,1)S(1)}, bf16[128,256]{1,0:T(8,128)(2,1)S(1)}, u32[]{:S(2)}, u32[]{:S(2)}) collective-permute-start(bf16[128,256]{1,0:T(8,128)(2,1)S(1)} %shard_map.121.refs_0_), channel_id=1, source_target_pairs={{0,24},{4,28},{8,0},{12,4},{16,8},{20,12},{24,16},{28,20},{1,25},{... | collective-permute-start | bytes 196616 | tf_op jit(solution)/shard_map/ppermute | solution.py:22
  47.3 17.2 %collective-permute-start.1 = (bf16[1536,128]{1,0:T(8,128)(2,1)S(1)}, bf16[1536,128]{1,0:T(8,128)(2,1)S(1)}, u32[]{:S(2)}, u32[]{:S(2)}) collective-permute-start(bf16[1536,128]{1,0:T(8,128)(2,1)S(1)} %collective-permute-done.rest_0_.rest_1_), channel_id=1, source_target_pairs={{0,2},{1,0},{2,3},{3,1},{4,6},{5,4},{6,7},{7,5},{8,10},{9,8},{10,1... | collective-permute-start | bytes 1179656 | tf_op jit(solution)/shard_map/ppermute | solution.py:157
  51.8 21.1 %collective-permute-start.14 = (bf16[1536,128]{1,0:T(8,128)(2,1)S(1)}, bf16[1536,128]{1,0:T(8,128)(2,1)S(1)}, u32[]{:S(2)}, u32[]{:S(2)}) collective-permute-start(bf16[1536,128]{1,0:T(8,128)(2,1)S(1)} %collective-permute-done.4.refs_1_.refs_0_), channel_id=1, source_target_pairs={{0,2},{1,0},{2,3},{3,1},{4,6},{5,4},{6,7},{7,5},{8,10},{9,8},{10,1... | collective-permute-start | bytes 1179656 | tf_op jit(solution)/shard_map/ppermute | solution.py:157
  51.9 26.3 %collective-permute-start.15 = (bf16[1536,128]{1,0:T(8,128)(2,1)S(1)}, bf16[1536,128]{1,0:T(8,128)(2,1)S(1)}, u32[]{:S(2)}, u32[]{:S(2)}) collective-permute-start(bf16[1536,128]{1,0:T(8,128)(2,1)S(1)} %collective-permute-done.6.refs_3_.refs_0_), channel_id=1, source_target_pairs={{0,2},{1,0},{2,3},{3,1},{4,6},{5,4},{6,7},{7,5},{8,10},{9,8},{10,1... | collective-permute-start | bytes 1179656 | tf_op jit(solution)/shard_map/ppermute | solution.py:157
  53.1 9.9 %collective-permute-start.13 = (bf16[512,256]{1,0:T(8,128)(2,1)S(1)}, bf16[512,256]{1,0:T(8,128)(2,1)S(1)}, u32[]{:S(2)}, u32[]{:S(2)}) collective-permute-start(bf16[512,256]{1,0:T(8,128)(2,1)S(1)} %shard_map.122), channel_id=1, source_target_pairs={{0,4},{4,0},{8,12},{12,8},{16,20},{20,16},{24,28},{28,24},{1,5},{5... | collective-permute-start | bytes 786440 | tf_op jit(solution)/shard_map/ppermute | solution.py:600
  53.1 4.2 %copy-start.6 = (s32[1,2]{1,0:T(1,128)S(1)}, s32[1,2]{1,0:T(1,128)}, u32[]{:S(2)}) copy-start(s32[1,2]{1,0:T(1,128)} %near_ref.21) | copy-start | bytes 28
  60.6 2.5 %copy-start.3 = (bf16[1,8,128,128]{3,2,1,0:T(8,128)(2,1)S(1)}, bf16[1,8,128,128]{3,2,1,0:T(8,128)(2,1)}, u32[]{:S(2)}) copy-start(bf16[1,8,128,128]{3,2,1,0:T(8,128)(2,1)} %param.17) | copy-start | bytes 786436
  60.6 2.5 %copy-start.4 = (bf16[1,4,128,128]{3,2,1,0:T(8,128)(2,1)S(1)}, bf16[1,4,128,128]{3,2,1,0:T(8,128)(2,1)}, u32[]{:S(2)}) copy-start(bf16[1,4,128,128]{3,2,1,0:T(8,128)(2,1)} %param.15) | copy-start | bytes 393220
  81.3 5.0 %collective-permute-start.20 = (bf16[128,256]{1,0:T(8,128)(2,1)S(1)}, bf16[128,256]{1,0:T(8,128)(2,1)S(1)}, u32[]{:S(2)}, u32[]{:S(2)}) collective-permute-start(bf16[128,256]{1,0:T(8,128)(2,1)S(1)} %get-tuple-element.27.refs_0_), channel_id=1, source_target_pairs={{0,1},{1,0},{2,3},{3,2},{4,5},{5,4},{6,7},{7,6},{8,9},{9,8},{10,11... | collective-permute-start | bytes 196616 | tf_op jit(solution)/shard_map/ppermute | solution.py:157
  84.1 28.2 %collective-permute-start.17 = (bf16[1536,128]{1,0:T(8,128)(2,1)S(1)}, bf16[1536,128]{1,0:T(8,128)(2,1)S(1)}, u32[]{:S(2)}, u32[]{:S(2)}) collective-permute-start(bf16[1536,128]{1,0:T(8,128)(2,1)S(1)} %get-tuple-element.20.lead_ref), channel_id=1, source_target_pairs={{0,0},{1,2},{2,1},{3,3},{4,4},{5,6},{6,5},{7,7},{8,8},{9,10},{10,9... | collective-permute-start | bytes 1179656 | tf_op jit(solution)/shard_map/ppermute | solution.py:157
  86.3 1.6 %collective-permute-start.21 = (bf16[256,256]{1,0:T(8,128)(2,1)S(1)}, bf16[256,256]{1,0:T(8,128)(2,1)S(1)}, u32[]{:S(2)}, u32[]{:S(2)}) collective-permute-start(bf16[256,256]{1,0:T(8,128)(2,1)S(1)} %shard_map.128.pair_ref.refs_0_), channel_id=1, source_target_pairs={{0,0},{1,2},{2,1},{3,3},{4,4},{5,6},{6,5},{7,7},{8,8},{9,10},{10,9... | collective-permute-start | bytes 393224 | tf_op jit(solution)/shard_map/ppermute | solution.py:157
  87.0 32.3 %collective-permute-start.19 = (bf16[1536,128]{1,0:T(8,128)(2,1)S(1)}, bf16[1536,128]{1,0:T(8,128)(2,1)S(1)}, u32[]{:S(2)}, u32[]{:S(2)}) collective-permute-start(bf16[1536,128]{1,0:T(8,128)(2,1)S(1)} %get-tuple-element.22.trail_ref), channel_id=1, source_target_pairs={{0,0},{1,2},{2,1},{3,3},{4,4},{5,6},{6,5},{7,7},{8,8},{9,10},{10,9... | collective-permute-start | bytes 1179656 | tf_op jit(solution)/shard_map/ppermute | solution.py:157
  88.2 17.3 %collective-permute-start.22 = (bf16[128,512]{1,0:T(8,128)(2,1)S(1)}, bf16[128,512]{1,0:T(8,128)(2,1)S(1)}, u32[]{:S(2)}, u32[]{:S(2)}) collective-permute-start(bf16[128,512]{1,0:T(8,128)(2,1)S(1)} %shard_map.129.summed_ref), channel_id=1, source_target_pairs={{0,1},{1,0},{2,3},{3,2},{4,5},{5,4},{6,7},{7,6},{8,9},{9,8},{10,11... | collective-permute-start | bytes 393224 | tf_op jit(solution)/shard_map/ppermute | solution.py:157
  101.1 23.6 %collective-permute-start.18 = (bf16[1536,128]{1,0:T(8,128)(2,1)S(1)}, bf16[1536,128]{1,0:T(8,128)(2,1)S(1)}, u32[]{:S(2)}, u32[]{:S(2)}) collective-permute-start(bf16[1536,128]{1,0:T(8,128)(2,1)S(1)} %get-tuple-element.22.trail_ref), channel_id=1, source_target_pairs={{0,1},{1,0},{2,3},{3,2},{4,5},{5,4},{6,7},{7,6},{8,9},{9,8},{10,11... | collective-permute-start | bytes 1179656 | tf_op jit(solution)/shard_map/ppermute | solution.py:157
  101.2 23.6 %collective-permute-start.16 = (bf16[1536,128]{1,0:T(8,128)(2,1)S(1)}, bf16[1536,128]{1,0:T(8,128)(2,1)S(1)}, u32[]{:S(2)}, u32[]{:S(2)}) collective-permute-start(bf16[1536,128]{1,0:T(8,128)(2,1)S(1)} %get-tuple-element.20.lead_ref), channel_id=1, source_target_pairs={{0,1},{1,0},{2,3},{3,2},{4,5},{5,4},{6,7},{7,6},{8,9},{9,8},{10,11... | collective-permute-start | bytes 1179656 | tf_op jit(solution)/shard_map/ppermute | solution.py:157
  105.5 5.2 %collective-permute-start.23 = (bf16[128,256]{1,0:T(8,128)(2,1)S(1)}, bf16[128,256]{1,0:T(8,128)(2,1)S(1)}, u32[]{:S(2)}, u32[]{:S(2)}) collective-permute-start(bf16[128,256]{1,0:T(8,128)(2,1)S(1)} %shard_map.130.refs_0_), channel_id=1, source_target_pairs={{0,8},{4,12},{8,16},{12,20},{16,24},{20,28},{24,0},{28,4},{1,9},{5... | collective-permute-start | bytes 196616 | tf_op jit(solution)/shard_map/ppermute | solution.py:22
  110.7 4.3 %collective-permute-start.24 = (bf16[128,256]{1,0:T(8,128)(2,1)S(1)}, bf16[128,256]{1,0:T(8,128)(2,1)S(1)}, u32[]{:S(2)}, u32[]{:S(2)}) collective-permute-start(bf16[128,256]{1,0:T(8,128)(2,1)S(1)} %shard_map.130.refs_0_), channel_id=1, source_target_pairs={{0,16},{4,20},{8,24},{12,28},{16,0},{20,4},{24,8},{28,12},{1,17},{... | collective-permute-start | bytes 196616 | tf_op jit(solution)/shard_map/ppermute | solution.py:22
  112.2 16.1 %collective-permute-start.27 = (bf16[1536,128]{1,0:T(8,128)(2,1)S(1)}, bf16[1536,128]{1,0:T(8,128)(2,1)S(1)}, u32[]{:S(2)}, u32[]{:S(2)}) collective-permute-start(bf16[1536,128]{1,0:T(8,128)(2,1)S(1)} %collective-permute-done.17.refs_1_.refs_0_), channel_id=1, source_target_pairs={{0,2},{1,0},{2,3},{3,1},{4,6},{5,4},{6,7},{7,5},{8,10},{9,8},{10,1... | collective-permute-start | bytes 1179656 | tf_op jit(solution)/shard_map/ppermute | solution.py:157
  115.0 4.3 %collective-permute-start.25 = (bf16[128,256]{1,0:T(8,128)(2,1)S(1)}, bf16[128,256]{1,0:T(8,128)(2,1)S(1)}, u32[]{:S(2)}, u32[]{:S(2)}) collective-permute-start(bf16[128,256]{1,0:T(8,128)(2,1)S(1)} %shard_map.130.refs_0_), channel_id=1, source_target_pairs={{0,24},{4,28},{8,0},{12,4},{16,8},{20,12},{24,16},{28,20},{1,25},{... | collective-permute-start | bytes 196616 | tf_op jit(solution)/shard_map/ppermute | solution.py:22
  119.2 8.0 %collective-permute-start.26 = (bf16[512,256]{1,0:T(8,128)(2,1)S(1)}, bf16[512,256]{1,0:T(8,128)(2,1)S(1)}, u32[]{:S(2)}, u32[]{:S(2)}) collective-permute-start(bf16[512,256]{1,0:T(8,128)(2,1)S(1)} %shard_map.131), channel_id=1, source_target_pairs={{0,4},{4,0},{8,12},{12,8},{16,20},{20,16},{24,28},{28,24},{1,5},{5... | collective-permute-start | bytes 786440 | tf_op jit(solution)/shard_map/ppermute | solution.py:600
  119.4 12.0 %collective-permute-start.28 = (bf16[1024,128]{1,0:T(8,128)(2,1)S(1)}, bf16[1024,128]{1,0:T(8,128)(2,1)S(1)}, u32[]{:S(2)}, u32[]{:S(2)}) collective-permute-start(bf16[1024,128]{1,0:T(8,128)(2,1)S(1)} %slice.10), channel_id=1, source_target_pairs={{0,2},{1,0},{2,3},{3,1},{4,6},{5,4},{6,7},{7,5},{8,10},{9,8},{10,1... | collective-permute-start | bytes 786440 | tf_op jit(solution)/shard_map/ppermute | solution.py:157
  124.7 8.5 %collective-permute-start.29 = (bf16[512,128]{1,0:T(8,128)(2,1)S(1)}, bf16[512,128]{1,0:T(8,128)(2,1)S(1)}, u32[]{:S(2)}, u32[]{:S(2)}) collective-permute-start(bf16[512,128]{1,0:T(8,128)(2,1)S(1)} %slice.11), channel_id=1, source_target_pairs={{0,2},{1,0},{2,3},{3,1},{4,6},{5,4},{6,7},{7,5},{8,10},{9,8},{10,1... | collective-permute-start | bytes 393224 | tf_op jit(solution)/shard_map/ppermute | solution.py:157

commit v4 on v3

--- a/solution.py
+++ b/solution.py
@@ -194,23 +194,48 @@
     return theta, rho_one * rho_zero, 2.0 * rho_one / delta
 
 
-def start_rows(ordered, low, high):
-    rows, width = ordered.shape
+def start_rows(right_sides, order, low, high):
+    rows, width = right_sides.shape
     half = width // 2
-
-    def body(low_ref, high_ref, ordered_ref, lead_ref, trail_ref):
+    step = tile_of(rows)
+
+    def body(low_ref, high_ref, right_ref, order_ref, lead_ref, trail_ref, turned):
         theta, _, _ = factors(low_ref, high_ref, width)
-
-        def tile(at):
-            v = (ordered_ref[at, :] / theta).astype(BF16)
+        turned[...] = (right_ref[...] / theta).astype(BF16).T
+
+        for k in range(rows // step):
+            at = pl.ds(k * step, step)
+            source = lax.broadcasted_iota(jnp.int32, (rows, step), 0)
+            places = jnp.where(source == order_ref[:, at], 1.0, 0.0).astype(BF16)
+            v = dot(turned[...], places).T.astype(BF16)
             lead_ref[at, :] = v[:, :half]
             trail_ref[at, :] = v[:, half:]
 
-        over_tiles(rows, tile)
-
-    return call(
-        body, (shape(BF16, rows, half), shape(BF16, rows, width - half)), (low, high, ordered),
-        flops=rows * width, bytes_=rows * width * 6,
+    return call(
+        body, (shape(BF16, rows, half), shape(BF16, rows, width - half)), (low, high, right_sides, order),
+        scratch=[VMEM((width, rows), BF16)],
+        flops=2 * rows * rows * width, bytes_=rows * width * 6,
+    )
+
+
+def order_rows(right_sides, order):
+    rows, width = right_sides.shape
+    step = tile_of(rows)
+
+    def body(right_ref, order_ref, out_ref, turned):
+        for k, piece in enumerate(pieces(right_ref[...])):
+            turned[k * width : (k + 1) * width, :] = piece.astype(BF16).T
+
+        for k in range(rows // step):
+            at = pl.ds(k * step, step)
+            source = lax.broadcasted_iota(jnp.int32, (rows, step), 0)
+            places = jnp.where(source == order_ref[:, at], 1.0, 0.0).astype(BF16)
+            v = dot(turned[...], places)
+            out_ref[at, :] = (v[:width] + v[width : 2 * width] + v[2 * width :]).T
+
+    return call(
+        body, shape(F32, rows, width), (right_sides, order), scratch=[VMEM((3 * width, rows), BF16)],
+        flops=6 * rows * rows * width, bytes_=rows * width * 8,
     )
 
 
@@ -644,14 +669,6 @@
     return moved
 
 
-def take_rows(rows, order):
-    dims = lax.GatherDimensionNumbers(offset_dims=(1,), collapsed_slice_dims=(0,), start_index_map=(0,))
-    return lax.gather(
-        rows, order[:, None], dims, (1, rows.shape[1]), unique_indices=True,
-        mode=lax.GatherScatterMode.PROMISE_IN_BOUNDS,
-    )
-
-
 def shards(
     points,
     right_sides,
@@ -682,8 +699,8 @@
     points_a, points_b = moved(points)
     block_a = near_block(0, near, points, points_a)
     block_b = near_block(1, near, points, points_b)
-    ordered = take_rows(right_sides, leaf_order[0])
-    lead, trail = start_rows(ordered, low, high)
+    lead, trail = start_rows(right_sides, leaf_order, low, high)
+    ordered = order_rows(right_sides, leaf_order)
     message = start_message(lead, trail, bases, transfer)
     rank = transfer.shape[0]
     messages, merged = merge_all(message, None, rank)

time: 136 us -> 145 us (1.066)
  waiting for transfers between devices: 26.8 us -> 34.1 us
  Pallas kernels: 34.8 us -> 40.4 us
  local copies, waits for them, and re-layouts: 4.5 us -> 2.15 us
    ppermute x22, waiting for transfers between devices: 15 us -> 27.7 us  [permute(): return lax.ppermute(block, 'member', pairs)]
    pallas_call x23 -> x24, Pallas kernels: 34.8 us -> 40.4 us  [call(): pl.pallas_call(body, out_shape=out, in_specs=in_specs or [SMEM_SPEC] * sc...]
    ppermute x6, waiting for transfers between devices: 11.8 us -> 6.48 us  [cycle(): lax.ppermute(array, axis, [(i, (i + by) % count) for i in range(count)])]
    gather x1 -> x0, local copies, waits for them, and re-layouts: 3.66 us -> none  [take_rows(): lax.gather(rows, order[:, None], dims, (1, rows.shape[1]), unique_indices...]
  transfers between devices with their start and end apart: 30 -> 30, of which waited for: 12 -> 13; matrix products, arithmetic and copies ran while one was open for 0% -> 0% of each run, Pallas kernels for 22% -> 23%
where the time goes in v4:
time: 145 us
  starting transfers between devices  65.8 us (45%)
  Pallas kernels  40.4 us (28%)
  waiting for transfers between devices  34.1 us (24%)
  between operations  2.49 us (2%)
  local copies, waits for them, and re-layouts  2.15 us (1%)
    ppermute x22, starting transfers between devices, permute(): return lax.ppermute(block, 'member', pairs)  56.6 us
    pallas_call x24, Pallas kernels, call(): pl.pallas_call(body, out_shape=out, in_specs=in_specs or [SMEM_SPEC] * sc...  40.4 us
    ppermute x22, waiting for transfers between devices, permute(): return lax.ppermute(block, 'member', pairs)  27.7 us
    ppermute x6, starting transfers between devices, cycle(): lax.ppermute(array, axis, [(i, (i + by) % count) for i in range(count)])  9.1 us
    ppermute x6, waiting for transfers between devices, cycle(): lax.ppermute(array, axis, [(i, (i + by) % count) for i in range(count)])  6.48 us
  transfers between devices with their start and end apart: 30, of which 13 were waited for; matrix products, arithmetic and copies ran while one was open for 0% of the time, Pallas kernels for 23%

profile of v4, /device:TPU:0, one launch (start us, length us, event | category | flops | bytes accessed | tf_op | source)
XLA Modules:
  0.0 145.0 jit_solution(13255785835514656162)
XLA Ops:
  1.9 1.4 copy-done.6
  3.3 0.7 copy-done.8
  4.0 1.6 %shard_map.114 = (bf16[1536,128]{1,0:T(8,128)(2,1)S(1)}, bf16[1536,128]{1,0:T(8,128)(2,1)S(1)}) custom-call(f32[1,1]{1,0:T(1,128)} %bitcast.5.low_ref, f32[1,1]{1,0:T(1,128)} %bitcast.10.high_ref, f32[1536,256]{1,0:T(8,128)S(1)} %copy-done.6, s32[1,1536]{1,0:T(1,128)S(1)} %copy-done.8), custom_call_target="tpu_custom_call" | custom-call | flops 1207959552 | bytes 2359296 | tf_op jit(solution)/shard_map/pallas_call | solution.py:54
  6.2 3.1 %collective-permute-start.7 = (bf16[128,384]{1,0:T(8,128)(2,1)S(1)}, bf16[128,384]{1,0:T(8,128)(2,1)S(1)}, u32[]{:S(2)}, u32[]{:S(2)}) collective-permute-start(bf16[128,384]{1,0:T(8,128)(2,1)S(1)} %shard_map.119.refs_0_), channel_id=1, source_target_pairs={{0,1},{1,0},{2,3},{3,2},{4,5},{5,4},{6,7},{7,6},{8,9},{9,8},{10,11... | collective-permute-start | bytes 294920 | tf_op jit(solution)/shard_map/ppermute | solution.py:157
  9.3 2.8 %collective-permute-done.7.refs_1_ = bf16[128,384]{1,0:T(8,128)(2,1)S(1)} collective-permute-done((bf16[128,384]{1,0:T(8,128)(2,1)S(1)}, bf16[128,384]{1,0:T(8,128)(2,1)S(1)}, u32[]{:S(2)}, u32[]{:S(2)}) %collective-permute-start.7) | collective-permute-done | bytes 98336 | tf_op jit(solution)/shard_map/ppermute | solution.py:157
  12.8 0.7 collective-permute-start.4
  13.5 0.7 collective-permute-start
  14.4 9.2 %collective-permute-start.9 = (bf16[128,512]{1,0:T(8,128)(2,1)S(1)}, bf16[128,512]{1,0:T(8,128)(2,1)S(1)}, u32[]{:S(2)}, u32[]{:S(2)}) collective-permute-start(bf16[128,512]{1,0:T(8,128)(2,1)S(1)} %shard_map.121.summed_ref), channel_id=1, source_target_pairs={{0,1},{1,0},{2,3},{3,2},{4,5},{5,4},{6,7},{7,6},{8,9},{9,8},{10,11... | collective-permute-start | bytes 393224 | tf_op jit(solution)/shard_map/ppermute | solution.py:157
  23.6 2.9 %collective-permute-done.9.handed_ref.refs_2_ = bf16[128,512]{1,0:T(8,128)(2,1)S(1)} collective-permute-done((bf16[128,512]{1,0:T(8,128)(2,1)S(1)}, bf16[128,512]{1,0:T(8,128)(2,1)S(1)}, u32[]{:S(2)}, u32[]{:S(2)}) %collective-permute-start.9) | collective-permute-done | bytes 131104 | tf_op jit(solution)/shard_map/ppermute | solution.py:157
  26.6 1.5 %collective-permute-start.10 = (bf16[128,256]{1,0:T(8,128)(2,1)S(1)}, bf16[128,256]{1,0:T(8,128)(2,1)S(1)}, u32[]{:S(2)}, u32[]{:S(2)}) collective-permute-start(bf16[128,256]{1,0:T(8,128)(2,1)S(1)} %shard_map.122.refs_0_), channel_id=1, source_target_pairs={{0,8},{4,12},{8,16},{12,20},{16,24},{20,28},{24,0},{28,4},{1,9},{5... | collective-permute-start | bytes 196616 | tf_op jit(solution)/shard_map/ppermute | solution.py:22
  28.1 1.5 %collective-permute-start.11 = (bf16[128,256]{1,0:T(8,128)(2,1)S(1)}, bf16[128,256]{1,0:T(8,128)(2,1)S(1)}, u32[]{:S(2)}, u32[]{:S(2)}) collective-permute-start(bf16[128,256]{1,0:T(8,128)(2,1)S(1)} %shard_map.122.refs_0_), channel_id=1, source_target_pairs={{0,16},{4,20},{8,24},{12,28},{16,0},{20,4},{24,8},{28,12},{1,17},{... | collective-permute-start | bytes 196616 | tf_op jit(solution)/shard_map/ppermute | solution.py:22
  29.7 1.4 collective-permute-start.12
  31.8 7.9 %collective-permute-start.3 = (bf16[1536,128]{1,0:T(8,128)(2,1)S(1)}, bf16[1536,128]{1,0:T(8,128)(2,1)S(1)}, u32[]{:S(2)}, u32[]{:S(2)}) collective-permute-start(bf16[1536,128]{1,0:T(8,128)(2,1)S(1)} %get-tuple-element.16.lead_ref), channel_id=1, source_target_pairs={{0,1},{1,0},{2,3},{3,2},{4,5},{5,4},{6,7},{7,6},{8,9},{9,8},{10,11... | collective-permute-start | bytes 1179656 | tf_op jit(solution)/shard_map/ppermute | solution.py:157
  39.7 2.0 %collective-permute-start.5 = (bf16[1536,128]{1,0:T(8,128)(2,1)S(1)}, bf16[1536,128]{1,0:T(8,128)(2,1)S(1)}, u32[]{:S(2)}, u32[]{:S(2)}) collective-permute-start(bf16[1536,128]{1,0:T(8,128)(2,1)S(1)} %get-tuple-element.17.trail_ref), channel_id=1, source_target_pairs={{0,1},{1,0},{2,3},{3,2},{4,5},{5,4},{6,7},{7,6},{8,9},{9,8},{10,11... | collective-permute-start | bytes 1179656 | tf_op jit(solution)/shard_map/ppermute | solution.py:157
  41.8 1.8 %collective-permute-start.1 = (bf16[1536,128]{1,0:T(8,128)(2,1)S(1)}, bf16[1536,128]{1,0:T(8,128)(2,1)S(1)}, u32[]{:S(2)}, u32[]{:S(2)}) collective-permute-start(bf16[1536,128]{1,0:T(8,128)(2,1)S(1)} %collective-permute-done.rest_0_.rest_1_), channel_id=1, source_target_pairs={{0,2},{1,0},{2,3},{3,1},{4,6},{5,4},{6,7},{7,5},{8,10},{9,8},{10,1... | collective-permute-start | bytes 1179656 | tf_op jit(solution)/shard_map/ppermute | solution.py:157
  43.6 4.0 %shard_map.113.ordered_ref = f32[1536,256]{1,0:T(8,128)S(1)} custom-call(f32[1536,256]{1,0:T(8,128)S(1)} %copy-done.7, s32[1,1536]{1,0:T(1,128)S(1)} %copy-done.8), custom_call_target="tpu_custom_call" | custom-call | flops 3623878656 | bytes 3145728 | tf_op jit(solution)/shard_map/pallas_call | solution.py:54
  47.6 2.0 %collective-permute-start.14 = (bf16[1536,128]{1,0:T(8,128)(2,1)S(1)}, bf16[1536,128]{1,0:T(8,128)(2,1)S(1)}, u32[]{:S(2)}, u32[]{:S(2)}) collective-permute-start(bf16[1536,128]{1,0:T(8,128)(2,1)S(1)} %collective-permute-done.4.refs_1_.refs_0_), channel_id=1, source_target_pairs={{0,2},{1,0},{2,3},{3,1},{4,6},{5,4},{6,7},{7,5},{8,10},{9,8},{10,1... | collective-permute-start | bytes 1179656 | tf_op jit(solution)/shard_map/ppermute | solution.py:157
  49.7 3.8 %collective-permute-start.15 = (bf16[1536,128]{1,0:T(8,128)(2,1)S(1)}, bf16[1536,128]{1,0:T(8,128)(2,1)S(1)}, u32[]{:S(2)}, u32[]{:S(2)}) collective-permute-start(bf16[1536,128]{1,0:T(8,128)(2,1)S(1)} %collective-permute-done.6.refs_3_.refs_0_), channel_id=1, source_target_pairs={{0,2},{1,0},{2,3},{3,1},{4,6},{5,4},{6,7},{7,5},{8,10},{9,8},{10,1... | collective-permute-start | bytes 1179656 | tf_op jit(solution)/shard_map/ppermute | solution.py:157
  53.4 4.7 %collective-permute-done.2.rest_0_ = bf16[1536,128]{1,0:T(8,128)(2,1)S(1)} collective-permute-done((bf16[1536,128]{1,0:T(8,128)(2,1)S(1)}, bf16[1536,128]{1,0:T(8,128)(2,1)S(1)}, u32[]{:S(2)}, u32[]{:S(2)}) %collective-permute-start.2) | collective-permute-done | bytes 393248 | tf_op jit(solution)/shard_map/ppermute | solution.py:157
  58.1 4.2 %shard_map.115 = (bf16[1536,1536]{1,0:T(8,128)(2,1)S(1)}, f32[1536,256]{1,0:T(8,128)S(1)}) custom-call(f32[1,1]{1,0:T(1,128)} %bitcast.6.low_ref, f32[1,1]{1,0:T(1,128)} %bitcast.11.high_ref, bf16[1536,128]{1,0:T(8,128)(2,1)S(1)} %copy-done.1, f32[1536,256]{1,0:T(8,128)S(1)} %shard_map.113.ordered_ref, bf16[1536,128]{1,0:T(8,128)(2,1)S(1)} %get-tuple-element.16.lead_ref, ...), custom_call_target="tpu_custom_call" | custom-call | flops 1811939328 | bytes 8650752 | tf_op jit(solution)/shard_map/pallas_call | solution.py:54
  62.4 3.2 %shard_map.117.block_ref = bf16[1536,1536]{1,0:T(8,128)(2,1)S(1)} custom-call(s32[1,2]{1,0:T(1,128)S(1)} %copy-done.5, bf16[1536,128]{1,0:T(8,128)(2,1)S(1)} %copy-done.1, bf16[1536,128]{1,0:T(8,128)(2,1)S(1)} %collective-permute-done.2.rest_0_, bf16[1536,128]{1,0:T(8,128)(2,1)S(1)} %collective-permute-done.rest_0_.rest_1_), custom_call_target="tpu_custom_call" | custom-call | flops 603979776 | bytes 5505024 | tf_op jit(solution)/shard_map/pallas_call | solution.py:54
  65.6 1.0 collective-permute-done.5.refs_2_
  66.5 2.6 %shard_map.118.rest_ref = f32[1536,256]{1,0:T(8,128)S(1)} custom-call(s32[1,2]{1,0:T(1,128)S(1)} %copy-done.5, bf16[1536,1536]{1,0:T(8,128)(2,1)S(1)} %shard_map.117.block_ref, f32[1536,256]{1,0:T(8,128)S(1)} %get-tuple-element.19.rest_ref, bf16[1536,128]{1,0:T(8,128)(2,1)S(1)} %collective-permute-done.3.refs_0_, ...), custom_call_target="tpu_custom_call" | custom-call | flops 1207959552 | bytes 8650752 | tf_op jit(solution)/shard_map/pallas_call | solution.py:54
  69.2 1.1 shard_map.124.coupled_ref
  70.3 4.7 %collective-permute-done.1.rest_1_ = bf16[1536,128]{1,0:T(8,128)(2,1)S(1)} collective-permute-done((bf16[1536,128]{1,0:T(8,128)(2,1)S(1)}, bf16[1536,128]{1,0:T(8,128)(2,1)S(1)}, u32[]{:S(2)}, u32[]{:S(2)}) %collective-permute-start.1) | collective-permute-done | bytes 393248 | tf_op jit(solution)/shard_map/ppermute | solution.py:157
  75.0 3.2 %shard_map.116.block_ref = bf16[1536,1536]{1,0:T(8,128)(2,1)S(1)} custom-call(s32[1,2]{1,0:T(1,128)S(1)} %copy-done.5, bf16[1536,128]{1,0:T(8,128)(2,1)S(1)} %copy-done.1, bf16[1536,128]{1,0:T(8,128)(2,1)S(1)} %collective-permute-done.rest_0_.rest_1_, bf16[1536,128]{1,0:T(8,128)(2,1)S(1)} %collective-permute-done.1.rest_1_), custom_call_target="tpu_custom_call" | custom-call | flops 603979776 | bytes 5505024 | tf_op jit(solution)/shard_map/pallas_call | solution.py:54
  78.2 5.2 %collective-permute-done.14.refs_1_ = bf16[1536,128]{1,0:T(8,128)(2,1)S(1)} collective-permute-done((bf16[1536,128]{1,0:T(8,128)(2,1)S(1)}, bf16[1536,128]{1,0:T(8,128)(2,1)S(1)}, u32[]{:S(2)}, u32[]{:S(2)}) %collective-permute-start.14) | collective-permute-done | bytes 393248 | tf_op jit(solution)/shard_map/ppermute | solution.py:157
  83.4 3.0 %shard_map.125 = (f32[1536,128]{1,0:T(8,128)S(1)}, bf16[1536,128]{1,0:T(8,128)(2,1)S(1)}, bf16[128,128]{1,0:T(8,128)(2,1)S(1)}) custom-call(s32[1,2]{1,0:T(1,128)S(1)} %copy-done.5, f32[1,1]{1,0:T(1,128)} %bitcast.7.low_ref, f32[1,1]{1,0:T(1,128)} %bitcast.12.high_ref, bf16[1536,1536]{1,0:T(8,128)(2,1)S(1)} %shard_map.116.block_ref, ...), custom_call_target="tpu_custom_call" | custom-call | flops 603979776 | bytes 7864320 | tf_op jit(solution)/shard_map/pallas_call | solution.py:54
  86.4 2.0 %collective-permute-done.15.refs_1_ = bf16[1536,128]{1,0:T(8,128)(2,1)S(1)} collective-permute-done((bf16[1536,128]{1,0:T(8,128)(2,1)S(1)}, bf16[1536,128]{1,0:T(8,128)(2,1)S(1)}, u32[]{:S(2)}, u32[]{:S(2)}) %collective-permute-start.15) | collective-permute-done | bytes 393248 | tf_op jit(solution)/shard_map/ppermute | solution.py:157
  88.5 3.1 %shard_map.126 = (f32[1536,128]{1,0:T(8,128)S(1)}, bf16[1536,128]{1,0:T(8,128)(2,1)S(1)}, bf16[128,256]{1,0:T(8,128)(2,1)S(1)}) custom-call(s32[1,2]{1,0:T(1,128)S(1)} %copy-done.5, f32[1,1]{1,0:T(1,128)} %bitcast.8.low_ref, f32[1,1]{1,0:T(1,128)} %bitcast.13.high_ref, bf16[1536,1536]{1,0:T(8,128)(2,1)S(1)} %shard_map.116.block_ref, ...), custom_call_target="tpu_custom_call" | custom-call | flops 603979776 | bytes 7864320 | tf_op jit(solution)/shard_map/pallas_call | solution.py:54
  91.6 1.7 %collective-permute-start.20 = (bf16[128,256]{1,0:T(8,128)(2,1)S(1)}, bf16[128,256]{1,0:T(8,128)(2,1)S(1)}, u32[]{:S(2)}, u32[]{:S(2)}) collective-permute-start(bf16[128,256]{1,0:T(8,128)(2,1)S(1)} %get-tuple-element.27.refs_0_), channel_id=1, source_target_pairs={{0,1},{1,0},{2,3},{3,2},{4,5},{5,4},{6,7},{7,6},{8,9},{9,8},{10,11... | collective-permute-start | bytes 196616 | tf_op jit(solution)/shard_map/ppermute | solution.py:157
  94.0 1.9 %collective-permute-done.20.refs_1_ = bf16[128,256]{1,0:T(8,128)(2,1)S(1)} collective-permute-done((bf16[128,256]{1,0:T(8,128)(2,1)S(1)}, bf16[128,256]{1,0:T(8,128)(2,1)S(1)}, u32[]{:S(2)}, u32[]{:S(2)}) %collective-permute-start.20) | collective-permute-done | bytes 65568 | tf_op jit(solution)/shard_map/ppermute | solution.py:157
  97.6 12.8 %collective-permute-start.22 = (bf16[128,512]{1,0:T(8,128)(2,1)S(1)}, bf16[128,512]{1,0:T(8,128)(2,1)S(1)}, u32[]{:S(2)}, u32[]{:S(2)}) collective-permute-start(bf16[128,512]{1,0:T(8,128)(2,1)S(1)} %shard_map.130.summed_ref), channel_id=1, source_target_pairs={{0,1},{1,0},{2,3},{3,2},{4,5},{5,4},{6,7},{7,6},{8,9},{9,8},{10,11... | collective-permute-start | bytes 393224 | tf_op jit(solution)/shard_map/ppermute | solution.py:157
  110.5 1.9 %collective-permute-start.16 = (bf16[1536,128]{1,0:T(8,128)(2,1)S(1)}, bf16[1536,128]{1,0:T(8,128)(2,1)S(1)}, u32[]{:S(2)}, u32[]{:S(2)}) collective-permute-start(bf16[1536,128]{1,0:T(8,128)(2,1)S(1)} %get-tuple-element.20.lead_ref), channel_id=1, source_target_pairs={{0,1},{1,0},{2,3},{3,2},{4,5},{5,4},{6,7},{7,6},{8,9},{9,8},{10,11... | collective-permute-start | bytes 1179656 | tf_op jit(solution)/shard_map/ppermute | solution.py:157
  112.4 2.3 %collective-permute-done.22.handed_ref.refs_2_ = bf16[128,512]{1,0:T(8,128)(2,1)S(1)} collective-permute-done((bf16[128,512]{1,0:T(8,128)(2,1)S(1)}, bf16[128,512]{1,0:T(8,128)(2,1)S(1)}, u32[]{:S(2)}, u32[]{:S(2)}) %collective-permute-start.22) | collective-permute-done | bytes 131104 | tf_op jit(solution)/shard_map/ppermute | solution.py:157
  114.8 1.5 %collective-permute-start.23 = (bf16[128,256]{1,0:T(8,128)(2,1)S(1)}, bf16[128,256]{1,0:T(8,128)(2,1)S(1)}, u32[]{:S(2)}, u32[]{:S(2)}) collective-permute-start(bf16[128,256]{1,0:T(8,128)(2,1)S(1)} %shard_map.131.refs_0_), channel_id=1, source_target_pairs={{0,8},{4,12},{8,16},{12,20},{16,24},{20,28},{24,0},{28,4},{1,9},{5... | collective-permute-start | bytes 196616 | tf_op jit(solution)/shard_map/ppermute | solution.py:22
  116.3 3.7 %collective-permute-done.23.refs_1_.refs_3_ = bf16[128,256]{1,0:T(8,128)(2,1)S(1)} collective-permute-done((bf16[128,256]{1,0:T(8,128)(2,1)S(1)}, bf16[128,256]{1,0:T(8,128)(2,1)S(1)}, u32[]{:S(2)}, u32[]{:S(2)}) %collective-permute-start.23) | collective-permute-done | bytes 65568 | tf_op jit(solution)/shard_map/ppermute | solution.py:22
  120.0 1.5 %collective-permute-start.24 = (bf16[128,256]{1,0:T(8,128)(2,1)S(1)}, bf16[128,256]{1,0:T(8,128)(2,1)S(1)}, u32[]{:S(2)}, u32[]{:S(2)}) collective-permute-start(bf16[128,256]{1,0:T(8,128)(2,1)S(1)} %shard_map.131.refs_0_), channel_id=1, source_target_pairs={{0,16},{4,20},{8,24},{12,28},{16,0},{20,4},{24,8},{28,12},{1,17},{... | collective-permute-start | bytes 196616 | tf_op jit(solution)/shard_map/ppermute | solution.py:22
  121.5 2.7 %collective-permute-start.27 = (bf16[1536,128]{1,0:T(8,128)(2,1)S(1)}, bf16[1536,128]{1,0:T(8,128)(2,1)S(1)}, u32[]{:S(2)}, u32[]{:S(2)}) collective-permute-start(bf16[1536,128]{1,0:T(8,128)(2,1)S(1)} %collective-permute-done.17.refs_1_.refs_0_), channel_id=1, source_target_pairs={{0,2},{1,0},{2,3},{3,1},{4,6},{5,4},{6,7},{7,5},{8,10},{9,8},{10,1... | collective-permute-start | bytes 1179656 | tf_op jit(solution)/shard_map/ppermute | solution.py:157
  124.2 1.5 %collective-permute-start.25 = (bf16[128,256]{1,0:T(8,128)(2,1)S(1)}, bf16[128,256]{1,0:T(8,128)(2,1)S(1)}, u32[]{:S(2)}, u32[]{:S(2)}) collective-permute-start(bf16[128,256]{1,0:T(8,128)(2,1)S(1)} %shard_map.131.refs_0_), channel_id=1, source_target_pairs={{0,24},{4,28},{8,0},{12,4},{16,8},{20,12},{24,16},{28,20},{1,25},{... | collective-permute-start | bytes 196616 | tf_op jit(solution)/shard_map/ppermute | solution.py:22
  125.8 2.7 %collective-permute-done.25.refs_3_.refs_5_ = bf16[128,256]{1,0:T(8,128)(2,1)S(1)} collective-permute-done((bf16[128,256]{1,0:T(8,128)(2,1)S(1)}, bf16[128,256]{1,0:T(8,128)(2,1)S(1)}, u32[]{:S(2)}, u32[]{:S(2)}) %collective-permute-start.25) | collective-permute-done | bytes 65568 | tf_op jit(solution)/shard_map/ppermute | solution.py:22
  128.6 2.7 %collective-permute-start.28 = (bf16[1024,128]{1,0:T(8,128)(2,1)S(1)}, bf16[1024,128]{1,0:T(8,128)(2,1)S(1)}, u32[]{:S(2)}, u32[]{:S(2)}) collective-permute-start(bf16[1024,128]{1,0:T(8,128)(2,1)S(1)} %slice.8), channel_id=1, source_target_pairs={{0,2},{1,0},{2,3},{3,1},{4,6},{5,4},{6,7},{7,5},{8,10},{9,8},{10,1... | collective-permute-start | bytes 786440 | tf_op jit(solution)/shard_map/ppermute | solution.py:157
  131.4 3.0 %shard_map.127 = (f32[1536,256]{1,0:T(8,128)}, f32[1536,256]{1,0:T(8,128)S(1)}) custom-call(f32[1,1]{1,0:T(1,128)} %bitcast.9.low_ref, f32[1,1]{1,0:T(1,128)} %bitcast.14.high_ref, bf16[1536,1536]{1,0:T(8,128)(2,1)S(1)} %get-tuple-element.18.block_ref, bf16[1536,128]{1,0:T(8,128)(2,1)S(1)} %get-tuple-element.20.lead_ref, ...), custom_call_target="tpu_custom_call" | custom-call | flops 1207959552 | bytes 11796480 | tf_op jit(solution)/shard_map/pallas_call | solution.py:54
  134.5 2.4 %shard_map.128.rest_ref = f32[1536,256]{1,0:T(8,128)S(1)} custom-call(s32[1,2]{1,0:T(1,128)S(1)} %copy-done.5, bf16[1536,1536]{1,0:T(8,128)(2,1)S(1)} %shard_map.117.block_ref, f32[1536,256]{1,0:T(8,128)S(1)} %get-tuple-element.26.rest_ref, bf16[1536,128]{1,0:T(8,128)(2,1)S(1)} %collective-permute-done.16.refs_0_, ...), custom_call_target="tpu_custom_call" | custom-call | flops 1207959552 | bytes 8650752 | tf_op jit(solution)/shard_map/pallas_call | solution.py:54
  136.9 1.1 shard_map.133.coupled_ref
  138.0 3.0 %shard_map.134 = (f32[1536,256]{1,0:T(8,128)}, f32[1536,128]{1,0:T(8,128)S(1)}) custom-call(s32[1,2]{1,0:T(1,128)S(1)} %copy-done.5, bf16[1536,1536]{1,0:T(8,128)(2,1)S(1)} %shard_map.116.block_ref, f32[1536,256]{1,0:T(8,128)S(1)} %shard_map.128.rest_ref, bf16[1536,128]{1,0:T(8,128)(2,1)S(1)} %copy-done, bf16[128,256]{1,0:T(8,128)(2,1)S(1)} %shard_map.133.coupled_ref, ...), custom_call_target="tpu_custom_call" | custom-call | flops 603979776 | bytes 6684672 | tf_op jit(solution)/shard_map/pallas_call | solution.py:54
  141.0 1.9 %shard_map.135.trail_ref = f32[1536,128]{1,0:T(8,128)S(1)} custom-call(s32[1,2]{1,0:T(1,128)S(1)} %copy-done.5, bf16[1536,1536]{1,0:T(8,128)(2,1)S(1)} %shard_map.116.block_ref, f32[1536,128]{1,0:T(8,128)S(1)} %get-tuple-element.28.trail_ref, bf16[1536,128]{1,0:T(8,128)(2,1)S(1)} %collective-permute-done.19.refs_3_.inner_ref, ...), custom_call_target="tpu_custom_call" | custom-call | flops 402653184 | bytes 4718592 | tf_op jit(solution)/shard_map/pallas_call | solution.py:54
  142.9 1.9 %shard_map.136 = f32[1536,256]{1,0:T(8,128)} custom-call(s32[1,2]{1,0:T(1,128)S(1)} %copy-done.5, bf16[1536,1536]{1,0:T(8,128)(2,1)S(1)} %shard_map.116.block_ref, f32[1536,128]{1,0:T(8,128)S(1)} %shard_map.135.trail_ref, bf16[512,128]{1,0:T(8,128)(2,1)S(1)} %collective-permute-done.29.refs_0_, ...), custom_call_target="tpu_custom_call", output_to_operand_aliasing={{}: (4, {})} | custom-call | flops 603979776 | bytes 6684672 | tf_op jit(solution)/shard_map/pallas_call | solution.py:54
  (56 shorter events, 4.9 us)
Async XLA Ops:
  1.9 1.4 copy-start.6
  3.3 0.7 copy-start.8
  4.0 1.7 %copy-start = (bf16[1536,128]{1,0:T(8,128)(2,1)S(1)}, bf16[1536,128]{1,0:T(8,128)(2,1)}, u32[]{:S(2)}) copy-start(bf16[1536,128]{1,0:T(8,128)(2,1)} %bases_ref.7) | copy-start | bytes 1179652
  4.0 1.7 %copy-start.4 = (bf16[1,128,128]{2,1,0:T(8,128)(2,1)S(1)}, bf16[1,128,128]{2,1,0:T(8,128)(2,1)}, u32[]{:S(2)}) copy-start(bf16[1,128,128]{2,1,0:T(8,128)(2,1)} %param.16) | copy-start | bytes 98308
  5.7 7.8 %copy-start.1 = (bf16[1536,128]{1,0:T(8,128)(2,1)S(1)}, bf16[1536,128]{1,0:T(8,128)(2,1)}, u32[]{:S(2)}) copy-start(bf16[1536,128]{1,0:T(8,128)(2,1)} %points_ref.5) | copy-start | bytes 1179652
  5.7 37.9 %copy-start.7 = (f32[1536,256]{1,0:T(8,128)S(1)}, f32[1536,256]{1,0:T(8,128)}, u32[]{:S(2)}) copy-start(f32[1536,256]{1,0:T(8,128)} %right_ref.3) | copy-start | bytes 4718596
  6.2 5.9 %collective-permute-start.7 = (bf16[128,384]{1,0:T(8,128)(2,1)S(1)}, bf16[128,384]{1,0:T(8,128)(2,1)S(1)}, u32[]{:S(2)}, u32[]{:S(2)}) collective-permute-start(bf16[128,384]{1,0:T(8,128)(2,1)S(1)} %shard_map.119.refs_0_), channel_id=1, source_target_pairs={{0,1},{1,0},{2,3},{3,2},{4,5},{5,4},{6,7},{7,6},{8,9},{9,8},{10,11... | collective-permute-start | bytes 294920 | tf_op jit(solution)/shard_map/ppermute | solution.py:157
  12.1 2.1 %collective-permute-start.8 = (bf16[256,384]{1,0:T(8,128)(2,1)S(1)}, bf16[256,384]{1,0:T(8,128)(2,1)S(1)}, u32[]{:S(2)}, u32[]{:S(2)}) collective-permute-start(bf16[256,384]{1,0:T(8,128)(2,1)S(1)} %shard_map.120.pair_ref.first_pair_ref.refs_0_), channel_id=1, source_target_pairs={{0,0},{1,2},{2,1},{3,3},{4,4},{5,6},{6,5},{7,7},{8,8},{9,10},{10,9... | collective-permute-start | bytes 589832 | tf_op jit(solution)/shard_map/ppermute | solution.py:157
  12.8 18.3 %collective-permute-start.4 = (bf16[1536,128]{1,0:T(8,128)(2,1)S(1)}, bf16[1536,128]{1,0:T(8,128)(2,1)S(1)}, u32[]{:S(2)}, u32[]{:S(2)}) collective-permute-start(bf16[1536,128]{1,0:T(8,128)(2,1)S(1)} %get-tuple-element.16.lead_ref), channel_id=1, source_target_pairs={{0,0},{1,2},{2,1},{3,3},{4,4},{5,6},{6,5},{7,7},{8,8},{9,10},{10,9... | collective-permute-start | bytes 1179656 | tf_op jit(solution)/shard_map/ppermute | solution.py:157
  13.5 18.3 %collective-permute-start = (bf16[1536,128]{1,0:T(8,128)(2,1)S(1)}, bf16[1536,128]{1,0:T(8,128)(2,1)S(1)}, u32[]{:S(2)}, u32[]{:S(2)}) collective-permute-start(bf16[1536,128]{1,0:T(8,128)(2,1)S(1)} %copy-done.1), channel_id=1, source_target_pairs={{0,0},{1,2},{2,1},{3,3},{4,4},{5,6},{6,5},{7,7},{8,8},{9,10},{10,9... | collective-permute-start | bytes 1179656 | tf_op jit(solution)/shard_map/ppermute | solution.py:157
  14.4 12.1 %collective-permute-start.9 = (bf16[128,512]{1,0:T(8,128)(2,1)S(1)}, bf16[128,512]{1,0:T(8,128)(2,1)S(1)}, u32[]{:S(2)}, u32[]{:S(2)}) collective-permute-start(bf16[128,512]{1,0:T(8,128)(2,1)S(1)} %shard_map.121.summed_ref), channel_id=1, source_target_pairs={{0,1},{1,0},{2,3},{3,2},{4,5},{5,4},{6,7},{7,6},{8,9},{9,8},{10,11... | collective-permute-start | bytes 393224 | tf_op jit(solution)/shard_map/ppermute | solution.py:157
  26.6 13.1 %collective-permute-start.10 = (bf16[128,256]{1,0:T(8,128)(2,1)S(1)}, bf16[128,256]{1,0:T(8,128)(2,1)S(1)}, u32[]{:S(2)}, u32[]{:S(2)}) collective-permute-start(bf16[128,256]{1,0:T(8,128)(2,1)S(1)} %shard_map.122.refs_0_), channel_id=1, source_target_pairs={{0,8},{4,12},{8,16},{12,20},{16,24},{20,28},{24,0},{28,4},{1,9},{5... | collective-permute-start | bytes 196616 | tf_op jit(solution)/shard_map/ppermute | solution.py:22
  28.1 11.6 %collective-permute-start.11 = (bf16[128,256]{1,0:T(8,128)(2,1)S(1)}, bf16[128,256]{1,0:T(8,128)(2,1)S(1)}, u32[]{:S(2)}, u32[]{:S(2)}) collective-permute-start(bf16[128,256]{1,0:T(8,128)(2,1)S(1)} %shard_map.122.refs_0_), channel_id=1, source_target_pairs={{0,16},{4,20},{8,24},{12,28},{16,0},{20,4},{24,8},{28,12},{1,17},{... | collective-permute-start | bytes 196616 | tf_op jit(solution)/shard_map/ppermute | solution.py:22
  29.7 12.1 %collective-permute-start.12 = (bf16[128,256]{1,0:T(8,128)(2,1)S(1)}, bf16[128,256]{1,0:T(8,128)(2,1)S(1)}, u32[]{:S(2)}, u32[]{:S(2)}) collective-permute-start(bf16[128,256]{1,0:T(8,128)(2,1)S(1)} %shard_map.122.refs_0_), channel_id=1, source_target_pairs={{0,24},{4,28},{8,0},{12,4},{16,8},{20,12},{24,16},{28,20},{1,25},{... | collective-permute-start | bytes 196616 | tf_op jit(solution)/shard_map/ppermute | solution.py:22
  31.1 16.5 %collective-permute-start.6 = (bf16[1536,128]{1,0:T(8,128)(2,1)S(1)}, bf16[1536,128]{1,0:T(8,128)(2,1)S(1)}, u32[]{:S(2)}, u32[]{:S(2)}) collective-permute-start(bf16[1536,128]{1,0:T(8,128)(2,1)S(1)} %get-tuple-element.17.trail_ref), channel_id=1, source_target_pairs={{0,0},{1,2},{2,1},{3,3},{4,4},{5,6},{6,5},{7,7},{8,8},{9,10},{10,9... | collective-permute-start | bytes 1179656 | tf_op jit(solution)/shard_map/ppermute | solution.py:157
  31.8 17.9 %collective-permute-start.3 = (bf16[1536,128]{1,0:T(8,128)(2,1)S(1)}, bf16[1536,128]{1,0:T(8,128)(2,1)S(1)}, u32[]{:S(2)}, u32[]{:S(2)}) collective-permute-start(bf16[1536,128]{1,0:T(8,128)(2,1)S(1)} %get-tuple-element.16.lead_ref), channel_id=1, source_target_pairs={{0,1},{1,0},{2,3},{3,2},{4,5},{5,4},{6,7},{7,6},{8,9},{9,8},{10,11... | collective-permute-start | bytes 1179656 | tf_op jit(solution)/shard_map/ppermute | solution.py:157
  39.7 18.4 %collective-permute-start.2 = (bf16[1536,128]{1,0:T(8,128)(2,1)S(1)}, bf16[1536,128]{1,0:T(8,128)(2,1)S(1)}, u32[]{:S(2)}, u32[]{:S(2)}) collective-permute-start(bf16[1536,128]{1,0:T(8,128)(2,1)S(1)} %copy-done.1), channel_id=1, source_target_pairs={{0,1},{1,0},{2,3},{3,2},{4,5},{5,4},{6,7},{7,6},{8,9},{9,8},{10,11... | collective-permute-start | bytes 1179656 | tf_op jit(solution)/shard_map/ppermute | solution.py:157
  39.7 26.8 %collective-permute-start.5 = (bf16[1536,128]{1,0:T(8,128)(2,1)S(1)}, bf16[1536,128]{1,0:T(8,128)(2,1)S(1)}, u32[]{:S(2)}, u32[]{:S(2)}) collective-permute-start(bf16[1536,128]{1,0:T(8,128)(2,1)S(1)} %get-tuple-element.17.trail_ref), channel_id=1, source_target_pairs={{0,1},{1,0},{2,3},{3,2},{4,5},{5,4},{6,7},{7,6},{8,9},{9,8},{10,11... | collective-permute-start | bytes 1179656 | tf_op jit(solution)/shard_map/ppermute | solution.py:157
  41.8 33.2 %collective-permute-start.1 = (bf16[1536,128]{1,0:T(8,128)(2,1)S(1)}, bf16[1536,128]{1,0:T(8,128)(2,1)S(1)}, u32[]{:S(2)}, u32[]{:S(2)}) collective-permute-start(bf16[1536,128]{1,0:T(8,128)(2,1)S(1)} %collective-permute-done.rest_0_.rest_1_), channel_id=1, source_target_pairs={{0,2},{1,0},{2,3},{3,1},{4,6},{5,4},{6,7},{7,5},{8,10},{9,8},{10,1... | collective-permute-start | bytes 1179656 | tf_op jit(solution)/shard_map/ppermute | solution.py:157
  47.6 35.8 %collective-permute-start.14 = (bf16[1536,128]{1,0:T(8,128)(2,1)S(1)}, bf16[1536,128]{1,0:T(8,128)(2,1)S(1)}, u32[]{:S(2)}, u32[]{:S(2)}) collective-permute-start(bf16[1536,128]{1,0:T(8,128)(2,1)S(1)} %collective-permute-done.4.refs_1_.refs_0_), channel_id=1, source_target_pairs={{0,2},{1,0},{2,3},{3,1},{4,6},{5,4},{6,7},{7,5},{8,10},{9,8},{10,1... | collective-permute-start | bytes 1179656 | tf_op jit(solution)/shard_map/ppermute | solution.py:157
  49.7 38.8 %collective-permute-start.15 = (bf16[1536,128]{1,0:T(8,128)(2,1)S(1)}, bf16[1536,128]{1,0:T(8,128)(2,1)S(1)}, u32[]{:S(2)}, u32[]{:S(2)}) collective-permute-start(bf16[1536,128]{1,0:T(8,128)(2,1)S(1)} %collective-permute-done.6.refs_3_.refs_0_), channel_id=1, source_target_pairs={{0,2},{1,0},{2,3},{3,1},{4,6},{5,4},{6,7},{7,5},{8,10},{9,8},{10,1... | collective-permute-start | bytes 1179656 | tf_op jit(solution)/shard_map/ppermute | solution.py:157
  58.1 11.0 %collective-permute-start.13 = (bf16[512,256]{1,0:T(8,128)(2,1)S(1)}, bf16[512,256]{1,0:T(8,128)(2,1)S(1)}, u32[]{:S(2)}, u32[]{:S(2)}) collective-permute-start(bf16[512,256]{1,0:T(8,128)(2,1)S(1)} %shard_map.123), channel_id=1, source_target_pairs={{0,4},{4,0},{8,12},{12,8},{16,20},{20,16},{24,28},{28,24},{1,5},{5... | collective-permute-start | bytes 786440 | tf_op jit(solution)/shard_map/ppermute | solution.py:625
  58.1 4.2 %copy-start.5 = (s32[1,2]{1,0:T(1,128)S(1)}, s32[1,2]{1,0:T(1,128)}, u32[]{:S(2)}) copy-start(s32[1,2]{1,0:T(1,128)} %near_ref.21) | copy-start | bytes 28
  66.5 2.6 %copy-start.2 = (bf16[1,8,128,128]{3,2,1,0:T(8,128)(2,1)S(1)}, bf16[1,8,128,128]{3,2,1,0:T(8,128)(2,1)}, u32[]{:S(2)}) copy-start(bf16[1,8,128,128]{3,2,1,0:T(8,128)(2,1)} %param.17) | copy-start | bytes 786436
  66.5 2.6 %copy-start.3 = (bf16[1,4,128,128]{3,2,1,0:T(8,128)(2,1)S(1)}, bf16[1,4,128,128]{3,2,1,0:T(8,128)(2,1)}, u32[]{:S(2)}) copy-start(bf16[1,4,128,128]{3,2,1,0:T(8,128)(2,1)} %param.15) | copy-start | bytes 393220
  91.6 4.3 %collective-permute-start.20 = (bf16[128,256]{1,0:T(8,128)(2,1)S(1)}, bf16[128,256]{1,0:T(8,128)(2,1)S(1)}, u32[]{:S(2)}, u32[]{:S(2)}) collective-permute-start(bf16[128,256]{1,0:T(8,128)(2,1)S(1)} %get-tuple-element.27.refs_0_), channel_id=1, source_target_pairs={{0,1},{1,0},{2,3},{3,2},{4,5},{5,4},{6,7},{7,6},{8,9},{9,8},{10,11... | collective-permute-start | bytes 196616 | tf_op jit(solution)/shard_map/ppermute | solution.py:157
  93.3 28.2 %collective-permute-start.17 = (bf16[1536,128]{1,0:T(8,128)(2,1)S(1)}, bf16[1536,128]{1,0:T(8,128)(2,1)S(1)}, u32[]{:S(2)}, u32[]{:S(2)}) collective-permute-start(bf16[1536,128]{1,0:T(8,128)(2,1)S(1)} %get-tuple-element.20.lead_ref), channel_id=1, source_target_pairs={{0,0},{1,2},{2,1},{3,3},{4,4},{5,6},{6,5},{7,7},{8,8},{9,10},{10,9... | collective-permute-start | bytes 1179656 | tf_op jit(solution)/shard_map/ppermute | solution.py:157
  95.9 1.4 collective-permute-start.21
  96.6 32.0 %collective-permute-start.19 = (bf16[1536,128]{1,0:T(8,128)(2,1)S(1)}, bf16[1536,128]{1,0:T(8,128)(2,1)S(1)}, u32[]{:S(2)}, u32[]{:S(2)}) collective-permute-start(bf16[1536,128]{1,0:T(8,128)(2,1)S(1)} %get-tuple-element.22.trail_ref), channel_id=1, source_target_pairs={{0,0},{1,2},{2,1},{3,3},{4,4},{5,6},{6,5},{7,7},{8,8},{9,10},{10,9... | collective-permute-start | bytes 1179656 | tf_op jit(solution)/shard_map/ppermute | solution.py:157
  97.6 17.2 %collective-permute-start.22 = (bf16[128,512]{1,0:T(8,128)(2,1)S(1)}, bf16[128,512]{1,0:T(8,128)(2,1)S(1)}, u32[]{:S(2)}, u32[]{:S(2)}) collective-permute-start(bf16[128,512]{1,0:T(8,128)(2,1)S(1)} %shard_map.130.summed_ref), channel_id=1, source_target_pairs={{0,1},{1,0},{2,3},{3,2},{4,5},{5,4},{6,7},{7,6},{8,9},{9,8},{10,11... | collective-permute-start | bytes 393224 | tf_op jit(solution)/shard_map/ppermute | solution.py:157
  110.4 24.0 %collective-permute-start.18 = (bf16[1536,128]{1,0:T(8,128)(2,1)S(1)}, bf16[1536,128]{1,0:T(8,128)(2,1)S(1)}, u32[]{:S(2)}, u32[]{:S(2)}) collective-permute-start(bf16[1536,128]{1,0:T(8,128)(2,1)S(1)} %get-tuple-element.22.trail_ref), channel_id=1, source_target_pairs={{0,1},{1,0},{2,3},{3,2},{4,5},{5,4},{6,7},{7,6},{8,9},{9,8},{10,11... | collective-permute-start | bytes 1179656 | tf_op jit(solution)/shard_map/ppermute | solution.py:157
  110.5 24.0 %collective-permute-start.16 = (bf16[1536,128]{1,0:T(8,128)(2,1)S(1)}, bf16[1536,128]{1,0:T(8,128)(2,1)S(1)}, u32[]{:S(2)}, u32[]{:S(2)}) collective-permute-start(bf16[1536,128]{1,0:T(8,128)(2,1)S(1)} %get-tuple-element.20.lead_ref), channel_id=1, source_target_pairs={{0,1},{1,0},{2,3},{3,2},{4,5},{5,4},{6,7},{7,6},{8,9},{9,8},{10,11... | collective-permute-start | bytes 1179656 | tf_op jit(solution)/shard_map/ppermute | solution.py:157
  114.8 5.2 %collective-permute-start.23 = (bf16[128,256]{1,0:T(8,128)(2,1)S(1)}, bf16[128,256]{1,0:T(8,128)(2,1)S(1)}, u32[]{:S(2)}, u32[]{:S(2)}) collective-permute-start(bf16[128,256]{1,0:T(8,128)(2,1)S(1)} %shard_map.131.refs_0_), channel_id=1, source_target_pairs={{0,8},{4,12},{8,16},{12,20},{16,24},{20,28},{24,0},{28,4},{1,9},{5... | collective-permute-start | bytes 196616 | tf_op jit(solution)/shard_map/ppermute | solution.py:22
  120.0 4.3 %collective-permute-start.24 = (bf16[128,256]{1,0:T(8,128)(2,1)S(1)}, bf16[128,256]{1,0:T(8,128)(2,1)S(1)}, u32[]{:S(2)}, u32[]{:S(2)}) collective-permute-start(bf16[128,256]{1,0:T(8,128)(2,1)S(1)} %shard_map.131.refs_0_), channel_id=1, source_target_pairs={{0,16},{4,20},{8,24},{12,28},{16,0},{20,4},{24,8},{28,12},{1,17},{... | collective-permute-start | bytes 196616 | tf_op jit(solution)/shard_map/ppermute | solution.py:22
  121.5 16.5 %collective-permute-start.27 = (bf16[1536,128]{1,0:T(8,128)(2,1)S(1)}, bf16[1536,128]{1,0:T(8,128)(2,1)S(1)}, u32[]{:S(2)}, u32[]{:S(2)}) collective-permute-start(bf16[1536,128]{1,0:T(8,128)(2,1)S(1)} %collective-permute-done.17.refs_1_.refs_0_), channel_id=1, source_target_pairs={{0,2},{1,0},{2,3},{3,1},{4,6},{5,4},{6,7},{7,5},{8,10},{9,8},{10,1... | collective-permute-start | bytes 1179656 | tf_op jit(solution)/shard_map/ppermute | solution.py:157
  124.2 4.3 %collective-permute-start.25 = (bf16[128,256]{1,0:T(8,128)(2,1)S(1)}, bf16[128,256]{1,0:T(8,128)(2,1)S(1)}, u32[]{:S(2)}, u32[]{:S(2)}) collective-permute-start(bf16[128,256]{1,0:T(8,128)(2,1)S(1)} %shard_map.131.refs_0_), channel_id=1, source_target_pairs={{0,24},{4,28},{8,0},{12,4},{16,8},{20,12},{24,16},{28,20},{1,25},{... | collective-permute-start | bytes 196616 | tf_op jit(solution)/shard_map/ppermute | solution.py:22
  128.5 8.4 %collective-permute-start.26 = (bf16[512,256]{1,0:T(8,128)(2,1)S(1)}, bf16[512,256]{1,0:T(8,128)(2,1)S(1)}, u32[]{:S(2)}, u32[]{:S(2)}) collective-permute-start(bf16[512,256]{1,0:T(8,128)(2,1)S(1)} %shard_map.132), channel_id=1, source_target_pairs={{0,4},{4,0},{8,12},{12,8},{16,20},{20,16},{24,28},{28,24},{1,5},{5... | collective-permute-start | bytes 786440 | tf_op jit(solution)/shard_map/ppermute | solution.py:625
  128.6 12.3 %collective-permute-start.28 = (bf16[1024,128]{1,0:T(8,128)(2,1)S(1)}, bf16[1024,128]{1,0:T(8,128)(2,1)S(1)}, u32[]{:S(2)}, u32[]{:S(2)}) collective-permute-start(bf16[1024,128]{1,0:T(8,128)(2,1)S(1)} %slice.8), channel_id=1, source_target_pairs={{0,2},{1,0},{2,3},{3,1},{4,6},{5,4},{6,7},{7,5},{8,10},{9,8},{10,1... | collective-permute-start | bytes 786440 | tf_op jit(solution)/shard_map/ppermute | solution.py:157
  134.4 8.5 %collective-permute-start.29 = (bf16[512,128]{1,0:T(8,128)(2,1)S(1)}, bf16[512,128]{1,0:T(8,128)(2,1)S(1)}, u32[]{:S(2)}, u32[]{:S(2)}) collective-permute-start(bf16[512,128]{1,0:T(8,128)(2,1)S(1)} %slice.9), channel_id=1, source_target_pairs={{0,2},{1,0},{2,3},{3,1},{4,6},{5,4},{6,7},{7,5},{8,10},{9,8},{10,1... | collective-permute-start | bytes 393224 | tf_op jit(solution)/shard_map/ppermute | solution.py:157

commit v5 on v4

--- a/solution.py
+++ b/solution.py
@@ -199,21 +199,32 @@
     half = width // 2
     step = tile_of(rows)
 
-    def body(low_ref, high_ref, right_ref, order_ref, lead_ref, trail_ref, turned):
+    def body(low_ref, high_ref, right_hbm, order_hbm, lead_ref, trail_ref, right, order, turned, sems):
         theta, _, _ = factors(low_ref, high_ref, width)
-        turned[...] = (right_ref[...] / theta).astype(BF16).T
-
-        for k in range(rows // step):
-            at = pl.ds(k * step, step)
+        tiles = [pl.ds(k * step, step) for k in range(rows // step)]
+        copies = [pltpu.make_async_copy(right_hbm.at[at, :], right.at[at, :], sems.at[k])
+                  for k, at in enumerate(tiles)]
+        copies.append(pltpu.make_async_copy(order_hbm, order, sems.at[len(tiles)]))
+        for copy in copies:
+            copy.start()
+        for copy, at in zip(copies, tiles):
+            copy.wait()
+            turned[:, at] = (right[at, :] / theta).astype(BF16).T
+        copies[-1].wait()
+        for at in tiles:
             source = lax.broadcasted_iota(jnp.int32, (rows, step), 0)
-            places = jnp.where(source == order_ref[:, at], 1.0, 0.0).astype(BF16)
+            places = jnp.where(source == order[:, at], 1.0, 0.0).astype(BF16)
             v = dot(turned[...], places).T.astype(BF16)
             lead_ref[at, :] = v[:, :half]
             trail_ref[at, :] = v[:, half:]
 
     return call(
-        body, (shape(BF16, rows, half), shape(BF16, rows, width - half)), (low, high, right_sides, order),
-        scratch=[VMEM((width, rows), BF16)],
+        body, (shape(BF16, rows, half), shape(BF16, rows, width - half)),
+        (low, high, pltpu.with_memory_space_constraint(right_sides, pltpu.HBM),
+         pltpu.with_memory_space_constraint(order, pltpu.HBM)),
+        in_specs=[VMEM_SPEC, VMEM_SPEC, HBM_SPEC, HBM_SPEC],
+        scratch=[VMEM((rows, width), F32), VMEM((1, rows), jnp.int32), VMEM((width, rows), BF16),
+                 pltpu.SemaphoreType.DMA((rows // step + 1,))],
         flops=2 * rows * rows * width, bytes_=rows * width * 6,
     )
 

time: 145 us -> 145 us (level)
  local copies, waits for them, and re-layouts: 2.15 us -> 0.07 us
  Pallas kernels: 40.4 us -> 41.9 us
    unnamed x18 -> x16, local copies, waits for them, and re-layouts: 2.13 us -> 0.04 us
where the time goes in v5:
time: 145 us; the launch traced here: 144 us
  starting transfers between devices  65.9 us (45%)
  Pallas kernels  41.9 us (29%)
  waiting for transfers between devices  34.1 us (24%)
  between operations  2.51 us (2%)
    ppermute x22, starting transfers between devices, permute(): return lax.ppermute(block, 'member', pairs)  56.6 us
    pallas_call x24, Pallas kernels, call(): pl.pallas_call(body, out_shape=out, in_specs=in_specs or [SMEM_SPEC] * sc...  41.9 us
    ppermute x22, waiting for transfers between devices, permute(): return lax.ppermute(block, 'member', pairs)  27.6 us
    ppermute x6, starting transfers between devices, cycle(): lax.ppermute(array, axis, [(i, (i + by) % count) for i in range(count)])  9.17 us
    ppermute x6, waiting for transfers between devices, cycle(): lax.ppermute(array, axis, [(i, (i + by) % count) for i in range(count)])  6.42 us
  transfers between devices with their start and end apart: 30, of which 13 were waited for; matrix products, arithmetic and copies ran while one was open for 0% of the time, Pallas kernels for 23%

profile of v5, /device:TPU:0, one launch (start us, length us, event | category | flops | bytes accessed | tf_op | source)
XLA Modules:
  0.0 144.4 jit_solution(5289368411237688726)
XLA Ops:
  1.9 3.1 %shard_map.114 = (bf16[1536,128]{1,0:T(8,128)(2,1)S(1)}, bf16[1536,128]{1,0:T(8,128)(2,1)S(1)}) custom-call(f32[1,1]{1,0:T(1,128)} %bitcast.5.low_ref, f32[1,1]{1,0:T(1,128)} %bitcast.10.high_ref, f32[1536,256]{1,0:T(8,128)} %right_hbm.1, s32[1,1536]{1,0:T(1,128)} %order_hbm.1), custom_call_target="tpu_custom_call" | custom-call | flops 1207959552 | bytes 2359296 | tf_op jit(solution)/shard_map/pallas_call | solution.py:54
  5.5 3.1 %collective-permute-start.7 = (bf16[128,384]{1,0:T(8,128)(2,1)S(1)}, bf16[128,384]{1,0:T(8,128)(2,1)S(1)}, u32[]{:S(2)}, u32[]{:S(2)}) collective-permute-start(bf16[128,384]{1,0:T(8,128)(2,1)S(1)} %shard_map.119.refs_0_), channel_id=1, source_target_pairs={{0,1},{1,0},{2,3},{3,2},{4,5},{5,4},{6,7},{7,6},{8,9},{9,8},{10,11... | collective-permute-start | bytes 294920 | tf_op jit(solution)/shard_map/ppermute | solution.py:157
  8.6 2.8 %collective-permute-done.7.refs_1_ = bf16[128,384]{1,0:T(8,128)(2,1)S(1)} collective-permute-done((bf16[128,384]{1,0:T(8,128)(2,1)S(1)}, bf16[128,384]{1,0:T(8,128)(2,1)S(1)}, u32[]{:S(2)}, u32[]{:S(2)}) %collective-permute-start.7) | collective-permute-done | bytes 98336 | tf_op jit(solution)/shard_map/ppermute | solution.py:157
  12.1 0.7 collective-permute-start.4
  12.8 0.7 collective-permute-start
  13.8 9.2 %collective-permute-start.9 = (bf16[128,512]{1,0:T(8,128)(2,1)S(1)}, bf16[128,512]{1,0:T(8,128)(2,1)S(1)}, u32[]{:S(2)}, u32[]{:S(2)}) collective-permute-start(bf16[128,512]{1,0:T(8,128)(2,1)S(1)} %shard_map.121.summed_ref), channel_id=1, source_target_pairs={{0,1},{1,0},{2,3},{3,2},{4,5},{5,4},{6,7},{7,6},{8,9},{9,8},{10,11... | collective-permute-start | bytes 393224 | tf_op jit(solution)/shard_map/ppermute | solution.py:157
  23.0 2.9 %collective-permute-done.9.handed_ref.refs_2_ = bf16[128,512]{1,0:T(8,128)(2,1)S(1)} collective-permute-done((bf16[128,512]{1,0:T(8,128)(2,1)S(1)}, bf16[128,512]{1,0:T(8,128)(2,1)S(1)}, u32[]{:S(2)}, u32[]{:S(2)}) %collective-permute-start.9) | collective-permute-done | bytes 131104 | tf_op jit(solution)/shard_map/ppermute | solution.py:157
  25.9 1.5 %collective-permute-start.10 = (bf16[128,256]{1,0:T(8,128)(2,1)S(1)}, bf16[128,256]{1,0:T(8,128)(2,1)S(1)}, u32[]{:S(2)}, u32[]{:S(2)}) collective-permute-start(bf16[128,256]{1,0:T(8,128)(2,1)S(1)} %shard_map.122.refs_0_), channel_id=1, source_target_pairs={{0,8},{4,12},{8,16},{12,20},{16,24},{20,28},{24,0},{28,4},{1,9},{5... | collective-permute-start | bytes 196616 | tf_op jit(solution)/shard_map/ppermute | solution.py:22
  27.5 1.5 %collective-permute-start.11 = (bf16[128,256]{1,0:T(8,128)(2,1)S(1)}, bf16[128,256]{1,0:T(8,128)(2,1)S(1)}, u32[]{:S(2)}, u32[]{:S(2)}) collective-permute-start(bf16[128,256]{1,0:T(8,128)(2,1)S(1)} %shard_map.122.refs_0_), channel_id=1, source_target_pairs={{0,16},{4,20},{8,24},{12,28},{16,0},{20,4},{24,8},{28,12},{1,17},{... | collective-permute-start | bytes 196616 | tf_op jit(solution)/shard_map/ppermute | solution.py:22
  29.0 1.4 collective-permute-start.12
  30.4 0.7 collective-permute-start.6
  31.1 7.9 %collective-permute-start.3 = (bf16[1536,128]{1,0:T(8,128)(2,1)S(1)}, bf16[1536,128]{1,0:T(8,128)(2,1)S(1)}, u32[]{:S(2)}, u32[]{:S(2)}) collective-permute-start(bf16[1536,128]{1,0:T(8,128)(2,1)S(1)} %get-tuple-element.16.lead_ref), channel_id=1, source_target_pairs={{0,1},{1,0},{2,3},{3,2},{4,5},{5,4},{6,7},{7,6},{8,9},{9,8},{10,11... | collective-permute-start | bytes 1179656 | tf_op jit(solution)/shard_map/ppermute | solution.py:157
  39.1 2.0 %collective-permute-start.5 = (bf16[1536,128]{1,0:T(8,128)(2,1)S(1)}, bf16[1536,128]{1,0:T(8,128)(2,1)S(1)}, u32[]{:S(2)}, u32[]{:S(2)}) collective-permute-start(bf16[1536,128]{1,0:T(8,128)(2,1)S(1)} %get-tuple-element.17.trail_ref), channel_id=1, source_target_pairs={{0,1},{1,0},{2,3},{3,2},{4,5},{5,4},{6,7},{7,6},{8,9},{9,8},{10,11... | collective-permute-start | bytes 1179656 | tf_op jit(solution)/shard_map/ppermute | solution.py:157
  41.1 1.8 %collective-permute-start.1 = (bf16[1536,128]{1,0:T(8,128)(2,1)S(1)}, bf16[1536,128]{1,0:T(8,128)(2,1)S(1)}, u32[]{:S(2)}, u32[]{:S(2)}) collective-permute-start(bf16[1536,128]{1,0:T(8,128)(2,1)S(1)} %collective-permute-done.rest_0_.rest_1_), channel_id=1, source_target_pairs={{0,2},{1,0},{2,3},{3,1},{4,6},{5,4},{6,7},{7,5},{8,10},{9,8},{10,1... | collective-permute-start | bytes 1179656 | tf_op jit(solution)/shard_map/ppermute | solution.py:157
  42.9 4.0 %shard_map.113.ordered_ref = f32[1536,256]{1,0:T(8,128)S(1)} custom-call(f32[1536,256]{1,0:T(8,128)S(1)} %copy-done.6, s32[1,1536]{1,0:T(1,128)S(1)} %copy-done.7), custom_call_target="tpu_custom_call" | custom-call | flops 3623878656 | bytes 3145728 | tf_op jit(solution)/shard_map/pallas_call | solution.py:54
  47.0 2.0 %collective-permute-start.14 = (bf16[1536,128]{1,0:T(8,128)(2,1)S(1)}, bf16[1536,128]{1,0:T(8,128)(2,1)S(1)}, u32[]{:S(2)}, u32[]{:S(2)}) collective-permute-start(bf16[1536,128]{1,0:T(8,128)(2,1)S(1)} %collective-permute-done.4.refs_1_.refs_0_), channel_id=1, source_target_pairs={{0,2},{1,0},{2,3},{3,1},{4,6},{5,4},{6,7},{7,5},{8,10},{9,8},{10,1... | collective-permute-start | bytes 1179656 | tf_op jit(solution)/shard_map/ppermute | solution.py:157
  49.0 3.8 %collective-permute-start.15 = (bf16[1536,128]{1,0:T(8,128)(2,1)S(1)}, bf16[1536,128]{1,0:T(8,128)(2,1)S(1)}, u32[]{:S(2)}, u32[]{:S(2)}) collective-permute-start(bf16[1536,128]{1,0:T(8,128)(2,1)S(1)} %collective-permute-done.6.refs_3_.refs_0_), channel_id=1, source_target_pairs={{0,2},{1,0},{2,3},{3,1},{4,6},{5,4},{6,7},{7,5},{8,10},{9,8},{10,1... | collective-permute-start | bytes 1179656 | tf_op jit(solution)/shard_map/ppermute | solution.py:157
  52.8 4.7 %collective-permute-done.2.rest_0_ = bf16[1536,128]{1,0:T(8,128)(2,1)S(1)} collective-permute-done((bf16[1536,128]{1,0:T(8,128)(2,1)S(1)}, bf16[1536,128]{1,0:T(8,128)(2,1)S(1)}, u32[]{:S(2)}, u32[]{:S(2)}) %collective-permute-start.2) | collective-permute-done | bytes 393248 | tf_op jit(solution)/shard_map/ppermute | solution.py:157
  57.5 4.2 %shard_map.115 = (bf16[1536,1536]{1,0:T(8,128)(2,1)S(1)}, f32[1536,256]{1,0:T(8,128)S(1)}) custom-call(f32[1,1]{1,0:T(1,128)} %bitcast.6.low_ref, f32[1,1]{1,0:T(1,128)} %bitcast.11.high_ref, bf16[1536,128]{1,0:T(8,128)(2,1)S(1)} %copy-done.1, f32[1536,256]{1,0:T(8,128)S(1)} %shard_map.113.ordered_ref, bf16[1536,128]{1,0:T(8,128)(2,1)S(1)} %get-tuple-element.16.lead_ref, ...), custom_call_target="tpu_custom_call" | custom-call | flops 1811939328 | bytes 8650752 | tf_op jit(solution)/shard_map/pallas_call | solution.py:54
  61.7 3.2 %shard_map.117.block_ref = bf16[1536,1536]{1,0:T(8,128)(2,1)S(1)} custom-call(s32[1,2]{1,0:T(1,128)S(1)} %copy-done.5, bf16[1536,128]{1,0:T(8,128)(2,1)S(1)} %copy-done.1, bf16[1536,128]{1,0:T(8,128)(2,1)S(1)} %collective-permute-done.2.rest_0_, bf16[1536,128]{1,0:T(8,128)(2,1)S(1)} %collective-permute-done.rest_0_.rest_1_), custom_call_target="tpu_custom_call" | custom-call | flops 603979776 | bytes 5505024 | tf_op jit(solution)/shard_map/pallas_call | solution.py:54
  64.9 1.0 collective-permute-done.5.refs_2_
  65.9 2.6 %shard_map.118.rest_ref = f32[1536,256]{1,0:T(8,128)S(1)} custom-call(s32[1,2]{1,0:T(1,128)S(1)} %copy-done.5, bf16[1536,1536]{1,0:T(8,128)(2,1)S(1)} %shard_map.117.block_ref, f32[1536,256]{1,0:T(8,128)S(1)} %get-tuple-element.19.rest_ref, bf16[1536,128]{1,0:T(8,128)(2,1)S(1)} %collective-permute-done.3.refs_0_, ...), custom_call_target="tpu_custom_call" | custom-call | flops 1207959552 | bytes 8650752 | tf_op jit(solution)/shard_map/pallas_call | solution.py:54
  68.5 1.1 shard_map.124.coupled_ref
  69.6 4.7 %collective-permute-done.1.rest_1_ = bf16[1536,128]{1,0:T(8,128)(2,1)S(1)} collective-permute-done((bf16[1536,128]{1,0:T(8,128)(2,1)S(1)}, bf16[1536,128]{1,0:T(8,128)(2,1)S(1)}, u32[]{:S(2)}, u32[]{:S(2)}) %collective-permute-start.1) | collective-permute-done | bytes 393248 | tf_op jit(solution)/shard_map/ppermute | solution.py:157
  74.3 3.2 %shard_map.116.block_ref = bf16[1536,1536]{1,0:T(8,128)(2,1)S(1)} custom-call(s32[1,2]{1,0:T(1,128)S(1)} %copy-done.5, bf16[1536,128]{1,0:T(8,128)(2,1)S(1)} %copy-done.1, bf16[1536,128]{1,0:T(8,128)(2,1)S(1)} %collective-permute-done.rest_0_.rest_1_, bf16[1536,128]{1,0:T(8,128)(2,1)S(1)} %collective-permute-done.1.rest_1_), custom_call_target="tpu_custom_call" | custom-call | flops 603979776 | bytes 5505024 | tf_op jit(solution)/shard_map/pallas_call | solution.py:54
  77.5 5.2 %collective-permute-done.14.refs_1_ = bf16[1536,128]{1,0:T(8,128)(2,1)S(1)} collective-permute-done((bf16[1536,128]{1,0:T(8,128)(2,1)S(1)}, bf16[1536,128]{1,0:T(8,128)(2,1)S(1)}, u32[]{:S(2)}, u32[]{:S(2)}) %collective-permute-start.14) | collective-permute-done | bytes 393248 | tf_op jit(solution)/shard_map/ppermute | solution.py:157
  82.8 3.0 %shard_map.125 = (f32[1536,128]{1,0:T(8,128)S(1)}, bf16[1536,128]{1,0:T(8,128)(2,1)S(1)}, bf16[128,128]{1,0:T(8,128)(2,1)S(1)}) custom-call(s32[1,2]{1,0:T(1,128)S(1)} %copy-done.5, f32[1,1]{1,0:T(1,128)} %bitcast.7.low_ref, f32[1,1]{1,0:T(1,128)} %bitcast.12.high_ref, bf16[1536,1536]{1,0:T(8,128)(2,1)S(1)} %shard_map.116.block_ref, ...), custom_call_target="tpu_custom_call" | custom-call | flops 603979776 | bytes 7864320 | tf_op jit(solution)/shard_map/pallas_call | solution.py:54
  85.8 2.0 %collective-permute-done.15.refs_1_ = bf16[1536,128]{1,0:T(8,128)(2,1)S(1)} collective-permute-done((bf16[1536,128]{1,0:T(8,128)(2,1)S(1)}, bf16[1536,128]{1,0:T(8,128)(2,1)S(1)}, u32[]{:S(2)}, u32[]{:S(2)}) %collective-permute-start.15) | collective-permute-done | bytes 393248 | tf_op jit(solution)/shard_map/ppermute | solution.py:157
  87.8 3.1 %shard_map.126 = (f32[1536,128]{1,0:T(8,128)S(1)}, bf16[1536,128]{1,0:T(8,128)(2,1)S(1)}, bf16[128,256]{1,0:T(8,128)(2,1)S(1)}) custom-call(s32[1,2]{1,0:T(1,128)S(1)} %copy-done.5, f32[1,1]{1,0:T(1,128)} %bitcast.8.low_ref, f32[1,1]{1,0:T(1,128)} %bitcast.13.high_ref, bf16[1536,1536]{1,0:T(8,128)(2,1)S(1)} %shard_map.116.block_ref, ...), custom_call_target="tpu_custom_call" | custom-call | flops 603979776 | bytes 7864320 | tf_op jit(solution)/shard_map/pallas_call | solution.py:54
  90.9 1.7 %collective-permute-start.20 = (bf16[128,256]{1,0:T(8,128)(2,1)S(1)}, bf16[128,256]{1,0:T(8,128)(2,1)S(1)}, u32[]{:S(2)}, u32[]{:S(2)}) collective-permute-start(bf16[128,256]{1,0:T(8,128)(2,1)S(1)} %get-tuple-element.27.refs_0_), channel_id=1, source_target_pairs={{0,1},{1,0},{2,3},{3,2},{4,5},{5,4},{6,7},{7,6},{8,9},{9,8},{10,11... | collective-permute-start | bytes 196616 | tf_op jit(solution)/shard_map/ppermute | solution.py:157
  93.3 1.9 %collective-permute-done.20.refs_1_ = bf16[128,256]{1,0:T(8,128)(2,1)S(1)} collective-permute-done((bf16[128,256]{1,0:T(8,128)(2,1)S(1)}, bf16[128,256]{1,0:T(8,128)(2,1)S(1)}, u32[]{:S(2)}, u32[]{:S(2)}) %collective-permute-start.20) | collective-permute-done | bytes 65568 | tf_op jit(solution)/shard_map/ppermute | solution.py:157
  95.9 0.7 collective-permute-start.19
  96.9 12.8 %collective-permute-start.22 = (bf16[128,512]{1,0:T(8,128)(2,1)S(1)}, bf16[128,512]{1,0:T(8,128)(2,1)S(1)}, u32[]{:S(2)}, u32[]{:S(2)}) collective-permute-start(bf16[128,512]{1,0:T(8,128)(2,1)S(1)} %shard_map.130.summed_ref), channel_id=1, source_target_pairs={{0,1},{1,0},{2,3},{3,2},{4,5},{5,4},{6,7},{7,6},{8,9},{9,8},{10,11... | collective-permute-start | bytes 393224 | tf_op jit(solution)/shard_map/ppermute | solution.py:157
  109.8 1.9 %collective-permute-start.16 = (bf16[1536,128]{1,0:T(8,128)(2,1)S(1)}, bf16[1536,128]{1,0:T(8,128)(2,1)S(1)}, u32[]{:S(2)}, u32[]{:S(2)}) collective-permute-start(bf16[1536,128]{1,0:T(8,128)(2,1)S(1)} %get-tuple-element.20.lead_ref), channel_id=1, source_target_pairs={{0,1},{1,0},{2,3},{3,2},{4,5},{5,4},{6,7},{7,6},{8,9},{9,8},{10,11... | collective-permute-start | bytes 1179656 | tf_op jit(solution)/shard_map/ppermute | solution.py:157
  111.8 2.3 %collective-permute-done.22.handed_ref.refs_2_ = bf16[128,512]{1,0:T(8,128)(2,1)S(1)} collective-permute-done((bf16[128,512]{1,0:T(8,128)(2,1)S(1)}, bf16[128,512]{1,0:T(8,128)(2,1)S(1)}, u32[]{:S(2)}, u32[]{:S(2)}) %collective-permute-start.22) | collective-permute-done | bytes 131104 | tf_op jit(solution)/shard_map/ppermute | solution.py:157
  114.1 1.5 %collective-permute-start.23 = (bf16[128,256]{1,0:T(8,128)(2,1)S(1)}, bf16[128,256]{1,0:T(8,128)(2,1)S(1)}, u32[]{:S(2)}, u32[]{:S(2)}) collective-permute-start(bf16[128,256]{1,0:T(8,128)(2,1)S(1)} %shard_map.131.refs_0_), channel_id=1, source_target_pairs={{0,8},{4,12},{8,16},{12,20},{16,24},{20,28},{24,0},{28,4},{1,9},{5... | collective-permute-start | bytes 196616 | tf_op jit(solution)/shard_map/ppermute | solution.py:22
  115.7 3.7 %collective-permute-done.23.refs_1_.refs_3_ = bf16[128,256]{1,0:T(8,128)(2,1)S(1)} collective-permute-done((bf16[128,256]{1,0:T(8,128)(2,1)S(1)}, bf16[128,256]{1,0:T(8,128)(2,1)S(1)}, u32[]{:S(2)}, u32[]{:S(2)}) %collective-permute-start.23) | collective-permute-done | bytes 65568 | tf_op jit(solution)/shard_map/ppermute | solution.py:22
  119.3 1.5 %collective-permute-start.24 = (bf16[128,256]{1,0:T(8,128)(2,1)S(1)}, bf16[128,256]{1,0:T(8,128)(2,1)S(1)}, u32[]{:S(2)}, u32[]{:S(2)}) collective-permute-start(bf16[128,256]{1,0:T(8,128)(2,1)S(1)} %shard_map.131.refs_0_), channel_id=1, source_target_pairs={{0,16},{4,20},{8,24},{12,28},{16,0},{20,4},{24,8},{28,12},{1,17},{... | collective-permute-start | bytes 196616 | tf_op jit(solution)/shard_map/ppermute | solution.py:22
  120.9 2.7 %collective-permute-start.27 = (bf16[1536,128]{1,0:T(8,128)(2,1)S(1)}, bf16[1536,128]{1,0:T(8,128)(2,1)S(1)}, u32[]{:S(2)}, u32[]{:S(2)}) collective-permute-start(bf16[1536,128]{1,0:T(8,128)(2,1)S(1)} %collective-permute-done.17.refs_1_.refs_0_), channel_id=1, source_target_pairs={{0,2},{1,0},{2,3},{3,1},{4,6},{5,4},{6,7},{7,5},{8,10},{9,8},{10,1... | collective-permute-start | bytes 1179656 | tf_op jit(solution)/shard_map/ppermute | solution.py:157
  123.6 1.6 %collective-permute-start.25 = (bf16[128,256]{1,0:T(8,128)(2,1)S(1)}, bf16[128,256]{1,0:T(8,128)(2,1)S(1)}, u32[]{:S(2)}, u32[]{:S(2)}) collective-permute-start(bf16[128,256]{1,0:T(8,128)(2,1)S(1)} %shard_map.131.refs_0_), channel_id=1, source_target_pairs={{0,24},{4,28},{8,0},{12,4},{16,8},{20,12},{24,16},{28,20},{1,25},{... | collective-permute-start | bytes 196616 | tf_op jit(solution)/shard_map/ppermute | solution.py:22
  125.2 2.7 %collective-permute-done.25.refs_3_.refs_5_ = bf16[128,256]{1,0:T(8,128)(2,1)S(1)} collective-permute-done((bf16[128,256]{1,0:T(8,128)(2,1)S(1)}, bf16[128,256]{1,0:T(8,128)(2,1)S(1)}, u32[]{:S(2)}, u32[]{:S(2)}) %collective-permute-start.25) | collective-permute-done | bytes 65568 | tf_op jit(solution)/shard_map/ppermute | solution.py:22
  128.0 2.7 %collective-permute-start.28 = (bf16[1024,128]{1,0:T(8,128)(2,1)S(1)}, bf16[1024,128]{1,0:T(8,128)(2,1)S(1)}, u32[]{:S(2)}, u32[]{:S(2)}) collective-permute-start(bf16[1024,128]{1,0:T(8,128)(2,1)S(1)} %slice.8), channel_id=1, source_target_pairs={{0,2},{1,0},{2,3},{3,1},{4,6},{5,4},{6,7},{7,5},{8,10},{9,8},{10,1... | collective-permute-start | bytes 786440 | tf_op jit(solution)/shard_map/ppermute | solution.py:157
  130.7 3.0 %shard_map.127 = (f32[1536,256]{1,0:T(8,128)}, f32[1536,256]{1,0:T(8,128)S(1)}) custom-call(f32[1,1]{1,0:T(1,128)} %bitcast.9.low_ref, f32[1,1]{1,0:T(1,128)} %bitcast.14.high_ref, bf16[1536,1536]{1,0:T(8,128)(2,1)S(1)} %get-tuple-element.18.block_ref, bf16[1536,128]{1,0:T(8,128)(2,1)S(1)} %get-tuple-element.20.lead_ref, ...), custom_call_target="tpu_custom_call" | custom-call | flops 1207959552 | bytes 11796480 | tf_op jit(solution)/shard_map/pallas_call | solution.py:54
  133.8 2.4 %shard_map.128.rest_ref = f32[1536,256]{1,0:T(8,128)S(1)} custom-call(s32[1,2]{1,0:T(1,128)S(1)} %copy-done.5, bf16[1536,1536]{1,0:T(8,128)(2,1)S(1)} %shard_map.117.block_ref, f32[1536,256]{1,0:T(8,128)S(1)} %get-tuple-element.26.rest_ref, bf16[1536,128]{1,0:T(8,128)(2,1)S(1)} %collective-permute-done.16.refs_0_, ...), custom_call_target="tpu_custom_call" | custom-call | flops 1207959552 | bytes 8650752 | tf_op jit(solution)/shard_map/pallas_call | solution.py:54
  136.3 1.1 shard_map.133.coupled_ref
  137.4 3.0 %shard_map.134 = (f32[1536,256]{1,0:T(8,128)}, f32[1536,128]{1,0:T(8,128)S(1)}) custom-call(s32[1,2]{1,0:T(1,128)S(1)} %copy-done.5, bf16[1536,1536]{1,0:T(8,128)(2,1)S(1)} %shard_map.116.block_ref, f32[1536,256]{1,0:T(8,128)S(1)} %shard_map.128.rest_ref, bf16[1536,128]{1,0:T(8,128)(2,1)S(1)} %copy-done, bf16[128,256]{1,0:T(8,128)(2,1)S(1)} %shard_map.133.coupled_ref, ...), custom_call_target="tpu_custom_call" | custom-call | flops 603979776 | bytes 6684672 | tf_op jit(solution)/shard_map/pallas_call | solution.py:54
  140.4 1.9 %shard_map.135.trail_ref = f32[1536,128]{1,0:T(8,128)S(1)} custom-call(s32[1,2]{1,0:T(1,128)S(1)} %copy-done.5, bf16[1536,1536]{1,0:T(8,128)(2,1)S(1)} %shard_map.116.block_ref, f32[1536,128]{1,0:T(8,128)S(1)} %get-tuple-element.28.trail_ref, bf16[1536,128]{1,0:T(8,128)(2,1)S(1)} %collective-permute-done.19.refs_3_.inner_ref, ...), custom_call_target="tpu_custom_call" | custom-call | flops 402653184 | bytes 4718592 | tf_op jit(solution)/shard_map/pallas_call | solution.py:54
  142.2 1.9 %shard_map.136 = f32[1536,256]{1,0:T(8,128)} custom-call(s32[1,2]{1,0:T(1,128)S(1)} %copy-done.5, bf16[1536,1536]{1,0:T(8,128)(2,1)S(1)} %shard_map.116.block_ref, f32[1536,128]{1,0:T(8,128)S(1)} %shard_map.135.trail_ref, bf16[512,128]{1,0:T(8,128)(2,1)S(1)} %collective-permute-done.29.refs_0_, ...), custom_call_target="tpu_custom_call", output_to_operand_aliasing={{}: (4, {})} | custom-call | flops 603979776 | bytes 6684672 | tf_op jit(solution)/shard_map/pallas_call | solution.py:54
  (54 shorter events, 3.5 us)
Async XLA Ops:
  1.9 3.1 %copy-start = (bf16[1536,128]{1,0:T(8,128)(2,1)S(1)}, bf16[1536,128]{1,0:T(8,128)(2,1)}, u32[]{:S(2)}) copy-start(bf16[1536,128]{1,0:T(8,128)(2,1)} %bases_ref.7) | copy-start | bytes 1179652
  1.9 3.1 %copy-start.4 = (bf16[1,128,128]{2,1,0:T(8,128)(2,1)S(1)}, bf16[1,128,128]{2,1,0:T(8,128)(2,1)}, u32[]{:S(2)}) copy-start(bf16[1,128,128]{2,1,0:T(8,128)(2,1)} %param.16) | copy-start | bytes 98308
  5.0 7.8 %copy-start.1 = (bf16[1536,128]{1,0:T(8,128)(2,1)S(1)}, bf16[1536,128]{1,0:T(8,128)(2,1)}, u32[]{:S(2)}) copy-start(bf16[1536,128]{1,0:T(8,128)(2,1)} %points_ref.5) | copy-start | bytes 1179652
  5.0 37.9 %copy-start.6 = (f32[1536,256]{1,0:T(8,128)S(1)}, f32[1536,256]{1,0:T(8,128)}, u32[]{:S(2)}) copy-start(f32[1536,256]{1,0:T(8,128)} %right_hbm.1) | copy-start | bytes 4718596
  5.1 37.9 %copy-start.7 = (s32[1,1536]{1,0:T(1,128)S(1)}, s32[1,1536]{1,0:T(1,128)}, u32[]{:S(2)}) copy-start(s32[1,1536]{1,0:T(1,128)} %order_hbm.1) | copy-start | bytes 18436
  5.5 5.9 %collective-permute-start.7 = (bf16[128,384]{1,0:T(8,128)(2,1)S(1)}, bf16[128,384]{1,0:T(8,128)(2,1)S(1)}, u32[]{:S(2)}, u32[]{:S(2)}) collective-permute-start(bf16[128,384]{1,0:T(8,128)(2,1)S(1)} %shard_map.119.refs_0_), channel_id=1, source_target_pairs={{0,1},{1,0},{2,3},{3,2},{4,5},{5,4},{6,7},{7,6},{8,9},{9,8},{10,11... | collective-permute-start | bytes 294920 | tf_op jit(solution)/shard_map/ppermute | solution.py:157
  11.5 2.1 %collective-permute-start.8 = (bf16[256,384]{1,0:T(8,128)(2,1)S(1)}, bf16[256,384]{1,0:T(8,128)(2,1)S(1)}, u32[]{:S(2)}, u32[]{:S(2)}) collective-permute-start(bf16[256,384]{1,0:T(8,128)(2,1)S(1)} %shard_map.120.pair_ref.first_pair_ref.refs_0_), channel_id=1, source_target_pairs={{0,0},{1,2},{2,1},{3,3},{4,4},{5,6},{6,5},{7,7},{8,8},{9,10},{10,9... | collective-permute-start | bytes 589832 | tf_op jit(solution)/shard_map/ppermute | solution.py:157
  12.1 18.3 %collective-permute-start.4 = (bf16[1536,128]{1,0:T(8,128)(2,1)S(1)}, bf16[1536,128]{1,0:T(8,128)(2,1)S(1)}, u32[]{:S(2)}, u32[]{:S(2)}) collective-permute-start(bf16[1536,128]{1,0:T(8,128)(2,1)S(1)} %get-tuple-element.16.lead_ref), channel_id=1, source_target_pairs={{0,0},{1,2},{2,1},{3,3},{4,4},{5,6},{6,5},{7,7},{8,8},{9,10},{10,9... | collective-permute-start | bytes 1179656 | tf_op jit(solution)/shard_map/ppermute | solution.py:157
  12.8 18.3 %collective-permute-start = (bf16[1536,128]{1,0:T(8,128)(2,1)S(1)}, bf16[1536,128]{1,0:T(8,128)(2,1)S(1)}, u32[]{:S(2)}, u32[]{:S(2)}) collective-permute-start(bf16[1536,128]{1,0:T(8,128)(2,1)S(1)} %copy-done.1), channel_id=1, source_target_pairs={{0,0},{1,2},{2,1},{3,3},{4,4},{5,6},{6,5},{7,7},{8,8},{9,10},{10,9... | collective-permute-start | bytes 1179656 | tf_op jit(solution)/shard_map/ppermute | solution.py:157
  13.8 12.1 %collective-permute-start.9 = (bf16[128,512]{1,0:T(8,128)(2,1)S(1)}, bf16[128,512]{1,0:T(8,128)(2,1)S(1)}, u32[]{:S(2)}, u32[]{:S(2)}) collective-permute-start(bf16[128,512]{1,0:T(8,128)(2,1)S(1)} %shard_map.121.summed_ref), channel_id=1, source_target_pairs={{0,1},{1,0},{2,3},{3,2},{4,5},{5,4},{6,7},{7,6},{8,9},{9,8},{10,11... | collective-permute-start | bytes 393224 | tf_op jit(solution)/shard_map/ppermute | solution.py:157
  25.9 13.1 %collective-permute-start.10 = (bf16[128,256]{1,0:T(8,128)(2,1)S(1)}, bf16[128,256]{1,0:T(8,128)(2,1)S(1)}, u32[]{:S(2)}, u32[]{:S(2)}) collective-permute-start(bf16[128,256]{1,0:T(8,128)(2,1)S(1)} %shard_map.122.refs_0_), channel_id=1, source_target_pairs={{0,8},{4,12},{8,16},{12,20},{16,24},{20,28},{24,0},{28,4},{1,9},{5... | collective-permute-start | bytes 196616 | tf_op jit(solution)/shard_map/ppermute | solution.py:22
  27.5 11.6 %collective-permute-start.11 = (bf16[128,256]{1,0:T(8,128)(2,1)S(1)}, bf16[128,256]{1,0:T(8,128)(2,1)S(1)}, u32[]{:S(2)}, u32[]{:S(2)}) collective-permute-start(bf16[128,256]{1,0:T(8,128)(2,1)S(1)} %shard_map.122.refs_0_), channel_id=1, source_target_pairs={{0,16},{4,20},{8,24},{12,28},{16,0},{20,4},{24,8},{28,12},{1,17},{... | collective-permute-start | bytes 196616 | tf_op jit(solution)/shard_map/ppermute | solution.py:22
  29.0 12.1 %collective-permute-start.12 = (bf16[128,256]{1,0:T(8,128)(2,1)S(1)}, bf16[128,256]{1,0:T(8,128)(2,1)S(1)}, u32[]{:S(2)}, u32[]{:S(2)}) collective-permute-start(bf16[128,256]{1,0:T(8,128)(2,1)S(1)} %shard_map.122.refs_0_), channel_id=1, source_target_pairs={{0,24},{4,28},{8,0},{12,4},{16,8},{20,12},{24,16},{28,20},{1,25},{... | collective-permute-start | bytes 196616 | tf_op jit(solution)/shard_map/ppermute | solution.py:22
  30.4 16.5 %collective-permute-start.6 = (bf16[1536,128]{1,0:T(8,128)(2,1)S(1)}, bf16[1536,128]{1,0:T(8,128)(2,1)S(1)}, u32[]{:S(2)}, u32[]{:S(2)}) collective-permute-start(bf16[1536,128]{1,0:T(8,128)(2,1)S(1)} %get-tuple-element.17.trail_ref), channel_id=1, source_target_pairs={{0,0},{1,2},{2,1},{3,3},{4,4},{5,6},{6,5},{7,7},{8,8},{9,10},{10,9... | collective-permute-start | bytes 1179656 | tf_op jit(solution)/shard_map/ppermute | solution.py:157
  31.1 17.9 %collective-permute-start.3 = (bf16[1536,128]{1,0:T(8,128)(2,1)S(1)}, bf16[1536,128]{1,0:T(8,128)(2,1)S(1)}, u32[]{:S(2)}, u32[]{:S(2)}) collective-permute-start(bf16[1536,128]{1,0:T(8,128)(2,1)S(1)} %get-tuple-element.16.lead_ref), channel_id=1, source_target_pairs={{0,1},{1,0},{2,3},{3,2},{4,5},{5,4},{6,7},{7,6},{8,9},{9,8},{10,11... | collective-permute-start | bytes 1179656 | tf_op jit(solution)/shard_map/ppermute | solution.py:157
  39.1 18.4 %collective-permute-start.2 = (bf16[1536,128]{1,0:T(8,128)(2,1)S(1)}, bf16[1536,128]{1,0:T(8,128)(2,1)S(1)}, u32[]{:S(2)}, u32[]{:S(2)}) collective-permute-start(bf16[1536,128]{1,0:T(8,128)(2,1)S(1)} %copy-done.1), channel_id=1, source_target_pairs={{0,1},{1,0},{2,3},{3,2},{4,5},{5,4},{6,7},{7,6},{8,9},{9,8},{10,11... | collective-permute-start | bytes 1179656 | tf_op jit(solution)/shard_map/ppermute | solution.py:157
  39.1 26.8 %collective-permute-start.5 = (bf16[1536,128]{1,0:T(8,128)(2,1)S(1)}, bf16[1536,128]{1,0:T(8,128)(2,1)S(1)}, u32[]{:S(2)}, u32[]{:S(2)}) collective-permute-start(bf16[1536,128]{1,0:T(8,128)(2,1)S(1)} %get-tuple-element.17.trail_ref), channel_id=1, source_target_pairs={{0,1},{1,0},{2,3},{3,2},{4,5},{5,4},{6,7},{7,6},{8,9},{9,8},{10,11... | collective-permute-start | bytes 1179656 | tf_op jit(solution)/shard_map/ppermute | solution.py:157
  41.1 33.2 %collective-permute-start.1 = (bf16[1536,128]{1,0:T(8,128)(2,1)S(1)}, bf16[1536,128]{1,0:T(8,128)(2,1)S(1)}, u32[]{:S(2)}, u32[]{:S(2)}) collective-permute-start(bf16[1536,128]{1,0:T(8,128)(2,1)S(1)} %collective-permute-done.rest_0_.rest_1_), channel_id=1, source_target_pairs={{0,2},{1,0},{2,3},{3,1},{4,6},{5,4},{6,7},{7,5},{8,10},{9,8},{10,1... | collective-permute-start | bytes 1179656 | tf_op jit(solution)/shard_map/ppermute | solution.py:157
  47.0 35.8 %collective-permute-start.14 = (bf16[1536,128]{1,0:T(8,128)(2,1)S(1)}, bf16[1536,128]{1,0:T(8,128)(2,1)S(1)}, u32[]{:S(2)}, u32[]{:S(2)}) collective-permute-start(bf16[1536,128]{1,0:T(8,128)(2,1)S(1)} %collective-permute-done.4.refs_1_.refs_0_), channel_id=1, source_target_pairs={{0,2},{1,0},{2,3},{3,1},{4,6},{5,4},{6,7},{7,5},{8,10},{9,8},{10,1... | collective-permute-start | bytes 1179656 | tf_op jit(solution)/shard_map/ppermute | solution.py:157
  49.0 38.8 %collective-permute-start.15 = (bf16[1536,128]{1,0:T(8,128)(2,1)S(1)}, bf16[1536,128]{1,0:T(8,128)(2,1)S(1)}, u32[]{:S(2)}, u32[]{:S(2)}) collective-permute-start(bf16[1536,128]{1,0:T(8,128)(2,1)S(1)} %collective-permute-done.6.refs_3_.refs_0_), channel_id=1, source_target_pairs={{0,2},{1,0},{2,3},{3,1},{4,6},{5,4},{6,7},{7,5},{8,10},{9,8},{10,1... | collective-permute-start | bytes 1179656 | tf_op jit(solution)/shard_map/ppermute | solution.py:157
  57.5 11.0 %collective-permute-start.13 = (bf16[512,256]{1,0:T(8,128)(2,1)S(1)}, bf16[512,256]{1,0:T(8,128)(2,1)S(1)}, u32[]{:S(2)}, u32[]{:S(2)}) collective-permute-start(bf16[512,256]{1,0:T(8,128)(2,1)S(1)} %shard_map.123), channel_id=1, source_target_pairs={{0,4},{4,0},{8,12},{12,8},{16,20},{20,16},{24,28},{28,24},{1,5},{5... | collective-permute-start | bytes 786440 | tf_op jit(solution)/shard_map/ppermute | solution.py:636
  57.5 4.2 %copy-start.5 = (s32[1,2]{1,0:T(1,128)S(1)}, s32[1,2]{1,0:T(1,128)}, u32[]{:S(2)}) copy-start(s32[1,2]{1,0:T(1,128)} %near_ref.21) | copy-start | bytes 28
  65.9 2.6 %copy-start.2 = (bf16[1,8,128,128]{3,2,1,0:T(8,128)(2,1)S(1)}, bf16[1,8,128,128]{3,2,1,0:T(8,128)(2,1)}, u32[]{:S(2)}) copy-start(bf16[1,8,128,128]{3,2,1,0:T(8,128)(2,1)} %param.17) | copy-start | bytes 786436
  65.9 2.6 %copy-start.3 = (bf16[1,4,128,128]{3,2,1,0:T(8,128)(2,1)S(1)}, bf16[1,4,128,128]{3,2,1,0:T(8,128)(2,1)}, u32[]{:S(2)}) copy-start(bf16[1,4,128,128]{3,2,1,0:T(8,128)(2,1)} %param.15) | copy-start | bytes 393220
  90.9 4.3 %collective-permute-start.20 = (bf16[128,256]{1,0:T(8,128)(2,1)S(1)}, bf16[128,256]{1,0:T(8,128)(2,1)S(1)}, u32[]{:S(2)}, u32[]{:S(2)}) collective-permute-start(bf16[128,256]{1,0:T(8,128)(2,1)S(1)} %get-tuple-element.27.refs_0_), channel_id=1, source_target_pairs={{0,1},{1,0},{2,3},{3,2},{4,5},{5,4},{6,7},{7,6},{8,9},{9,8},{10,11... | collective-permute-start | bytes 196616 | tf_op jit(solution)/shard_map/ppermute | solution.py:157
  92.7 28.2 %collective-permute-start.17 = (bf16[1536,128]{1,0:T(8,128)(2,1)S(1)}, bf16[1536,128]{1,0:T(8,128)(2,1)S(1)}, u32[]{:S(2)}, u32[]{:S(2)}) collective-permute-start(bf16[1536,128]{1,0:T(8,128)(2,1)S(1)} %get-tuple-element.20.lead_ref), channel_id=1, source_target_pairs={{0,0},{1,2},{2,1},{3,3},{4,4},{5,6},{6,5},{7,7},{8,8},{9,10},{10,9... | collective-permute-start | bytes 1179656 | tf_op jit(solution)/shard_map/ppermute | solution.py:157
  95.3 1.4 collective-permute-start.21
  95.9 32.0 %collective-permute-start.19 = (bf16[1536,128]{1,0:T(8,128)(2,1)S(1)}, bf16[1536,128]{1,0:T(8,128)(2,1)S(1)}, u32[]{:S(2)}, u32[]{:S(2)}) collective-permute-start(bf16[1536,128]{1,0:T(8,128)(2,1)S(1)} %get-tuple-element.22.trail_ref), channel_id=1, source_target_pairs={{0,0},{1,2},{2,1},{3,3},{4,4},{5,6},{6,5},{7,7},{8,8},{9,10},{10,9... | collective-permute-start | bytes 1179656 | tf_op jit(solution)/shard_map/ppermute | solution.py:157
  96.9 17.2 %collective-permute-start.22 = (bf16[128,512]{1,0:T(8,128)(2,1)S(1)}, bf16[128,512]{1,0:T(8,128)(2,1)S(1)}, u32[]{:S(2)}, u32[]{:S(2)}) collective-permute-start(bf16[128,512]{1,0:T(8,128)(2,1)S(1)} %shard_map.130.summed_ref), channel_id=1, source_target_pairs={{0,1},{1,0},{2,3},{3,2},{4,5},{5,4},{6,7},{7,6},{8,9},{9,8},{10,11... | collective-permute-start | bytes 393224 | tf_op jit(solution)/shard_map/ppermute | solution.py:157
  109.8 24.0 %collective-permute-start.18 = (bf16[1536,128]{1,0:T(8,128)(2,1)S(1)}, bf16[1536,128]{1,0:T(8,128)(2,1)S(1)}, u32[]{:S(2)}, u32[]{:S(2)}) collective-permute-start(bf16[1536,128]{1,0:T(8,128)(2,1)S(1)} %get-tuple-element.22.trail_ref), channel_id=1, source_target_pairs={{0,1},{1,0},{2,3},{3,2},{4,5},{5,4},{6,7},{7,6},{8,9},{9,8},{10,11... | collective-permute-start | bytes 1179656 | tf_op jit(solution)/shard_map/ppermute | solution.py:157
  109.8 24.0 %collective-permute-start.16 = (bf16[1536,128]{1,0:T(8,128)(2,1)S(1)}, bf16[1536,128]{1,0:T(8,128)(2,1)S(1)}, u32[]{:S(2)}, u32[]{:S(2)}) collective-permute-start(bf16[1536,128]{1,0:T(8,128)(2,1)S(1)} %get-tuple-element.20.lead_ref), channel_id=1, source_target_pairs={{0,1},{1,0},{2,3},{3,2},{4,5},{5,4},{6,7},{7,6},{8,9},{9,8},{10,11... | collective-permute-start | bytes 1179656 | tf_op jit(solution)/shard_map/ppermute | solution.py:157
  114.1 5.2 %collective-permute-start.23 = (bf16[128,256]{1,0:T(8,128)(2,1)S(1)}, bf16[128,256]{1,0:T(8,128)(2,1)S(1)}, u32[]{:S(2)}, u32[]{:S(2)}) collective-permute-start(bf16[128,256]{1,0:T(8,128)(2,1)S(1)} %shard_map.131.refs_0_), channel_id=1, source_target_pairs={{0,8},{4,12},{8,16},{12,20},{16,24},{20,28},{24,0},{28,4},{1,9},{5... | collective-permute-start | bytes 196616 | tf_op jit(solution)/shard_map/ppermute | solution.py:22
  119.3 4.3 %collective-permute-start.24 = (bf16[128,256]{1,0:T(8,128)(2,1)S(1)}, bf16[128,256]{1,0:T(8,128)(2,1)S(1)}, u32[]{:S(2)}, u32[]{:S(2)}) collective-permute-start(bf16[128,256]{1,0:T(8,128)(2,1)S(1)} %shard_map.131.refs_0_), channel_id=1, source_target_pairs={{0,16},{4,20},{8,24},{12,28},{16,0},{20,4},{24,8},{28,12},{1,17},{... | collective-permute-start | bytes 196616 | tf_op jit(solution)/shard_map/ppermute | solution.py:22
  120.9 16.5 %collective-permute-start.27 = (bf16[1536,128]{1,0:T(8,128)(2,1)S(1)}, bf16[1536,128]{1,0:T(8,128)(2,1)S(1)}, u32[]{:S(2)}, u32[]{:S(2)}) collective-permute-start(bf16[1536,128]{1,0:T(8,128)(2,1)S(1)} %collective-permute-done.17.refs_1_.refs_0_), channel_id=1, source_target_pairs={{0,2},{1,0},{2,3},{3,1},{4,6},{5,4},{6,7},{7,5},{8,10},{9,8},{10,1... | collective-permute-start | bytes 1179656 | tf_op jit(solution)/shard_map/ppermute | solution.py:157
  123.6 4.3 %collective-permute-start.25 = (bf16[128,256]{1,0:T(8,128)(2,1)S(1)}, bf16[128,256]{1,0:T(8,128)(2,1)S(1)}, u32[]{:S(2)}, u32[]{:S(2)}) collective-permute-start(bf16[128,256]{1,0:T(8,128)(2,1)S(1)} %shard_map.131.refs_0_), channel_id=1, source_target_pairs={{0,24},{4,28},{8,0},{12,4},{16,8},{20,12},{24,16},{28,20},{1,25},{... | collective-permute-start | bytes 196616 | tf_op jit(solution)/shard_map/ppermute | solution.py:22
  127.9 8.4 %collective-permute-start.26 = (bf16[512,256]{1,0:T(8,128)(2,1)S(1)}, bf16[512,256]{1,0:T(8,128)(2,1)S(1)}, u32[]{:S(2)}, u32[]{:S(2)}) collective-permute-start(bf16[512,256]{1,0:T(8,128)(2,1)S(1)} %shard_map.132), channel_id=1, source_target_pairs={{0,4},{4,0},{8,12},{12,8},{16,20},{20,16},{24,28},{28,24},{1,5},{5... | collective-permute-start | bytes 786440 | tf_op jit(solution)/shard_map/ppermute | solution.py:636
  128.0 12.3 %collective-permute-start.28 = (bf16[1024,128]{1,0:T(8,128)(2,1)S(1)}, bf16[1024,128]{1,0:T(8,128)(2,1)S(1)}, u32[]{:S(2)}, u32[]{:S(2)}) collective-permute-start(bf16[1024,128]{1,0:T(8,128)(2,1)S(1)} %slice.8), channel_id=1, source_target_pairs={{0,2},{1,0},{2,3},{3,1},{4,6},{5,4},{6,7},{7,5},{8,10},{9,8},{10,1... | collective-permute-start | bytes 786440 | tf_op jit(solution)/shard_map/ppermute | solution.py:157
  133.8 8.5 %collective-permute-start.29 = (bf16[512,128]{1,0:T(8,128)(2,1)S(1)}, bf16[512,128]{1,0:T(8,128)(2,1)S(1)}, u32[]{:S(2)}, u32[]{:S(2)}) collective-permute-start(bf16[512,128]{1,0:T(8,128)(2,1)S(1)} %slice.9), channel_id=1, source_target_pairs={{0,2},{1,0},{2,3},{3,1},{4,6},{5,4},{6,7},{7,5},{8,10},{9,8},{10,1... | collective-permute-start | bytes 393224 | tf_op jit(solution)/shard_map/ppermute | solution.py:157
